TPU v7x, 32 devices: a whole 2x2x4 slice. The times are simulated.
32 devices in a mesh: lon: 8 (over z, x), lat: 4 (over y, core).
Axes of the slice: x: 2, y: 2, z: 4, core: 2. Of those that a mesh axis runs over, the one named last changes fastest.
Arguments:
- right_side: float32 [70, 32, 512], P(None, 'lon', 'lat'), may hold values from -12 to 12
- first_guess: float32 [70, 32, 512], P(None, 'lon', 'lat'), may hold values from -1.8 to 1.8
- cell_scale: float32 [70, 32, 512], P(None, 'lon', 'lat'), may hold values from 0.6 to 1.6
- helmholtz_term: float32 [70, 32, 512], P(None, 'lon', 'lat'), may hold values from 0.05 to 0.5
- vertical_coupling: float32 [69], replicated, may hold values from 0.5 to 4
Outputs:
- solution: float32 [70, 32, 512], P(None, 'lon', 'lat')
- residual: float32 [70, 32, 512], P(None, 'lon', 'lat')
All inputs are finite; a program needn't handle non-finite values.
Results may differ from a plain program's by a relative error of at most 0.00026.
Values sent between devices are 32-bit elements; how exact they have to be, the bound alone decides.
No kernel may reach another device: no remote copies, remote signals or barrier semaphores. Data moves between devices by JAX's collectives and lax.ppermute only.
A program may use at most 64 MiB of HBM per device.

v0:
```python
import jax
import jax.numpy as jnp
from jax import lax
from jax.sharding import PartitionSpec as P

ITERS = 2


def padded(value, sides, width, wrap):
    for axis, dim in sides:
        peers, length = (lax.axis_size(axis), value.shape[dim])
        up = [(i, (i + 1) % peers) for i in range(peers if wrap else peers - 1)]
        down = [(j, i) for i, j in up]
        last = lax.slice_in_dim(value, length - width, length, axis=dim)
        leading = lax.slice_in_dim(value, 0, width, axis=dim)
        before = lax.ppermute(last, axis, up)
        after = lax.ppermute(leading, axis, down)
        value = jnp.concatenate([before, value, after], axis=dim)
    return value


def shifted(value, axis, steps):
    count = lax.axis_size(axis)
    pairs = [(source, (source + steps) % count) for source in range(count)]
    return lax.ppermute(value, axis, pairs)


def extend(stacked):
    lon_side = padded(stacked, (("lon", 2),), 1, True)
    lat_side = padded(stacked, (("lat", 3),), 1, False)
    edge_rows = jnp.concatenate([stacked[..., :1], stacked[..., -1:]], axis=3)
    partner = shifted(edge_rows, "lon", lax.axis_size("lon") // 2)
    band_index = lax.axis_index("lat")
    last_band = lax.axis_size("lat") - 1
    top_row = jnp.where(band_index == 0, partner[..., :1], lat_side[..., :1])
    bottom = jnp.where(band_index == last_band, partner[..., 1:], lat_side[..., -1:])
    lat_side = jnp.concatenate([top_row, lat_side[..., 1:-1], bottom], axis=3)
    return (lon_side, lat_side)


def reduce_all(terms):
    return lax.psum(terms, ("lon", "lat"))


def apply_operator(
    field, lon_side, lat_side, cell_scale, scale_lon, scale_lat, helmholtz_term, vertical_coupling
):
    scaled = cell_scale * field
    scaled_lon = scale_lon * lon_side
    scaled_lat = scale_lat * lat_side
    horizontal = (
        (4.0 + helmholtz_term) * scaled
        - scaled_lon[:, 2:, :]
        - scaled_lon[:, :-2, :]
        - scaled_lat[:, :, :-2]
        - scaled_lat[:, :, 2:]
    )
    vert_flux = vertical_coupling[:, None, None] * (scaled[:-1] - scaled[1:])
    zero_layer = jnp.zeros_like(scaled[:1])
    vertical = jnp.concatenate([vert_flux, zero_layer], axis=0) - jnp.concatenate(
        [zero_layer, vert_flux], axis=0
    )
    return cell_scale * (horizontal + vertical)


def body(right_side, first_guess, cell_scale, helmholtz_term, vertical_coupling):
    start_lon, start_lat = extend(jnp.stack([cell_scale, first_guess]))
    scale_lon = start_lon[0]
    scale_lat = start_lat[0]

    def operate(field, lon_side, lat_side):
        return apply_operator(
            field,
            lon_side,
            lat_side,
            cell_scale,
            scale_lon,
            scale_lat,
            helmholtz_term,
            vertical_coupling,
        )

    solution = first_guess
    residual = right_side - operate(first_guess, start_lon[1], start_lat[1])
    shadow = residual
    direction = residual
    rho_now = None
    for iteration in range(ITERS):
        dir_lon, dir_lat = extend(direction[None])
        image_vec = operate(direction, dir_lon[0], dir_lat[0])
        if iteration == 0:
            rho_now, denominator = reduce_all(
                (jnp.sum(residual * residual), jnp.sum(shadow * image_vec))
            )
        else:
            (denominator,) = reduce_all((jnp.sum(shadow * image_vec),))
        alpha_step = rho_now / denominator
        half_step = residual - alpha_step * image_vec
        pair_lon, pair_lat = extend(jnp.stack([residual, image_vec]))
        half_lon = pair_lon[0] - alpha_step * pair_lon[1]
        half_lat = pair_lat[0] - alpha_step * pair_lat[1]
        second_image = operate(half_step, half_lon, half_lat)
        if iteration + 1 < ITERS:
            tee_half, tee_tee, shadow_half, shadow_tee = reduce_all(
                (
                    jnp.sum(second_image * half_step),
                    jnp.sum(second_image * second_image),
                    jnp.sum(shadow * half_step),
                    jnp.sum(shadow * second_image),
                )
            )
        else:
            tee_half, tee_tee = reduce_all(
                (jnp.sum(second_image * half_step), jnp.sum(second_image * second_image))
            )
        omega_step = tee_half / tee_tee
        solution = solution + alpha_step * direction + omega_step * half_step
        residual = half_step - omega_step * second_image
        if iteration + 1 < ITERS:
            rho_next = shadow_half - omega_step * shadow_tee
            beta_step = rho_next / rho_now * (alpha_step / omega_step)
            direction = residual + beta_step * (direction - omega_step * image_vec)
            rho_now = rho_next
    return (solution, residual)


def solution(mesh):
    in_specs = (
        P(None, "lon", "lat"),
        P(None, "lon", "lat"),
        P(None, "lon", "lat"),
        P(None, "lon", "lat"),
        P(),
    )
    out_specs = (P(None, "lon", "lat"), P(None, "lon", "lat"))
    return jax.shard_map(body, mesh=mesh, in_specs=in_specs, out_specs=out_specs, check_vma=False)
```

profile of v0, /device:TPU:0, one launch (start us, length us, event | category | flops | bytes accessed | tf_op | source)
XLA Modules:
  0.0 255.7 jit_solution(18363924335968696570)
XLA Ops:
  0.6 1.1 copy.127
  1.9 2.4 collective-permute-start.3
  4.3 1.3 collective-permute-start.4
  5.6 3.5 %collective-permute-start.2 = (f32[2,70,4,2]{1,3,2,0:T(2,128)S(1)}, f32[2,70,4,2]{1,3,2,0:T(2,128)S(1)}, u32[]{:S(2)}, u32[]{:S(2)}) collective-permute-start(f32[2,70,4,2]{1,3,2,0:T(2,128)S(1)} %pad_maximum_fusion.6), channel_id=1, source_target_pairs={{0,16},{4,20},{8,24},{12,28},{16,0},{20,4},{24,8},{28,12},{1,17},{... | collective-permute-start | bytes 13448 | tf_op jit(solution)/shard_map/ppermute | solution.py:25
  9.1 1.5 collective-permute-start
  10.7 3.2 %collective-permute-start.1 = (f32[2,70,1,128]{1,3,2,0:T(8,128)S(1)}, f32[2,70,1,128]{1,3,2,0:T(8,128)S(1)}, u32[]{:S(2)}, u32[]{:S(2)}) collective-permute-start(f32[2,70,1,128]{1,3,2,0:T(8,128)S(1)} %get-tuple-element.47), channel_id=1, source_target_pairs={{4,0},{8,4},{12,8},{16,12},{20,16},{24,20},{28,24},{0,28},{5,1},{9... | collective-permute-start | bytes 215048 | tf_op jit(solution)/shard_map/ppermute | solution.py:17
  16.1 1.1 collective-permute-done
  17.2 1.8 collective-permute-done.1
  19.3 2.6 %collective-permute-start.8 = (f32[1,70,4,1]{1,3,2,0:T(1,128)S(1)}, f32[1,70,4,1]{1,3,2,0:T(1,128)S(1)}, u32[]{:S(2)}, u32[]{:S(2)}) collective-permute-start(f32[1,70,4,1]{1,3,2,0:T(1,128)S(1)} %get-tuple-element.58), channel_id=1, source_target_pairs={{0,1},{1,2},{2,3},{4,5},{5,6},{6,7},{8,9},{9,10},{10,11},{12,13},{... | collective-permute-start | bytes 3368 | tf_op jit(solution)/shard_map/ppermute | solution.py:16
  21.9 1.3 collective-permute-start.9
  23.3 4.7 %collective-permute-start.6 = (f32[1,70,1,128]{1,3,2,0:T(8,128)S(1)}, f32[1,70,1,128]{1,3,2,0:T(8,128)S(1)}, u32[]{:S(2)}, u32[]{:S(2)}) collective-permute-start(f32[1,70,1,128]{1,3,2,0:T(8,128)S(1)} %get-tuple-element.57), channel_id=1, source_target_pairs={{4,0},{8,4},{12,8},{16,12},{20,16},{24,20},{28,24},{0,28},{5,1},{9... | collective-permute-start | bytes 107528 | tf_op jit(solution)/shard_map/ppermute | solution.py:17
  28.2 4.3 %collective-permute-done.7 = f32[1,70,4,2]{1,3,2,0:T(2,128)S(1)} collective-permute-done((f32[1,70,4,2]{1,3,2,0:T(2,128)S(1)}, f32[1,70,4,2]{1,3,2,0:T(2,128)S(1)}, u32[]{:S(2)}, u32[]{:S(2)}) %collective-permute-start.7) | collective-permute-done | bytes 2272 | tf_op jit(solution)/shard_map/ppermute | solution.py:25
  33.5 2.5 collective-permute-start.13
  36.1 1.3 collective-permute-start.14
  37.4 4.7 %collective-permute-start.11 = (f32[2,70,1,128]{1,3,2,0:T(8,128)S(1)}, f32[2,70,1,128]{1,3,2,0:T(8,128)S(1)}, u32[]{:S(2)}, u32[]{:S(2)}) collective-permute-start(f32[2,70,1,128]{1,3,2,0:T(8,128)S(1)} %get-tuple-element.43), channel_id=1, source_target_pairs={{4,0},{8,4},{12,8},{16,12},{20,16},{24,20},{28,24},{0,28},{5,1},{9... | collective-permute-start | bytes 215048 | tf_op jit(solution)/shard_map/ppermute | solution.py:17
  42.1 43.8 %all-reduce.12 = (f32[]{:T(128)}, f32[]{:T(128)}) all-reduce(f32[]{:T(128)} %get-tuple-element.15, f32[]{:T(128)} %get-tuple-element.14), channel_id=1, replica_groups=mesh['lon'=8,'lat'=4] {'lon','lat'}, use_global_device_ids=true, to_apply=%region_1.2 | all-reduce | flops 2 | bytes 16 | tf_op jit(solution)/shard_map/psum | solution.py:42
  87.8 1.7 multiply_reduce_fusion.3
  89.5 40.3 %all-reduce.11 = (f32[]{:T(128)}, f32[]{:T(128)}, f32[]{:T(128)}, f32[]{:T(128)}) all-reduce(f32[]{:T(128)} %get-tuple-element.13, f32[]{:T(128)} %get-tuple-element.12, f32[]{:T(128)} %get-tuple-element.11, f32[]{:T(128)} %get-tuple-element.10), channel_id=1, replica_groups=mesh['lon'=8,'lat'=4] {'lon','lat'}, use_global_device_ids=true, to_apply=%region_9.10 | all-reduce | flops 4 | bytes 32 | tf_op jit(solution)/shard_map/psum | solution.py:42
  136.6 1.3 collective-permute-start.18
  137.9 1.3 collective-permute-start.19
  139.2 2.3 collective-permute-start.15
  141.5 2.4 collective-permute-start.16
  144.0 1.1 collective-permute-start.17
  145.3 3.3 %collective-permute-done.17 = f32[1,70,4,2]{1,3,2,0:T(2,128)S(1)} collective-permute-done((f32[1,70,4,2]{1,3,2,0:T(2,128)S(1)}, f32[1,70,4,2]{1,3,2,0:T(2,128)S(1)}, u32[]{:S(2)}, u32[]{:S(2)}) %collective-permute-start.17) | collective-permute-done | bytes 2272 | tf_op jit(solution)/shard_map/ppermute | solution.py:25
  150.3 3.9 %collective-permute-start.23 = (f32[2,70,4,1]{1,3,2,0:T(1,128)S(1)}, f32[2,70,4,1]{1,3,2,0:T(1,128)S(1)}, u32[]{:S(2)}, u32[]{:S(2)}) collective-permute-start(f32[2,70,4,1]{1,3,2,0:T(1,128)S(1)} %get-tuple-element.39), channel_id=1, source_target_pairs={{0,1},{1,2},{2,3},{4,5},{5,6},{6,7},{8,9},{9,10},{10,11},{12,13},{... | collective-permute-start | bytes 6728 | tf_op jit(solution)/shard_map/ppermute | solution.py:16
  154.3 1.3 collective-permute-start.24
  155.6 4.7 %collective-permute-start.21 = (f32[2,70,1,128]{1,3,2,0:T(8,128)}, f32[2,70,1,128]{1,3,2,0:T(8,128)}, u32[]{:S(2)}, u32[]{:S(2)}) collective-permute-start(f32[2,70,1,128]{1,3,2,0:T(8,128)} %get-tuple-element.38), channel_id=1, source_target_pairs={{4,0},{8,4},{12,8},{16,12},{20,16},{24,20},{28,24},{0,28},{5,1},{9... | collective-permute-start | bytes 215048 | tf_op jit(solution)/shard_map/ppermute | solution.py:17
  160.3 40.7 %psum.69 = f32[]{:T(128)} all-reduce(f32[]{:T(128)} %get-tuple-element.27), channel_id=1, replica_groups=mesh['lon'=8,'lat'=4] {'lon','lat'}, use_global_device_ids=true, to_apply=%region_13.14 | all-reduce | flops 1 | bytes 8 | tf_op jit(solution)/shard_map/psum | solution.py:42
  201.8 3.1 %collective-permute-start.22 = (f32[2,70,4,2]{1,3,2,0:T(2,128)S(1)}, f32[2,70,4,2]{1,3,2,0:T(2,128)S(1)}, u32[]{:S(2)}, u32[]{:S(2)}) collective-permute-start(f32[2,70,4,2]{1,3,2,0:T(2,128)S(1)} %pad_maximum_fusion.8), channel_id=1, source_target_pairs={{0,16},{4,20},{8,24},{12,28},{16,0},{20,4},{24,8},{28,12},{1,17},{... | collective-permute-start | bytes 13448 | tf_op jit(solution)/shard_map/ppermute | solution.py:25
  206.7 1.0 pad_maximum_fusion.2
  208.6 43.1 %all-reduce.10 = (f32[]{:T(128)}, f32[]{:T(128)}) all-reduce(f32[]{:T(128)} %get-tuple-element.9, f32[]{:T(128)} %get-tuple-element.8), channel_id=1, replica_groups=mesh['lon'=8,'lat'=4] {'lon','lat'}, use_global_device_ids=true, to_apply=%region_15.16 | all-reduce | flops 2 | bytes 16 | tf_op jit(solution)/shard_map/psum | solution.py:42
  253.0 1.1 multiply_subtract_fusion
  (89 shorter events, 11.3 us)
Async XLA Ops:
  0.6 1.1 copy-start.1
  1.9 14.0 %collective-permute-start.3 = (f32[2,70,4,1]{1,3,2,0:T(1,128)S(1)}, f32[2,70,4,1]{1,3,2,0:T(1,128)S(1)}, u32[]{:S(2)}, u32[]{:S(2)}) collective-permute-start(f32[2,70,4,1]{1,3,2,0:T(1,128)S(1)} %get-tuple-element.48), channel_id=1, source_target_pairs={{0,1},{1,2},{2,3},{4,5},{5,6},{6,7},{8,9},{9,10},{10,11},{12,13},{... | collective-permute-start | bytes 6728 | tf_op jit(solution)/shard_map/ppermute | solution.py:16
  4.3 11.6 %collective-permute-start.4 = (f32[2,70,4,1]{1,3,2,0:T(1,128)S(1)}, f32[2,70,4,1]{1,3,2,0:T(1,128)S(1)}, u32[]{:S(2)}, u32[]{:S(2)}) collective-permute-start(f32[2,70,4,1]{1,3,2,0:T(1,128)S(1)} %get-tuple-element.49), channel_id=1, source_target_pairs={{1,0},{2,1},{3,2},{5,4},{6,5},{7,6},{9,8},{10,9},{11,10},{13,12},{... | collective-permute-start | bytes 6728 | tf_op jit(solution)/shard_map/ppermute | solution.py:17
  5.6 10.3 %collective-permute-start.2 = (f32[2,70,4,2]{1,3,2,0:T(2,128)S(1)}, f32[2,70,4,2]{1,3,2,0:T(2,128)S(1)}, u32[]{:S(2)}, u32[]{:S(2)}) collective-permute-start(f32[2,70,4,2]{1,3,2,0:T(2,128)S(1)} %pad_maximum_fusion.6), channel_id=1, source_target_pairs={{0,16},{4,20},{8,24},{12,28},{16,0},{20,4},{24,8},{28,12},{1,17},{... | collective-permute-start | bytes 13448 | tf_op jit(solution)/shard_map/ppermute | solution.py:25
  9.1 8.0 %collective-permute-start = (f32[2,70,1,128]{1,3,2,0:T(8,128)S(1)}, f32[2,70,1,128]{1,3,2,0:T(8,128)S(1)}, u32[]{:S(2)}, u32[]{:S(2)}) collective-permute-start(f32[2,70,1,128]{1,3,2,0:T(8,128)S(1)} %get-tuple-element.46), channel_id=1, source_target_pairs={{0,4},{4,8},{8,12},{12,16},{16,20},{20,24},{24,28},{28,0},{1,5},{5... | collective-permute-start | bytes 215048 | tf_op jit(solution)/shard_map/ppermute | solution.py:16
  10.7 3.3 %copy-start.4 = (f32[69]{0:T(128)S(1)}, f32[69]{0:T(128)}, u32[]{:S(2)}) copy-start(f32[69]{0:T(128)} %param.9) | copy-start | bytes 832
  10.7 8.3 %collective-permute-start.1 = (f32[2,70,1,128]{1,3,2,0:T(8,128)S(1)}, f32[2,70,1,128]{1,3,2,0:T(8,128)S(1)}, u32[]{:S(2)}, u32[]{:S(2)}) collective-permute-start(f32[2,70,1,128]{1,3,2,0:T(8,128)S(1)} %get-tuple-element.47), channel_id=1, source_target_pairs={{4,0},{8,4},{12,8},{16,12},{20,16},{24,20},{28,24},{0,28},{5,1},{9... | collective-permute-start | bytes 215048 | tf_op jit(solution)/shard_map/ppermute | solution.py:17
  13.9 0.9 copy-start.2
  14.8 0.9 copy-start.3
  19.3 8.9 %collective-permute-start.8 = (f32[1,70,4,1]{1,3,2,0:T(1,128)S(1)}, f32[1,70,4,1]{1,3,2,0:T(1,128)S(1)}, u32[]{:S(2)}, u32[]{:S(2)}) collective-permute-start(f32[1,70,4,1]{1,3,2,0:T(1,128)S(1)} %get-tuple-element.58), channel_id=1, source_target_pairs={{0,1},{1,2},{2,3},{4,5},{5,6},{6,7},{8,9},{9,10},{10,11},{12,13},{... | collective-permute-start | bytes 3368 | tf_op jit(solution)/shard_map/ppermute | solution.py:16
  21.9 6.2 %collective-permute-start.9 = (f32[1,70,4,1]{1,3,2,0:T(1,128)S(1)}, f32[1,70,4,1]{1,3,2,0:T(1,128)S(1)}, u32[]{:S(2)}, u32[]{:S(2)}) collective-permute-start(f32[1,70,4,1]{1,3,2,0:T(1,128)S(1)} %get-tuple-element.59), channel_id=1, source_target_pairs={{1,0},{2,1},{3,2},{5,4},{6,5},{7,6},{9,8},{10,9},{11,10},{13,12},{... | collective-permute-start | bytes 3368 | tf_op jit(solution)/shard_map/ppermute | solution.py:17
  23.2 9.3 %collective-permute-start.5 = (f32[1,70,1,128]{1,3,2,0:T(8,128)S(1)}, f32[1,70,1,128]{1,3,2,0:T(8,128)S(1)}, u32[]{:S(2)}, u32[]{:S(2)}) collective-permute-start(f32[1,70,1,128]{1,3,2,0:T(8,128)S(1)} %get-tuple-element.56), channel_id=1, source_target_pairs={{0,4},{4,8},{8,12},{12,16},{16,20},{20,24},{24,28},{28,0},{1,5},{5... | collective-permute-start | bytes 107528 | tf_op jit(solution)/shard_map/ppermute | solution.py:16
  23.3 9.3 %collective-permute-start.6 = (f32[1,70,1,128]{1,3,2,0:T(8,128)S(1)}, f32[1,70,1,128]{1,3,2,0:T(8,128)S(1)}, u32[]{:S(2)}, u32[]{:S(2)}) collective-permute-start(f32[1,70,1,128]{1,3,2,0:T(8,128)S(1)} %get-tuple-element.57), channel_id=1, source_target_pairs={{4,0},{8,4},{12,8},{16,12},{20,16},{24,20},{28,24},{0,28},{5,1},{9... | collective-permute-start | bytes 107528 | tf_op jit(solution)/shard_map/ppermute | solution.py:17
  28.0 4.5 %collective-permute-start.7 = (f32[1,70,4,2]{1,3,2,0:T(2,128)S(1)}, f32[1,70,4,2]{1,3,2,0:T(2,128)S(1)}, u32[]{:S(2)}, u32[]{:S(2)}) collective-permute-start(f32[1,70,4,2]{1,3,2,0:T(2,128)S(1)} %pad_maximum_fusion.12), channel_id=1, source_target_pairs={{0,16},{4,20},{8,24},{12,28},{16,0},{20,4},{24,8},{28,12},{1,17},{... | collective-permute-start | bytes 6728 | tf_op jit(solution)/shard_map/ppermute | solution.py:25
  33.5 54.0 %collective-permute-start.13 = (f32[2,70,4,1]{1,3,2,0:T(1,128)S(1)}, f32[2,70,4,1]{1,3,2,0:T(1,128)S(1)}, u32[]{:S(2)}, u32[]{:S(2)}) collective-permute-start(f32[2,70,4,1]{1,3,2,0:T(1,128)S(1)} %get-tuple-element.44), channel_id=1, source_target_pairs={{0,1},{1,2},{2,3},{4,5},{5,6},{6,7},{8,9},{9,10},{10,11},{12,13},{... | collective-permute-start | bytes 6728 | tf_op jit(solution)/shard_map/ppermute | solution.py:16
  36.1 51.4 %collective-permute-start.14 = (f32[2,70,4,1]{1,3,2,0:T(1,128)S(1)}, f32[2,70,4,1]{1,3,2,0:T(1,128)S(1)}, u32[]{:S(2)}, u32[]{:S(2)}) collective-permute-start(f32[2,70,4,1]{1,3,2,0:T(1,128)S(1)} %get-tuple-element.45), channel_id=1, source_target_pairs={{1,0},{2,1},{3,2},{5,4},{6,5},{7,6},{9,8},{10,9},{11,10},{13,12},{... | collective-permute-start | bytes 6728 | tf_op jit(solution)/shard_map/ppermute | solution.py:17
  37.4 50.3 %collective-permute-start.10 = (f32[2,70,1,128]{1,3,2,0:T(8,128)S(1)}, f32[2,70,1,128]{1,3,2,0:T(8,128)S(1)}, u32[]{:S(2)}, u32[]{:S(2)}) collective-permute-start(f32[2,70,1,128]{1,3,2,0:T(8,128)S(1)} %get-tuple-element.42), channel_id=1, source_target_pairs={{0,4},{4,8},{8,12},{12,16},{16,20},{20,24},{24,28},{28,0},{1,5},{5... | collective-permute-start | bytes 215048 | tf_op jit(solution)/shard_map/ppermute | solution.py:16
  37.4 50.2 %collective-permute-start.11 = (f32[2,70,1,128]{1,3,2,0:T(8,128)S(1)}, f32[2,70,1,128]{1,3,2,0:T(8,128)S(1)}, u32[]{:S(2)}, u32[]{:S(2)}) collective-permute-start(f32[2,70,1,128]{1,3,2,0:T(8,128)S(1)} %get-tuple-element.43), channel_id=1, source_target_pairs={{4,0},{8,4},{12,8},{16,12},{20,16},{24,20},{28,24},{0,28},{5,1},{9... | collective-permute-start | bytes 215048 | tf_op jit(solution)/shard_map/ppermute | solution.py:17
  42.1 45.4 %collective-permute-start.12 = (f32[2,70,4,2]{1,3,2,0:T(2,128)S(1)}, f32[2,70,4,2]{1,3,2,0:T(2,128)S(1)}, u32[]{:S(2)}, u32[]{:S(2)}) collective-permute-start(f32[2,70,4,2]{1,3,2,0:T(2,128)S(1)} %pad_maximum_fusion.7), channel_id=1, source_target_pairs={{0,16},{4,20},{8,24},{12,28},{16,0},{20,4},{24,8},{28,12},{1,17},{... | collective-permute-start | bytes 13448 | tf_op jit(solution)/shard_map/ppermute | solution.py:25
  136.6 8.6 %collective-permute-start.18 = (f32[1,70,4,1]{1,3,2,0:T(1,128)S(1)}, f32[1,70,4,1]{1,3,2,0:T(1,128)S(1)}, u32[]{:S(2)}, u32[]{:S(2)}) collective-permute-start(f32[1,70,4,1]{1,3,2,0:T(1,128)S(1)} %get-tuple-element.54), channel_id=1, source_target_pairs={{0,1},{1,2},{2,3},{4,5},{5,6},{6,7},{8,9},{9,10},{10,11},{12,13},{... | collective-permute-start | bytes 3368 | tf_op jit(solution)/shard_map/ppermute | solution.py:16
  137.9 7.3 %collective-permute-start.19 = (f32[1,70,4,1]{1,3,2,0:T(1,128)S(1)}, f32[1,70,4,1]{1,3,2,0:T(1,128)S(1)}, u32[]{:S(2)}, u32[]{:S(2)}) collective-permute-start(f32[1,70,4,1]{1,3,2,0:T(1,128)S(1)} %get-tuple-element.55), channel_id=1, source_target_pairs={{1,0},{2,1},{3,2},{5,4},{6,5},{7,6},{9,8},{10,9},{11,10},{13,12},{... | collective-permute-start | bytes 3368 | tf_op jit(solution)/shard_map/ppermute | solution.py:17
  139.2 9.4 %collective-permute-start.15 = (f32[1,70,1,128]{1,3,2,0:T(8,128)S(1)}, f32[1,70,1,128]{1,3,2,0:T(8,128)S(1)}, u32[]{:S(2)}, u32[]{:S(2)}) collective-permute-start(f32[1,70,1,128]{1,3,2,0:T(8,128)S(1)} %get-tuple-element.52), channel_id=1, source_target_pairs={{0,4},{4,8},{8,12},{12,16},{16,20},{20,24},{24,28},{28,0},{1,5},{5... | collective-permute-start | bytes 107528 | tf_op jit(solution)/shard_map/ppermute | solution.py:16
  141.5 7.1 %collective-permute-start.16 = (f32[1,70,1,128]{1,3,2,0:T(8,128)S(1)}, f32[1,70,1,128]{1,3,2,0:T(8,128)S(1)}, u32[]{:S(2)}, u32[]{:S(2)}) collective-permute-start(f32[1,70,1,128]{1,3,2,0:T(8,128)S(1)} %get-tuple-element.53), channel_id=1, source_target_pairs={{4,0},{8,4},{12,8},{16,12},{20,16},{24,20},{28,24},{0,28},{5,1},{9... | collective-permute-start | bytes 107528 | tf_op jit(solution)/shard_map/ppermute | solution.py:17
  144.0 4.6 %collective-permute-start.17 = (f32[1,70,4,2]{1,3,2,0:T(2,128)S(1)}, f32[1,70,4,2]{1,3,2,0:T(2,128)S(1)}, u32[]{:S(2)}, u32[]{:S(2)}) collective-permute-start(f32[1,70,4,2]{1,3,2,0:T(2,128)S(1)} %pad_maximum_fusion.13), channel_id=1, source_target_pairs={{0,16},{4,20},{8,24},{12,28},{16,0},{20,4},{24,8},{28,12},{1,17},{... | collective-permute-start | bytes 6728 | tf_op jit(solution)/shard_map/ppermute | solution.py:25
  150.3 55.7 %collective-permute-start.23 = (f32[2,70,4,1]{1,3,2,0:T(1,128)S(1)}, f32[2,70,4,1]{1,3,2,0:T(1,128)S(1)}, u32[]{:S(2)}, u32[]{:S(2)}) collective-permute-start(f32[2,70,4,1]{1,3,2,0:T(1,128)S(1)} %get-tuple-element.39), channel_id=1, source_target_pairs={{0,1},{1,2},{2,3},{4,5},{5,6},{6,7},{8,9},{9,10},{10,11},{12,13},{... | collective-permute-start | bytes 6728 | tf_op jit(solution)/shard_map/ppermute | solution.py:16
  154.3 51.8 %collective-permute-start.24 = (f32[2,70,4,1]{1,3,2,0:T(1,128)S(1)}, f32[2,70,4,1]{1,3,2,0:T(1,128)S(1)}, u32[]{:S(2)}, u32[]{:S(2)}) collective-permute-start(f32[2,70,4,1]{1,3,2,0:T(1,128)S(1)} %get-tuple-element.40), channel_id=1, source_target_pairs={{1,0},{2,1},{3,2},{5,4},{6,5},{7,6},{9,8},{10,9},{11,10},{13,12},{... | collective-permute-start | bytes 6728 | tf_op jit(solution)/shard_map/ppermute | solution.py:17
  155.6 51.1 %collective-permute-start.20 = (f32[2,70,1,128]{1,3,2,0:T(8,128)}, f32[2,70,1,128]{1,3,2,0:T(8,128)}, u32[]{:S(2)}, u32[]{:S(2)}) collective-permute-start(f32[2,70,1,128]{1,3,2,0:T(8,128)} %get-tuple-element.37), channel_id=1, source_target_pairs={{0,4},{4,8},{8,12},{12,16},{16,20},{20,24},{24,28},{28,0},{1,5},{5... | collective-permute-start | bytes 215048 | tf_op jit(solution)/shard_map/ppermute | solution.py:16
  155.6 51.0 %collective-permute-start.21 = (f32[2,70,1,128]{1,3,2,0:T(8,128)}, f32[2,70,1,128]{1,3,2,0:T(8,128)}, u32[]{:S(2)}, u32[]{:S(2)}) collective-permute-start(f32[2,70,1,128]{1,3,2,0:T(8,128)} %get-tuple-element.38), channel_id=1, source_target_pairs={{4,0},{8,4},{12,8},{16,12},{20,16},{24,20},{28,24},{0,28},{5,1},{9... | collective-permute-start | bytes 215048 | tf_op jit(solution)/shard_map/ppermute | solution.py:17
  201.8 4.7 %collective-permute-start.22 = (f32[2,70,4,2]{1,3,2,0:T(2,128)S(1)}, f32[2,70,4,2]{1,3,2,0:T(2,128)S(1)}, u32[]{:S(2)}, u32[]{:S(2)}) collective-permute-start(f32[2,70,4,2]{1,3,2,0:T(2,128)S(1)} %pad_maximum_fusion.8), channel_id=1, source_target_pairs={{0,16},{4,20},{8,24},{12,28},{16,0},{20,4},{24,8},{28,12},{1,17},{... | collective-permute-start | bytes 13448 | tf_op jit(solution)/shard_map/ppermute | solution.py:25
  205.9 1.9 copy-start
where the time goes:
time: 257 us; the launch traced here: 256 us
  blocking collectives  168 us (65%)
  starting transfers between devices  50.8 us (20%)
  waiting for transfers between devices  11.1 us (4%)
  other arithmetic  10.9 us (4%)
  between operations  10.4 us (4%)
  local copies, waits for them, and re-layouts  4.62 us (2%)
    psum x4, blocking collectives, reduce_all(): return lax.psum(terms, ('lon', 'lat'))  168 us
    ppermute x10, starting transfers between devices, padded(): after = lax.ppermute(leading, axis, down)  26.3 us
    ppermute x10, starting transfers between devices, padded(): before = lax.ppermute(last, axis, up)  16.8 us
    ppermute x5, waiting for transfers between devices, shifted(): return lax.ppermute(value, axis, pairs)  8.13 us
    ppermute x5, starting transfers between devices, shifted(): return lax.ppermute(value, axis, pairs)  7.67 us
  transfers between devices with their start and end apart: 25, of which 5 were waited for; matrix products, arithmetic and copies ran while one was open for 1% of the time, Pallas kernels for 0%

commit v1 on v0

v1 whole, which is shorter than its diff:
```python
import jax
import jax.numpy as jnp
from jax import lax
from jax.sharding import PartitionSpec as P

AXES = ("lon", "lat")
ITERS = 2


def swap_pairs(n_lon, n_lat):
    half = n_lon // 2

    def flat(move):
        pairs = []
        for i in range(n_lon):
            for j in range(n_lat):
                k, m = move(i, j)
                pairs.append((i * n_lat + j, k * n_lat + m))
        return pairs

    def lat_odd(i, j):
        if j == 0 or j == n_lat - 1:
            return (i + half) % n_lon, j
        return i, ((j + 1) ^ 1) - 1

    return {
        "lon_even": flat(lambda i, j: (i ^ 1, j)),
        "lon_odd": flat(lambda i, j: ((((i + 1) ^ 1) - 1) % n_lon, j)),
        "lat_even": flat(lambda i, j: (i, j ^ 1)),
        "lat_odd": flat(lat_odd),
    }


def convolve(a, b):
    out = [None] * (len(a) + len(b) - 1)
    for i, x in enumerate(a):
        for j, y in enumerate(b):
            out[i + j] = x * y if out[i + j] is None else out[i + j] + x * y
    return out


def inner(a, b, moments):
    total = None
    for k, c in enumerate(convolve(a, b)):
        term = c * moments[k]
        total = term if total is None else total + term
    return total


def add_scaled(a, scale, b):
    out = []
    for k in range(max(len(a), len(b))):
        if k >= len(b):
            out.append(a[k])
        elif k >= len(a):
            out.append(scale * b[k])
        else:
            out.append(a[k] + scale * b[k])
    return out


def krylov_coefficients(moments, shift, one):
    def times_a(a):
        return add_scaled([0.0 * one] + list(a), shift, a)

    shadow = [one]
    residual = [one]
    direction = [one]
    solution = []
    rho = moments[0]
    for iteration in range(ITERS):
        image = times_a(direction)
        alpha = rho / inner(shadow, image, moments)
        half = add_scaled(residual, -alpha, image)
        second = times_a(half)
        omega = inner(second, half, moments) / inner(second, second, moments)
        solution = add_scaled(solution, alpha, direction)
        solution = add_scaled(solution, omega, half)
        residual = add_scaled(half, -omega, second)
        if iteration + 1 < ITERS:
            rho_next = inner(shadow, half, moments) - omega * inner(shadow, second, moments)
            beta = rho_next / rho * (alpha / omega)
            direction = add_scaled(residual, beta, add_scaled(direction, -omega, image))
            rho = rho_next
    return solution, residual


def body(right_side, first_guess, cell_scale, helmholtz_term, vertical_coupling):
    n_lon, n_lat = lax.axis_size("lon"), lax.axis_size("lat")
    devices = n_lon * n_lat
    pairs = swap_pairs(n_lon, n_lat)
    lon_even = lax.axis_index("lon") % 2 == 0
    lat_even = lax.axis_index("lat") % 2 == 0
    zero = jnp.zeros((1,), jnp.float32)
    below = jnp.concatenate([vertical_coupling, zero])[:, None, None]
    above = jnp.concatenate([zero, vertical_coupling])[:, None, None]
    diagonal = (4.0 + helmholtz_term) + (below + above)

    def everywhere(row):
        spread = jnp.broadcast_to(row[None], (devices,) + row.shape)
        return jnp.sum(lax.all_to_all(spread, AXES, 0, 0, tiled=True), axis=0)

    def stencil(q, west, east, north, south):
        level = jnp.zeros_like(q[:1])
        under = jnp.concatenate([q[1:], level], axis=0)
        over = jnp.concatenate([level, q[:-1]], axis=0)
        lon_sum = jnp.concatenate([q[:, 1:], east], axis=1) + jnp.concatenate([west, q[:, :-1]], axis=1)
        lat_sum = jnp.concatenate([q[:, :, 1:], south], axis=2) + jnp.concatenate([north, q[:, :, :-1]], axis=2)
        return diagonal * q - lon_sum - lat_sum - below * under - above * over

    def apply(q):
        west, east, north, south = q[:, :1], q[:, -1:], q[:, :, :1], q[:, :, -1:]
        a = lax.ppermute(jnp.where(lon_even, east, west), AXES, pairs["lon_even"])
        b = lax.ppermute(jnp.where(lon_even, west, east), AXES, pairs["lon_odd"])
        c = lax.ppermute(jnp.where(lat_even, south, north), AXES, pairs["lat_even"])
        d = lax.ppermute(jnp.where(lat_even, north, south), AXES, pairs["lat_odd"])
        return cell_scale * stencil(
            q,
            jnp.where(lon_even, b, a),
            jnp.where(lon_even, a, b),
            jnp.where(lat_even, d, c),
            jnp.where(lat_even, c, d),
        )

    scaled_guess = cell_scale * first_guess
    rough = right_side - cell_scale * stencil(
        scaled_guess,
        jnp.zeros_like(scaled_guess[:, :1]),
        jnp.zeros_like(scaled_guess[:, :1]),
        jnp.zeros_like(scaled_guess[:, :, :1]),
        jnp.zeros_like(scaled_guess[:, :, :1]),
    )
    weight = rough * rough
    lanes = jnp.arange(128)[None]
    row = jnp.where(
        lanes == 0,
        jnp.sum(weight * (cell_scale * cell_scale) * diagonal),
        jnp.where(lanes == 1, jnp.sum(weight), 0.0),
    )
    sums = everywhere(row)[0]
    shift = jnp.where(sums[1] > 0, sums[0] / sums[1], 1.0)

    vectors = [right_side - apply(scaled_guess)]
    for _ in range(2 * ITERS):
        last = vectors[-1]
        vectors.append(apply(cell_scale * last) - shift * last)
    row = jnp.zeros((1, 128), jnp.float32)
    for k in range(4 * ITERS + 1):
        row = jnp.where(lanes == k, jnp.sum(vectors[k // 2] * vectors[k - k // 2]), row)
    sums = everywhere(row)[0]
    moments = [sums[k] for k in range(4 * ITERS + 1)]
    solution, residual = krylov_coefficients(moments, shift, jnp.float32(1.0))
    out = first_guess
    for c, v in zip(solution, vectors):
        out = out + c * v
    rest = residual[0] * vectors[0]
    for c, v in zip(residual[1:], vectors[1:]):
        rest = rest + c * v
    return out, rest


def solution(mesh):
    spec = P(None, "lon", "lat")
    return jax.shard_map(
        body, mesh=mesh, in_specs=(spec, spec, spec, spec, P()), out_specs=(spec, spec), check_vma=False
    )
```

time: 257 us -> 107 us (0.42)
  blocking collectives: 168 us -> 10.8 us
  starting transfers between devices: 50.8 us -> 30.1 us
  between operations: 10.4 us -> 28.1 us
  waiting for transfers between devices: 11.1 us -> 18.3 us
  other arithmetic: 10.9 us -> 14 us
    psum x4 -> x0, blocking collectives: 168 us -> none  [reduce_all(): return lax.psum(terms, ('lon', 'lat'))]
    ppermute x25 -> x20, starting transfers between devices: 50.8 us -> 25.8 us  [the longest x5 15.6 us: apply(): b = lax.ppermute(jnp.where(lon_even, west, east), AXES, pairs['lon_odd'])]
    all_to_all x0 -> x1, blocking collectives: none -> 10.8 us  [everywhere(): return jnp.sum(lax.all_to_all(spread, AXES, 0, 0, tiled=True), axis=0)]
    select_n x5 -> x22, other arithmetic: 0.05 us -> 8.2 us  [the longest x1 5.55 us: body(): jnp.where(lanes == k, jnp.sum(vectors[k // 2] * vectors[k - k // 2]), row)]
    ppermute x25 -> x20, waiting for transfers between devices: 11.1 us -> 16.4 us  [the longest x5 14.7 us: apply(): d = lax.ppermute(jnp.where(lat_even, north, south), AXES, pairs['lat_odd'])]
    all_to_all x0 -> x1, starting transfers between devices: none -> 4.36 us  [everywhere(): return jnp.sum(lax.all_to_all(spread, AXES, 0, 0, tiled=True), axis=0)]
    unnamed x16 -> x10, local copies, waits for them, and re-layouts: 4.58 us -> 1.53 us
  transfers between devices with their start and end apart: 25 -> 21, of which waited for: 5 -> 9; matrix products, arithmetic and copies ran while one was open for 1% -> 3% of each run, Pallas kernels for 0% -> 0%
where the time goes in v1:
time: 107 us; the launch traced here: 106 us
  starting transfers between devices  30.1 us (28%)
  between operations  28.1 us (26%)
  waiting for transfers between devices  18.3 us (17%)
  other arithmetic  14 us (13%)
  blocking collectives  10.8 us (10%)
  local copies, waits for them, and re-layouts  4.6 us (4%)
    ppermute x5, starting transfers between devices, apply(): b = lax.ppermute(jnp.where(lon_even, west, east), AXES, pairs['lon_odd'])  15.6 us
    ppermute x5, waiting for transfers between devices, apply(): d = lax.ppermute(jnp.where(lat_even, north, south), AXES, pairs['lat_odd'])  14.7 us
    all_to_all x1, blocking collectives, everywhere(): return jnp.sum(lax.all_to_all(spread, AXES, 0, 0, tiled=True), axis=0)  10.8 us
    ppermute x5, starting transfers between devices, apply(): a = lax.ppermute(jnp.where(lon_even, east, west), AXES, pairs['lon_even'])  7.02 us
    select_n x1, other arithmetic, body(): jnp.where(lanes == k, jnp.sum(vectors[k // 2] * vectors[k - k // 2]), row)  5.55 us
    all_to_all x1, starting transfers between devices, everywhere(): return jnp.sum(lax.all_to_all(spread, AXES, 0, 0, tiled=True), axis=0)  4.36 us
    ppermute x5, starting transfers between devices, apply(): d = lax.ppermute(jnp.where(lat_even, north, south), AXES, pairs['lat_odd'])  2.82 us
  transfers between devices with their start and end apart: 21, of which 9 were waited for; matrix products, arithmetic and copies ran while one was open for 3% of the time, Pallas kernels for 0%

profile of v1, /device:TPU:0, one launch (start us, length us, event | category | flops | bytes accessed | tf_op | source)
XLA Modules:
  0.0 106.0 jit_solution(12827044729647265533)
XLA Ops:
  0.6 1.0 mul.584
  1.7 3.0 %collective-permute-start = (f32[70,1,128]{2,1,0:T(1,128)S(1)}, f32[70,1,128]{2,1,0:T(1,128)S(1)}, u32[]{:S(2)}, u32[]{:S(2)}) collective-permute-start(f32[70,1,128]{2,1,0:T(1,128)S(1)} %get-tuple-element.78), channel_id=1, source_target_pairs={{0,4},{1,5},{2,6},{3,7},{4,0},{5,1},{6,2},{7,3},{8,12},{9,13},{10,... | collective-permute-start | bytes 107528 | tf_op jit(solution)/shard_map/ppermute | solution.py:113
  4.8 3.6 %collective-permute-start.1 = (f32[70,1,128]{2,1,0:T(1,128)S(1)}, f32[70,1,128]{2,1,0:T(1,128)S(1)}, u32[]{:S(2)}, u32[]{:S(2)}) collective-permute-start(f32[70,1,128]{2,1,0:T(1,128)S(1)} %get-tuple-element.79), channel_id=1, source_target_pairs={{0,28},{1,29},{2,30},{3,31},{4,8},{5,9},{6,10},{7,11},{8,4},{9,5},... | collective-permute-start | bytes 107528 | tf_op jit(solution)/shard_map/ppermute | solution.py:114
  8.9 0.6 copy-done.4
  9.9 4.7 %collective-permute-done.3 = f32[70,4,1]{2,1,0:T(4,128)S(1)} collective-permute-done((f32[70,4,1]{2,1,0:T(4,128)S(1)}, f32[70,4,1]{2,1,0:T(4,128)S(1)}, u32[]{:S(2)}, u32[]{:S(2)}) %collective-permute-start.3) | collective-permute-done | bytes 1152 | tf_op jit(solution)/shard_map/ppermute | solution.py:116
  14.7 0.8 copy-done.1
  15.7 1.2 %multiply_reduce_fusion.9 = (f32[]{:T(128)}, f32[]{:T(128)}, f32[70,4,128]{2,1,0:T(4,128)S(1)}, f32[70,4,128]{2,1,0:T(4,128)S(1)}) fusion(f32[70,4,128]{2,1,0:T(4,128)S(1)} %copy-done, f32[70]{0:T(128)S(1)} %get-tuple-element.107, f32[70,4,128]{2,1,0:T(4,128)S(1)} %copy-done.1, f32[70,4,128]{2,1,0:T(4,128)S(1)} %copy-done.3, ...), kind=kLoop, calls=%fused_computation.51 | loop fusion | flops 1146878 | bytes 1717072 | tf_op jit(solution)/shard_map/reduce_sum | solution.py:137
  17.6 1.3 %compare_select_fusion.10 = f32[128]{0:T(128)S(1)} fusion(f32[]{:T(128)} %get-tuple-element.12, f32[]{:T(128)} %get-tuple-element.11), kind=kLoop, calls=%fused_computation.106 | loop fusion | flops 512 | bytes 520 | tf_op jit(solution)/shard_map/jit(_where)/select_n | solution.py:135
  18.9 0.6 broadcast_in_dim.58
  19.6 4.4 %all-to-all-start = ((f32[32,1,128]{2,1,0:T(1,128)}), f32[32,1,128]{2,1,0:T(1,128)S(1)}, u32[]{:S(2)}, u32[]{:S(2)}) async-start(f32[32,1,128]{2,1,0:T(1,128)} %broadcast_in_dim.58), calls=%async_computation | async-start | bytes 32768 | tf_op jit(solution)/shard_map/all_to_all | solution.py:101
  23.9 1.8 %collective-permute-start.4 = (f32[70,1,128]{2,1,0:T(1,128)S(1)}, f32[70,1,128]{2,1,0:T(1,128)S(1)}, u32[]{:S(2)}, u32[]{:S(2)}) collective-permute-start(f32[70,1,128]{2,1,0:T(1,128)S(1)} %get-tuple-element.68), channel_id=1, source_target_pairs={{0,4},{1,5},{2,6},{3,7},{4,0},{5,1},{6,2},{7,3},{8,12},{9,13},{10,... | collective-permute-start | bytes 107528 | tf_op jit(solution)/shard_map/ppermute | solution.py:113
  25.8 3.3 %collective-permute-start.5 = (f32[70,1,128]{2,1,0:T(1,128)S(1)}, f32[70,1,128]{2,1,0:T(1,128)S(1)}, u32[]{:S(2)}, u32[]{:S(2)}) collective-permute-start(f32[70,1,128]{2,1,0:T(1,128)S(1)} %get-tuple-element.69), channel_id=1, source_target_pairs={{0,28},{1,29},{2,30},{3,31},{4,8},{5,9},{6,10},{7,11},{8,4},{9,5},... | collective-permute-start | bytes 107528 | tf_op jit(solution)/shard_map/ppermute | solution.py:114
  29.1 1.9 %all-to-all-done = f32[32,1,128]{2,1,0:T(1,128)S(1)} async-done(((f32[32,1,128]{2,1,0:T(1,128)}), f32[32,1,128]{2,1,0:T(1,128)S(1)}, u32[]{:S(2)}, u32[]{:S(2)}) %all-to-all-start) | async-done | bytes 16416 | tf_op jit(solution)/shard_map/all_to_all | solution.py:101
  31.1 0.6 fusion.56
  34.7 0.7 collective-permute-start.11
  35.4 0.6 collective-permute-start.8
  36.0 3.3 %collective-permute-start.9 = (f32[70,1,128]{2,1,0:T(1,128)S(1)}, f32[70,1,128]{2,1,0:T(1,128)S(1)}, u32[]{:S(2)}, u32[]{:S(2)}) collective-permute-start(f32[70,1,128]{2,1,0:T(1,128)S(1)} %get-tuple-element.59), channel_id=1, source_target_pairs={{0,28},{1,29},{2,30},{3,31},{4,8},{5,9},{6,10},{7,11},{8,4},{9,5},... | collective-permute-start | bytes 107528 | tf_op jit(solution)/shard_map/ppermute | solution.py:114
  39.3 3.4 %collective-permute-done.11 = f32[70,4,1]{2,1,0:T(4,128)S(1)} collective-permute-done((f32[70,4,1]{2,1,0:T(4,128)S(1)}, f32[70,4,1]{2,1,0:T(4,128)S(1)}, u32[]{:S(2)}, u32[]{:S(2)}) %collective-permute-start.11) | collective-permute-done | bytes 1152 | tf_op jit(solution)/shard_map/ppermute | solution.py:116
  43.8 1.0 collective-permute-start.15
  44.8 1.1 collective-permute-start.12
  45.9 2.3 %collective-permute-start.13 = (f32[70,1,128]{2,1,0:T(1,128)S(1)}, f32[70,1,128]{2,1,0:T(1,128)S(1)}, u32[]{:S(2)}, u32[]{:S(2)}) collective-permute-start(f32[70,1,128]{2,1,0:T(1,128)S(1)} %get-tuple-element.49), channel_id=1, source_target_pairs={{0,28},{1,29},{2,30},{3,31},{4,8},{5,9},{6,10},{7,11},{8,4},{9,5},... | collective-permute-start | bytes 107528 | tf_op jit(solution)/shard_map/ppermute | solution.py:114
  48.2 3.3 %collective-permute-done.15 = f32[70,4,1]{2,1,0:T(4,128)S(1)} collective-permute-done((f32[70,4,1]{2,1,0:T(4,128)S(1)}, f32[70,4,1]{2,1,0:T(4,128)S(1)}, u32[]{:S(2)}, u32[]{:S(2)}) %collective-permute-start.15) | collective-permute-done | bytes 1152 | tf_op jit(solution)/shard_map/ppermute | solution.py:116
  51.5 1.1 %collective-permute-done.13 = f32[70,1,128]{2,1,0:T(1,128)S(1)} collective-permute-done((f32[70,1,128]{2,1,0:T(1,128)S(1)}, f32[70,1,128]{2,1,0:T(1,128)S(1)}, u32[]{:S(2)}, u32[]{:S(2)}) %collective-permute-start.13) | collective-permute-done | bytes 35872 | tf_op jit(solution)/shard_map/ppermute | solution.py:114
  53.6 0.9 collective-permute-start.19
  54.5 0.5 collective-permute-start.16
  55.0 3.2 %collective-permute-start.17 = (f32[70,1,128]{2,1,0:T(1,128)S(1)}, f32[70,1,128]{2,1,0:T(1,128)S(1)}, u32[]{:S(2)}, u32[]{:S(2)}) collective-permute-start(f32[70,1,128]{2,1,0:T(1,128)S(1)} %get-tuple-element.39), channel_id=1, source_target_pairs={{0,28},{1,29},{2,30},{3,31},{4,8},{5,9},{6,10},{7,11},{8,4},{9,5},... | collective-permute-start | bytes 107528 | tf_op jit(solution)/shard_map/ppermute | solution.py:114
  58.1 3.3 %collective-permute-done.19 = f32[70,4,1]{2,1,0:T(4,128)S(1)} collective-permute-done((f32[70,4,1]{2,1,0:T(4,128)S(1)}, f32[70,4,1]{2,1,0:T(4,128)S(1)}, u32[]{:S(2)}, u32[]{:S(2)}) %collective-permute-start.19) | collective-permute-done | bytes 1152 | tf_op jit(solution)/shard_map/ppermute | solution.py:116
  61.7 1.3 %multiply_reduce_fusion.8 = (f32[]{:T(128)}, f32[]{:T(128)}, f32[]{:T(128)}, f32[]{:T(128)}, f32[]{:T(128)}, /*index=5*/f32[]{:T(128)}, f32[]{:T(128)}, f32[]{:T(128)}, f32[]{:T(128)}, f32[70,4,128]{2,1,0:T(4,128)S(1)}) fusion(f32[70,4,128]{2,1,0:T(4,128)S(1)} %get-tuple-element.15, f32[70,4,128]{2,1,0:T(4,128)S(1)} %get-tuple-element.17, ...), kind=kLoop, calls=%fused_computation.50 | loop fusion | flops 1290231 | bytes 2003824 | tf_op jit(solution)/shard_map/reduce_sum | solution.py:149
  63.0 5.5 %compare_select_fusion.6 = f32[128]{0:T(128)S(1)} fusion(f32[]{:T(128)} %get-tuple-element.7, f32[]{:T(128)} %get-tuple-element.6, f32[]{:T(128)} %get-tuple-element.8, f32[]{:T(128)} %get-tuple-element.5, f32[]{:T(128)} %get-tuple-element.9, f32[]{:T(128)} %get-tuple-element.4, f32[]{:T(128)} %get-tuple-element.10, f32[]{:T(128)} %get-tuple-element.3, ...), kind=kLoop, calls=%fused_computation.102 | loop fusion | flops 2304 | bytes 548 | tf_op jit(solution)/shard_map/jit(_where)/select_n | solution.py:149
  68.5 10.8 %all_to_all.10 = f32[32,1,128]{2,1,0:T(1,128)S(1)} all-to-all(f32[32,1,128]{2,1,0:T(1,128)S(1)} %broadcast_in_dim.68), channel_id=1, replica_groups=mesh['lon'=8,'lat'=4] {'lon','lat'}, dimensions={0} | all-to-all | bytes 32768 | tf_op jit(solution)/shard_map/all_to_all | solution.py:101
  79.4 0.7 fusion.55
  105.2 0.8 multiply_add_fusion
  (72 shorter events, 5.5 us)
Async XLA Ops:
  1.7 12.9 %collective-permute-start = (f32[70,1,128]{2,1,0:T(1,128)S(1)}, f32[70,1,128]{2,1,0:T(1,128)S(1)}, u32[]{:S(2)}, u32[]{:S(2)}) collective-permute-start(f32[70,1,128]{2,1,0:T(1,128)S(1)} %get-tuple-element.78), channel_id=1, source_target_pairs={{0,4},{1,5},{2,6},{3,7},{4,0},{5,1},{6,2},{7,3},{8,12},{9,13},{10,... | collective-permute-start | bytes 107528 | tf_op jit(solution)/shard_map/ppermute | solution.py:113
  4.8 9.9 %collective-permute-start.1 = (f32[70,1,128]{2,1,0:T(1,128)S(1)}, f32[70,1,128]{2,1,0:T(1,128)S(1)}, u32[]{:S(2)}, u32[]{:S(2)}) collective-permute-start(f32[70,1,128]{2,1,0:T(1,128)S(1)} %get-tuple-element.79), channel_id=1, source_target_pairs={{0,28},{1,29},{2,30},{3,31},{4,8},{5,9},{6,10},{7,11},{8,4},{9,5},... | collective-permute-start | bytes 107528 | tf_op jit(solution)/shard_map/ppermute | solution.py:114
  8.5 1.4 %collective-permute-start.2 = (f32[70,4,1]{2,1,0:T(4,128)S(1)}, f32[70,4,1]{2,1,0:T(4,128)S(1)}, u32[]{:S(2)}, u32[]{:S(2)}) collective-permute-start(f32[70,4,1]{2,1,0:T(4,128)S(1)} %get-tuple-element.82), channel_id=1, source_target_pairs={{0,1},{1,0},{2,3},{3,2},{4,5},{5,4},{6,7},{7,6},{8,9},{9,8},{10,11... | collective-permute-start | bytes 3368 | tf_op jit(solution)/shard_map/ppermute | solution.py:115
  8.6 6.1 %collective-permute-start.3 = (f32[70,4,1]{2,1,0:T(4,128)S(1)}, f32[70,4,1]{2,1,0:T(4,128)S(1)}, u32[]{:S(2)}, u32[]{:S(2)}) collective-permute-start(f32[70,4,1]{2,1,0:T(4,128)S(1)} %get-tuple-element.83), channel_id=1, source_target_pairs={{0,16},{1,2},{2,1},{3,19},{4,20},{5,6},{6,5},{7,23},{8,24},{9,10},... | collective-permute-start | bytes 3368 | tf_op jit(solution)/shard_map/ppermute | solution.py:116
  8.8 0.7 copy-start.4
  14.6 0.9 copy-start.1
  14.6 1.0 copy-start.3
  14.7 1.0 copy-start
  17.3 11.8 %collective-permute-start.6 = (f32[70,4,1]{2,1,0:T(4,128)S(1)}, f32[70,4,1]{2,1,0:T(4,128)S(1)}, u32[]{:S(2)}, u32[]{:S(2)}) collective-permute-start(f32[70,4,1]{2,1,0:T(4,128)S(1)} %get-tuple-element.72), channel_id=1, source_target_pairs={{0,1},{1,0},{2,3},{3,2},{4,5},{5,4},{6,7},{7,6},{8,9},{9,8},{10,11... | collective-permute-start | bytes 3368 | tf_op jit(solution)/shard_map/ppermute | solution.py:115
  17.4 11.7 %collective-permute-start.7 = (f32[70,4,1]{2,1,0:T(4,128)S(1)}, f32[70,4,1]{2,1,0:T(4,128)S(1)}, u32[]{:S(2)}, u32[]{:S(2)}) collective-permute-start(f32[70,4,1]{2,1,0:T(4,128)S(1)} %get-tuple-element.73), channel_id=1, source_target_pairs={{0,16},{1,2},{2,1},{3,19},{4,20},{5,6},{6,5},{7,23},{8,24},{9,10},... | collective-permute-start | bytes 3368 | tf_op jit(solution)/shard_map/ppermute | solution.py:116
  19.6 11.5 %all-to-all-start = ((f32[32,1,128]{2,1,0:T(1,128)}), f32[32,1,128]{2,1,0:T(1,128)S(1)}, u32[]{:S(2)}, u32[]{:S(2)}) async-start(f32[32,1,128]{2,1,0:T(1,128)} %broadcast_in_dim.58), calls=%async_computation | async-start | bytes 32768 | tf_op jit(solution)/shard_map/all_to_all | solution.py:101
  23.9 9.7 %collective-permute-start.4 = (f32[70,1,128]{2,1,0:T(1,128)S(1)}, f32[70,1,128]{2,1,0:T(1,128)S(1)}, u32[]{:S(2)}, u32[]{:S(2)}) collective-permute-start(f32[70,1,128]{2,1,0:T(1,128)S(1)} %get-tuple-element.68), channel_id=1, source_target_pairs={{0,4},{1,5},{2,6},{3,7},{4,0},{5,1},{6,2},{7,3},{8,12},{9,13},{10,... | collective-permute-start | bytes 107528 | tf_op jit(solution)/shard_map/ppermute | solution.py:113
  25.8 7.9 %collective-permute-start.5 = (f32[70,1,128]{2,1,0:T(1,128)S(1)}, f32[70,1,128]{2,1,0:T(1,128)S(1)}, u32[]{:S(2)}, u32[]{:S(2)}) collective-permute-start(f32[70,1,128]{2,1,0:T(1,128)S(1)} %get-tuple-element.69), channel_id=1, source_target_pairs={{0,28},{1,29},{2,30},{3,31},{4,8},{5,9},{6,10},{7,11},{8,4},{9,5},... | collective-permute-start | bytes 107528 | tf_op jit(solution)/shard_map/ppermute | solution.py:114
  34.6 4.7 %collective-permute-start.10 = (f32[70,4,1]{2,1,0:T(4,128)S(1)}, f32[70,4,1]{2,1,0:T(4,128)S(1)}, u32[]{:S(2)}, u32[]{:S(2)}) collective-permute-start(f32[70,4,1]{2,1,0:T(4,128)S(1)} %get-tuple-element.62), channel_id=1, source_target_pairs={{0,1},{1,0},{2,3},{3,2},{4,5},{5,4},{6,7},{7,6},{8,9},{9,8},{10,11... | collective-permute-start | bytes 3368 | tf_op jit(solution)/shard_map/ppermute | solution.py:115
  34.7 8.0 %collective-permute-start.11 = (f32[70,4,1]{2,1,0:T(4,128)S(1)}, f32[70,4,1]{2,1,0:T(4,128)S(1)}, u32[]{:S(2)}, u32[]{:S(2)}) collective-permute-start(f32[70,4,1]{2,1,0:T(4,128)S(1)} %get-tuple-element.63), channel_id=1, source_target_pairs={{0,16},{1,2},{2,1},{3,19},{4,20},{5,6},{6,5},{7,23},{8,24},{9,10},... | collective-permute-start | bytes 3368 | tf_op jit(solution)/shard_map/ppermute | solution.py:116
  35.4 7.3 %collective-permute-start.8 = (f32[70,1,128]{2,1,0:T(1,128)S(1)}, f32[70,1,128]{2,1,0:T(1,128)S(1)}, u32[]{:S(2)}, u32[]{:S(2)}) collective-permute-start(f32[70,1,128]{2,1,0:T(1,128)S(1)} %get-tuple-element.58), channel_id=1, source_target_pairs={{0,4},{1,5},{2,6},{3,7},{4,0},{5,1},{6,2},{7,3},{8,12},{9,13},{10,... | collective-permute-start | bytes 107528 | tf_op jit(solution)/shard_map/ppermute | solution.py:113
  36.0 6.7 %collective-permute-start.9 = (f32[70,1,128]{2,1,0:T(1,128)S(1)}, f32[70,1,128]{2,1,0:T(1,128)S(1)}, u32[]{:S(2)}, u32[]{:S(2)}) collective-permute-start(f32[70,1,128]{2,1,0:T(1,128)S(1)} %get-tuple-element.59), channel_id=1, source_target_pairs={{0,28},{1,29},{2,30},{3,31},{4,8},{5,9},{6,10},{7,11},{8,4},{9,5},... | collective-permute-start | bytes 107528 | tf_op jit(solution)/shard_map/ppermute | solution.py:114
  43.7 4.5 %collective-permute-start.14 = (f32[70,4,1]{2,1,0:T(4,128)S(1)}, f32[70,4,1]{2,1,0:T(4,128)S(1)}, u32[]{:S(2)}, u32[]{:S(2)}) collective-permute-start(f32[70,4,1]{2,1,0:T(4,128)S(1)} %get-tuple-element.52), channel_id=1, source_target_pairs={{0,1},{1,0},{2,3},{3,2},{4,5},{5,4},{6,7},{7,6},{8,9},{9,8},{10,11... | collective-permute-start | bytes 3368 | tf_op jit(solution)/shard_map/ppermute | solution.py:115
  43.8 7.7 %collective-permute-start.15 = (f32[70,4,1]{2,1,0:T(4,128)S(1)}, f32[70,4,1]{2,1,0:T(4,128)S(1)}, u32[]{:S(2)}, u32[]{:S(2)}) collective-permute-start(f32[70,4,1]{2,1,0:T(4,128)S(1)} %get-tuple-element.53), channel_id=1, source_target_pairs={{0,16},{1,2},{2,1},{3,19},{4,20},{5,6},{6,5},{7,23},{8,24},{9,10},... | collective-permute-start | bytes 3368 | tf_op jit(solution)/shard_map/ppermute | solution.py:116
  44.8 6.7 %collective-permute-start.12 = (f32[70,1,128]{2,1,0:T(1,128)S(1)}, f32[70,1,128]{2,1,0:T(1,128)S(1)}, u32[]{:S(2)}, u32[]{:S(2)}) collective-permute-start(f32[70,1,128]{2,1,0:T(1,128)S(1)} %get-tuple-element.48), channel_id=1, source_target_pairs={{0,4},{1,5},{2,6},{3,7},{4,0},{5,1},{6,2},{7,3},{8,12},{9,13},{10,... | collective-permute-start | bytes 107528 | tf_op jit(solution)/shard_map/ppermute | solution.py:113
  45.9 6.7 %collective-permute-start.13 = (f32[70,1,128]{2,1,0:T(1,128)S(1)}, f32[70,1,128]{2,1,0:T(1,128)S(1)}, u32[]{:S(2)}, u32[]{:S(2)}) collective-permute-start(f32[70,1,128]{2,1,0:T(1,128)S(1)} %get-tuple-element.49), channel_id=1, source_target_pairs={{0,28},{1,29},{2,30},{3,31},{4,8},{5,9},{6,10},{7,11},{8,4},{9,5},... | collective-permute-start | bytes 107528 | tf_op jit(solution)/shard_map/ppermute | solution.py:114
  53.5 4.6 %collective-permute-start.18 = (f32[70,4,1]{2,1,0:T(4,128)S(1)}, f32[70,4,1]{2,1,0:T(4,128)S(1)}, u32[]{:S(2)}, u32[]{:S(2)}) collective-permute-start(f32[70,4,1]{2,1,0:T(4,128)S(1)} %get-tuple-element.42), channel_id=1, source_target_pairs={{0,1},{1,0},{2,3},{3,2},{4,5},{5,4},{6,7},{7,6},{8,9},{9,8},{10,11... | collective-permute-start | bytes 3368 | tf_op jit(solution)/shard_map/ppermute | solution.py:115
  53.6 7.8 %collective-permute-start.19 = (f32[70,4,1]{2,1,0:T(4,128)S(1)}, f32[70,4,1]{2,1,0:T(4,128)S(1)}, u32[]{:S(2)}, u32[]{:S(2)}) collective-permute-start(f32[70,4,1]{2,1,0:T(4,128)S(1)} %get-tuple-element.43), channel_id=1, source_target_pairs={{0,16},{1,2},{2,1},{3,19},{4,20},{5,6},{6,5},{7,23},{8,24},{9,10},... | collective-permute-start | bytes 3368 | tf_op jit(solution)/shard_map/ppermute | solution.py:116
  54.5 6.9 %collective-permute-start.16 = (f32[70,1,128]{2,1,0:T(1,128)S(1)}, f32[70,1,128]{2,1,0:T(1,128)S(1)}, u32[]{:S(2)}, u32[]{:S(2)}) collective-permute-start(f32[70,1,128]{2,1,0:T(1,128)S(1)} %get-tuple-element.38), channel_id=1, source_target_pairs={{0,4},{1,5},{2,6},{3,7},{4,0},{5,1},{6,2},{7,3},{8,12},{9,13},{10,... | collective-permute-start | bytes 107528 | tf_op jit(solution)/shard_map/ppermute | solution.py:113
  55.0 6.6 %collective-permute-start.17 = (f32[70,1,128]{2,1,0:T(1,128)S(1)}, f32[70,1,128]{2,1,0:T(1,128)S(1)}, u32[]{:S(2)}, u32[]{:S(2)}) collective-permute-start(f32[70,1,128]{2,1,0:T(1,128)S(1)} %get-tuple-element.39), channel_id=1, source_target_pairs={{0,28},{1,29},{2,30},{3,31},{4,8},{5,9},{6,10},{7,11},{8,4},{9,5},... | collective-permute-start | bytes 107528 | tf_op jit(solution)/shard_map/ppermute | solution.py:114
  94.5 10.7 %copy-start.2 = (f32[70,4,128]{2,1,0:T(4,128)S(1)}, f32[70,4,128]{2,1,0:T(4,128)}, u32[]{:S(2)}) copy-start(f32[70,4,128]{2,1,0:T(4,128)} %param.6) | copy-start | bytes 430084

commit v2 on v1

v2 whole, which is shorter than its diff:
```python
import functools

import jax
import jax.numpy as jnp
from jax import lax
from jax.experimental import pallas as pl
from jax.experimental.pallas import tpu as pltpu
from jax.sharding import PartitionSpec as P

AXES = ("lon", "lat")
ITERS = 2
LANES = 128
NEAR, FAR = 2, 3
GROUP = 8
VMEM = pl.BlockSpec(memory_space=pltpu.VMEM)
SMEM = pl.BlockSpec(memory_space=pltpu.SMEM)
FIRST = (("q", 1), ("q", 2), ("g", 1), ("g", 2), ("d", 1), ("d", 2), ("s", 1))
FIELDS = ("q", "g", "d", "s")


def swap_pairs(n_lon, n_lat):
    half = n_lon // 2

    def flat(move):
        pairs = []
        for i in range(n_lon):
            for j in range(n_lat):
                k, m = move(i, j)
                pairs.append((i * n_lat + j, k * n_lat + m))
        return pairs

    def lat_odd(i, j):
        if j == 0 or j == n_lat - 1:
            return (i + half) % n_lon, j
        return i, ((j + 1) ^ 1) - 1

    return {
        "lon_even": flat(lambda i, j: (i ^ 1, j)),
        "lon_odd": flat(lambda i, j: ((((i + 1) ^ 1) - 1) % n_lon, j)),
        "lat_even": flat(lambda i, j: (i, j ^ 1)),
        "lat_odd": flat(lat_odd),
    }


def convolve(a, b):
    out = [None] * (len(a) + len(b) - 1)
    for i, x in enumerate(a):
        for j, y in enumerate(b):
            out[i + j] = x * y if out[i + j] is None else out[i + j] + x * y
    return out


def inner(a, b, moments):
    total = None
    for k, c in enumerate(convolve(a, b)):
        term = c * moments[k]
        total = term if total is None else total + term
    return total


def add_scaled(a, scale, b):
    out = []
    for k in range(max(len(a), len(b))):
        if k >= len(b):
            out.append(a[k])
        elif k >= len(a):
            out.append(scale * b[k])
        else:
            out.append(a[k] + scale * b[k])
    return out


def krylov_coefficients(moments, shift, one):
    def times_a(a):
        return add_scaled([0.0 * one] + list(a), shift, a)

    shadow = [one]
    residual = [one]
    direction = [one]
    solution = []
    rho = moments[0]
    for iteration in range(ITERS):
        image = times_a(direction)
        alpha = rho / inner(shadow, image, moments)
        half = add_scaled(residual, -alpha, image)
        second = times_a(half)
        omega = inner(second, half, moments) / inner(second, second, moments)
        solution = add_scaled(solution, alpha, direction)
        solution = add_scaled(solution, omega, half)
        residual = add_scaled(half, -omega, second)
        if iteration + 1 < ITERS:
            rho_next = inner(shadow, half, moments) - omega * inner(shadow, second, moments)
            beta = rho_next / rho * (alpha / omega)
            direction = add_scaled(residual, beta, add_scaled(direction, -omega, image))
            rho = rho_next
    return solution, residual


def lanes_of(levels):
    return lax.broadcasted_iota(jnp.int32, (levels, LANES), 1)


def turn(value, shift):
    shift %= LANES
    return value if shift == 0 else pltpu.roll(value, shift, 1)


def plane(ref, column, columns, levels, shift=0):
    return ref.at[pl.ds((1 + shift) * columns + column, levels, stride=columns), :]


def clear_ends(ref, columns, levels):
    ref[0:columns, :] = jnp.zeros((columns, LANES), jnp.float32)
    ref[(levels + 1) * columns : (levels + 2) * columns, :] = jnp.zeros((columns, LANES), jnp.float32)


def column(ref, i, own, levels):
    return ref[pl.ds(i, levels, stride=own), :]


def shifted_rows(main, strip, lane):
    main_s, main_n = turn(main, -1), turn(main, 1)
    strip_s, strip_n = turn(strip, -1), turn(strip, 1)
    first, last = lane == 0, lane == LANES - 1
    return (
        jnp.where(last, strip_s, main_s) + jnp.where(first, strip_n, main_n),
        jnp.where(last, main_s, strip_s) + jnp.where(first, main_n, strip_n),
    )


def transformed(x, b, c, h, above, below):
    return {"q": c * x, "g": c * c, "d": (4.0 + h) + (above + below), "s": c * b}


def pack_kernel(own, levels, flags, x, b, c, h, above, below, to_a, to_b, lat_a, lat_b, *fields):
    lane = lanes_of(levels)
    group = lane // GROUP
    groups = LANES // GROUP
    lon_even, lat_even, pole = flags[0], flags[1], flags[2]
    store = dict(zip(FIELDS, fields))
    north = jnp.zeros((levels, LANES), jnp.float32)
    south = north
    for i in range(own):
        values = transformed(
            column(x, i, own, levels),
            column(b, i, own, levels),
            column(c, i, own, levels),
            column(h, i, own, levels),
            above[...],
            below[...],
        )
        for f, name in enumerate(FIELDS):
            store[name][pl.ds(i, levels, stride=own), :] = values[name]
            slot = f * own + i
            rolled = turn(values[name], GROUP * slot)
            north = jnp.where(group == slot, rolled, north)
            south = jnp.where(group == (slot - 1) % groups, rolled, south)
    for k, (name, distance) in enumerate(FIRST):
        east, west = own - distance, distance - 1
        a = jnp.where(lon_even == 1, east, west)
        to_a[k] = store[name][pl.ds(a, levels, stride=own), :]
        to_b[k] = store[name][pl.ds(east + west - a, levels, stride=own), :]
    even = jnp.full((levels, LANES), lat_even, jnp.int32) == 1
    over = jnp.full((levels, LANES), pole, jnp.int32) == 1
    lat_a[...] = jnp.where(even, south, north)
    other = jnp.where(even, north, south)
    mirror = other
    for bit in (1, 2, 4):
        mirror = jnp.where((lane & bit) != 0, turn(mirror, bit), turn(mirror, -bit))
    mirror = jnp.where(even, turn(mirror, -GROUP), turn(mirror, GROUP))
    lat_b[...] = jnp.where(over, mirror, other)


def shift_kernel(own, levels, x, b, c, h, above, below, out, q_ref):
    lane = lanes_of(levels)
    clear_ends(q_ref, own, levels)
    for i in range(own):
        plane(q_ref, i, own, levels)[...] = column(c, i, own, levels) * column(x, i, own, levels)
    weighted = jnp.zeros((levels, LANES), jnp.float32)
    total = weighted
    for i in range(own):
        q = plane(q_ref, i, own, levels)[...]
        scale = column(c, i, own, levels)
        diagonal = (4.0 + column(h, i, own, levels)) + (above[...] + below[...])
        near = jnp.where(lane == LANES - 1, 0.0, turn(q, -1)) + jnp.where(lane == 0, 0.0, turn(q, 1))
        if i > 0:
            near = near + plane(q_ref, i - 1, own, levels)[...]
        if i < own - 1:
            near = near + plane(q_ref, i + 1, own, levels)[...]
        near = near + below[...] * plane(q_ref, i, own, levels, 1)[...]
        near = near + above[...] * plane(q_ref, i, own, levels, -1)[...]
        rough = column(b, i, own, levels) - scale * (diagonal * q - near)
        weight = rough * rough
        total = total + weight
        weighted = weighted + weight * (scale * scale * diagonal)
    row_lane = lax.broadcasted_iota(jnp.int32, (1, LANES), 1)
    row = jnp.where(
        row_lane == 0,
        jnp.sum(weighted, keepdims=True),
        jnp.where(row_lane == 1, jnp.sum(total, keepdims=True), 0.0),
    )
    out[...] = jnp.broadcast_to(row[None], out.shape)


def lane_value(row, k):
    lane = lax.broadcasted_iota(jnp.int32, (1, LANES), 1)
    return jnp.sum(jnp.where(lane == k, row, 0.0), axis=1, keepdims=True)


def total_row(gathered):
    return jnp.sum(gathered[...], axis=0)


class Extended:
    def __init__(self, columns, levels, d, g, above, below, lane):
        self.columns, self.levels = columns, levels
        self.d, self.g = d, g
        self.above, self.below, self.lane = above, below, lane

    def at(self, pair, k, e, shift=0):
        return plane(pair[k], e, self.columns, self.levels, shift)[...]

    def put(self, pair, k, e, value):
        plane(pair[k], e, self.columns, self.levels)[...] = value

    def stencil(self, pair, e, strips=True):
        main, strip = self.at(pair, 0, e), self.at(pair, 1, e)
        near = shifted_rows(main, strip, self.lane)
        out = []
        for k, q in enumerate((main, strip) if strips else (main,)):
            side = self.at(pair, k, e - 1) + self.at(pair, k, e + 1)
            levels = self.below[...] * self.at(pair, k, e, 1) + self.above[...] * self.at(pair, k, e, -1)
            out.append((q, self.at(self.d, k, e) * q - (side + near[k]) - levels))
        return out


def first_kernel(own, levels, columns, flags, fq, fg, fd, fs, above, below, from_a, from_b, lat_a, lat_b,
                 strips_a, strips_b, sums, k0, k1, k1_strip, to_a, to_b, g_main, g_strip, d_main, d_strip,
                 shift_out, qa_main, qa_strip, qb_main, qb_strip, s_main, s_strip):
    lane = lanes_of(levels)
    low = lane < LANES // 2
    lon_even, lat_even = flags[0], flags[1]
    even = jnp.full((levels, LANES), lat_even, jnp.int32) == 1
    qa, qb = (qa_main, qa_strip), (qb_main, qb_strip)
    where_to = {"q": qa, "g": (g_main, g_strip), "d": (d_main, d_strip), "s": (s_main, s_strip)}
    ext = Extended(columns, levels, where_to["d"], where_to["g"], above, below, lane)
    for ref in (*qa, *qb):
        clear_ends(ref, columns, levels)

    row = total_row(sums)
    weighted, total = lane_value(row, 0), lane_value(row, 1)
    shift = jnp.where(total > 0.0, weighted / jnp.where(total > 0.0, total, 1.0), 1.0)
    shift_out[...] = jnp.broadcast_to(shift, shift_out.shape)
    shift = jnp.broadcast_to(shift, (levels, LANES))

    def unpack(north, south, name, i):
        slot = FIELDS.index(name) * own + i
        back = -GROUP * slot
        return jnp.where(low, turn(south, back), turn(north, back))

    def halves(a, b):
        return jnp.where(even, b, a), jnp.where(even, a, b)

    fields = dict(zip(FIELDS, (fq, fg, fd, fs)))
    north, south = halves(lat_a[...], lat_b[...])
    for name in FIELDS:
        for i in range(own):
            ext.put(where_to[name], 0, FAR + i, column(fields[name], i, own, levels))
            ext.put(where_to[name], 1, FAR + i, unpack(north, south, name, i))
    for block, tiles, east in ((from_a, strips_a, lon_even), (from_b, strips_b, 1 - lon_even)):
        north, south = halves(tiles[0], tiles[1])
        is_east = jnp.full((levels, LANES), east, jnp.int32) == 1
        for k, (name, distance) in enumerate(FIRST):
            e_east, e_west = FAR + own - 1 + distance, FAR - distance
            e = jnp.where(east == 1, e_east, e_west)
            ext.put(where_to[name], 0, e, block[k])
            strip = jnp.where(
                is_east,
                unpack(north, south, name, distance - 1),
                unpack(north, south, name, own - distance),
            )
            ext.put(where_to[name], 1, e, strip)
    for e in range(FAR - 1, FAR + own + 1):
        for k, (_, image) in enumerate(ext.stencil(qa, e)):
            value = ext.at(where_to["s"], k, e) - ext.at(where_to["g"], k, e) * image
            ext.put(qb, k, e, value)
            if k == 0 and FAR <= e < FAR + own:
                k0[pl.ds(e - FAR, levels, stride=own), :] = value
    for e in range(FAR, FAR + own):
        for k, (q, image) in enumerate(ext.stencil(qb, e)):
            value = ext.at(where_to["g"], k, e) * image - shift * q
            out = k1 if k == 0 else k1_strip
            out[pl.ds(e - FAR, levels, stride=own), :] = value
    for out, side in ((to_a, lon_even), (to_b, 1 - lon_even)):
        packed = jnp.zeros((levels, LANES), jnp.float32)
        for distance in range(1, FAR + 1):
            i = jnp.where(side == 1, own - distance, distance - 1)
            out[distance - 1] = k1[pl.ds(i, levels, stride=own), :]
            offset = 2 * GROUP * (distance - 1) + GROUP
            rolled = turn(k1_strip[pl.ds(i, levels, stride=own), :], offset)
            packed = jnp.where(lane // (2 * GROUP) == distance - 1, rolled, packed)
        out[FAR] = packed


def second_kernel(own, levels, columns, flags, k0, k1, k1_strip, from_a, from_b, g_main, g_strip, d_main, d_strip,
                  above, below, shift_row, k2, k3, k4, out, qa_main, qa_strip, qb_main, qb_strip):
    lane = lanes_of(levels)
    lon_even = flags[0]
    qa, qb = (qa_main, qa_strip), (qb_main, qb_strip)
    g = (g_main, g_strip)
    ext = Extended(columns, levels, (d_main, d_strip), g, above, below, lane)
    for ref in (*qa, *qb):
        clear_ends(ref, columns, levels)
    shift = jnp.broadcast_to(shift_row[...], (levels, LANES))
    for i in range(own):
        ext.put(qa, 0, FAR + i, column(k1, i, own, levels))
        ext.put(qa, 1, FAR + i, column(k1_strip, i, own, levels))
    for block, east in ((from_a, lon_even), (from_b, 1 - lon_even)):
        for distance in range(1, FAR + 1):
            e = jnp.where(east == 1, FAR + own - 1 + distance, FAR - distance)
            ext.put(qa, 0, e, block[distance - 1])
            ext.put(qa, 1, e, turn(block[FAR], -(2 * GROUP * (distance - 1) + GROUP)))
    source, target = qa, qb
    for step, reach in ((0, FAR - 1), (1, FAR - 2)):
        for e in range(FAR - reach, FAR + own + reach):
            for k, (q, image) in enumerate(ext.stencil(source, e)):
                value = ext.at(g, k, e) * image - shift * q
                ext.put(target, k, e, value)
                if k == 0 and FAR <= e < FAR + own:
                    (k2, k3)[step][pl.ds(e - FAR, levels, stride=own), :] = value
        source, target = target, source
    count = 4 * ITERS + 1
    sums = [jnp.zeros((levels, LANES), jnp.float32) for _ in range(count)]
    for i in range(own):
        e = FAR + i
        ((q, image),) = ext.stencil(source, e, strips=False)
        scale = ext.at(g, 0, e)
        last = scale * image - shift * q
        k4[pl.ds(i, levels, stride=own), :] = last
        v = [column(k0, i, own, levels), column(k1, i, own, levels), column(k2, i, own, levels), q, last]
        w = 1.0 / scale
        for k in range(count):
            if k % 2 == 0:
                lead = v[k // 2] * w
            sums[k] = sums[k] + lead * v[k - k // 2]
    row_lane = lax.broadcasted_iota(jnp.int32, (1, LANES), 1)
    row = jnp.zeros((1, LANES), jnp.float32)
    for k in range(count):
        row = jnp.where(row_lane == k, jnp.sum(sums[k], keepdims=True), row)
    out[...] = jnp.broadcast_to(row[None], out.shape)


def final_kernel(sums, shift_row, x, c, k0, k1, k2, k3, k4, out, rest):
    row = total_row(sums)
    moments = [lane_value(row, k) for k in range(4 * ITERS + 1)]
    shift = lane_value(shift_row[...], 0)
    solution, residual = krylov_coefficients(moments, shift, jnp.ones((1, 1), jnp.float32))
    vectors = (k0, k1, k2, k3, k4)
    inverse = 1.0 / c[...]

    def combined(coefficients):
        total = None
        for a, v in zip(coefficients, vectors):
            term = a * v[...]
            total = term if total is None else total + term
        return total * inverse

    out[...] = x[...] + combined(solution)
    rest[...] = combined(residual)


def body(right_side, first_guess, cell_scale, helmholtz_term, vertical_coupling):
    n_lon, n_lat = lax.axis_size("lon"), lax.axis_size("lat")
    levels, own, width = right_side.shape
    assert width == LANES and own >= FAR and len(FIELDS) * own * GROUP <= LANES
    assert n_lon % 4 == 0 and n_lat % 2 == 0
    columns = own + 2 * FAR
    pairs = swap_pairs(n_lon, n_lat)
    i, j = lax.axis_index("lon"), lax.axis_index("lat")
    flags = jnp.stack([1 - i % 2, 1 - j % 2, ((j == 0) | (j == n_lat - 1)).astype(jnp.int32)]).astype(jnp.int32)
    zero = jnp.zeros((1,), jnp.float32)
    below = jnp.broadcast_to(jnp.concatenate([vertical_coupling, zero])[:, None], (levels, LANES))
    above = jnp.broadcast_to(jnp.concatenate([zero, vertical_coupling])[:, None], (levels, LANES))
    b, x, c, h = (v.reshape(levels * own, LANES) for v in (right_side, first_guess, cell_scale, helmholtz_term))

    def real(*shape):
        return jax.ShapeDtypeStruct(shape, jnp.float32)

    def call(kernel, ins, outs, scratch=(), flagged=True):
        return pl.pallas_call(
            kernel,
            out_shape=tuple(outs) if len(outs) > 1 else outs[0],
            in_specs=[SMEM] * flagged + [VMEM] * (len(ins) - flagged),
            out_specs=tuple([VMEM] * len(outs)) if len(outs) > 1 else VMEM,
            scratch_shapes=[pltpu.VMEM(s, jnp.float32) for s in scratch],
            compiler_params=pltpu.CompilerParams(vmem_limit_bytes=32 * 1024 * 1024),
        )(*ins)

    def swap(value, name):
        return lax.ppermute(value, AXES, pairs[name])

    def everywhere(rows):
        return lax.all_to_all(rows, AXES, 0, 0, tiled=True)

    whole = real(levels * own, LANES)
    tile = real(levels, LANES)
    rows = real(n_lon * n_lat, 1, LANES)
    padded = ((levels + 2) * own, LANES)
    extended = ((levels + 2) * columns, LANES)

    to_a, to_b, lat_a, lat_b, *fields = call(
        functools.partial(pack_kernel, own, levels),
        (flags, x, b, c, h, above, below),
        [real(len(FIRST), levels, LANES)] * 2 + [tile] * 2 + [whole] * len(FIELDS),
    )
    from_a, from_b = swap(to_a, "lon_even"), swap(to_b, "lon_odd")
    lat_a, lat_b = swap(lat_a, "lat_even"), swap(lat_b, "lat_odd")
    strips = jnp.stack([lat_a, lat_b])
    strips_a, strips_b = swap(strips, "lon_even"), swap(strips, "lon_odd")
    weights = call(
        functools.partial(shift_kernel, own, levels), (x, b, c, h, above, below), [rows], [padded], flagged=False
    )
    weights = everywhere(weights)
    k0, k1, k1_strip, to_a, to_b, *coefficients, shift = call(
        functools.partial(first_kernel, own, levels, columns),
        (flags, *fields, above, below, from_a, from_b, lat_a, lat_b, strips_a, strips_b, weights),
        [whole] * 3 + [real(FAR + 1, levels, LANES)] * 2 + [real(*extended)] * 4 + [real(1, LANES)],
        [extended] * 6,
    )
    from_a, from_b = swap(to_a, "lon_even"), swap(to_b, "lon_odd")
    k2, k3, k4, sums = call(
        functools.partial(second_kernel, own, levels, columns),
        (flags, k0, k1, k1_strip, from_a, from_b, *coefficients, above, below, shift),
        [whole] * 3 + [rows],
        [extended] * 4,
    )
    sums = everywhere(sums)
    out, rest = call(final_kernel, (sums, shift, x, c, k0, k1, k2, k3, k4), [whole] * 2, flagged=False)
    return out.reshape(right_side.shape), rest.reshape(right_side.shape)


def solution(mesh):
    spec = P(None, "lon", "lat")
    return jax.shard_map(
        body, mesh=mesh, in_specs=(spec, spec, spec, spec, P()), out_specs=(spec, spec), check_vma=False
    )
```

time: 107 us -> 56.2 us (0.53)
  between operations: 28.1 us -> 0.74 us
  starting transfers between devices: 30.1 us -> 13.1 us
  other arithmetic: 14 us -> 0.89 us
  blocking collectives: 10.8 us -> 19.2 us
  Pallas kernels: 0 us -> 6.65 us
  waiting for transfers between devices: 18.3 us -> 12.5 us
  local copies, waits for them, and re-layouts: 4.6 us -> 2.89 us
    ppermute x20 -> x8, starting transfers between devices: 25.8 us -> 13.1 us  [swap(): return lax.ppermute(value, AXES, pairs[name])]
    all_to_all x1 -> x2, blocking collectives: 10.8 us -> 19.2 us  [everywhere(): return lax.all_to_all(rows, AXES, 0, 0, tiled=True)]
    select_n x22 -> x0, other arithmetic: 8.2 us -> none  [the longest x1 5.55 us: body(): jnp.where(lanes == k, jnp.sum(vectors[k // 2] * vectors[k - k // 2]), row)]
    pallas_call x0 -> x5, Pallas kernels: none -> 6.65 us  [call(): pl.pallas_call(kernel, out_shape=tuple(outs) if len(outs) > 1 else outs[0...]
    all_to_all x1 -> x0, starting transfers between devices: 4.36 us -> none  [everywhere(): return jnp.sum(lax.all_to_all(spread, AXES, 0, 0, tiled=True), axis=0)]
    ppermute x20 -> x8, waiting for transfers between devices: 16.4 us -> 12.5 us  [swap(): return lax.ppermute(value, AXES, pairs[name])]
    reduce_sum x4 -> x0, other arithmetic: 2.51 us -> none  [the longest x1 1.31 us: body(): jnp.sum(vectors[k // 2] * vectors[k - k // 2])]
    slice x17 -> x0, local copies, waits for them, and re-layouts: 2.44 us -> none  [the longest x5 0.69 us: stencil(): q[:, :, 1:]]
  transfers between devices with their start and end apart: 21 -> 8, of which waited for: 9 -> 3; matrix products, arithmetic and copies ran while one was open for 3% -> 0% of each run, Pallas kernels for 0% -> 1%
where the time goes in v2:
time: 56.2 us; the launch traced here: 56 us
  blocking collectives  19.2 us (34%)
  starting transfers between devices  13.1 us (23%)
  waiting for transfers between devices  12.5 us (22%)
  Pallas kernels  6.65 us (12%)
  local copies, waits for them, and re-layouts  2.89 us (5%)
  other arithmetic  0.89 us (2%)
  between operations  0.74 us (1%)
    all_to_all x2, blocking collectives, everywhere(): return lax.all_to_all(rows, AXES, 0, 0, tiled=True)  19.2 us
    ppermute x8, starting transfers between devices, swap(): return lax.ppermute(value, AXES, pairs[name])  13.1 us
    ppermute x8, waiting for transfers between devices, swap(): return lax.ppermute(value, AXES, pairs[name])  12.5 us
    pallas_call x5, Pallas kernels, call(): pl.pallas_call(kernel, out_shape=tuple(outs) if len(outs) > 1 else outs[0...  6.65 us
    unnamed x10, local copies, waits for them, and re-layouts  2.74 us
  transfers between devices with their start and end apart: 8, of which 3 were waited for; matrix products, arithmetic and copies ran while one was open for 0% of the time, Pallas kernels for 1%

profile of v2, /device:TPU:0, one launch (start us, length us, event | category | flops | bytes accessed | tf_op | source)
XLA Modules:
  0.0 56.0 jit_solution(3372160746568113585)
XLA Ops:
  0.7 0.8 %pad_maximum_fusion.2 = (f32[70]{0:T(128)S(1)}, f32[70]{0:T(128)S(1)}) fusion(f32[1]{0:T(128)} %constant.31.clone.1, f32[69]{0:T(128)} %param.9), kind=kLoop, calls=%fused_computation.3 | loop fusion | flops 140 | bytes 840 | tf_op jit(solution)/shard_map/concatenate | solution.py:382
  1.5 0.1 pad_add_fusion.flags
  1.5 0.1 broadcast_in_dim.5.below
  1.6 0.1 broadcast_in_dim.4.above
  1.7 0.0 copy-start.1
  1.7 0.9 %copy-done.1 = f32[70,4,128]{2,1,0:T(4,128)S(1)} copy-done((f32[70,4,128]{2,1,0:T(4,128)S(1)}, f32[70,4,128]{2,1,0:T(4,128)}, u32[]{:S(2)}) %copy-start.1) | copy-done | bytes 143384
  2.6 0.9 %copy-done.3 = f32[70,4,128]{2,1,0:T(4,128)S(1)} copy-done((f32[70,4,128]{2,1,0:T(4,128)S(1)}, f32[70,4,128]{2,1,0:T(4,128)}, u32[]{:S(2)}) %copy-start.3) | copy-done | bytes 143384
  3.5 0.9 %copy-done.4 = f32[70,4,128]{2,1,0:T(4,128)S(1)} copy-done((f32[70,4,128]{2,1,0:T(4,128)S(1)}, f32[70,4,128]{2,1,0:T(4,128)}, u32[]{:S(2)}) %copy-start.4) | copy-done | bytes 143384
  4.4 1.2 %shard_map.68 = (f32[7,70,128]{2,1,0:T(8,128)S(1)}, f32[7,70,128]{2,1,0:T(8,128)S(1)}, f32[70,128]{1,0:T(8,128)S(1)}, f32[70,128]{1,0:T(8,128)S(1)}, f32[280,128...) custom-call(s32[3]{0:T(128)S(1)} %pad_add_fusion.flags, ...), custom_call_target="tpu_custom_call" | custom-call | tf_op jit(solution)/shard_map/pallas_call | solution.py:390
  5.6 0.0 copy-start.2
  5.6 3.0 %collective-permute-start = (f32[7,70,128]{2,1,0:T(8,128)S(1)}, f32[7,70,128]{2,1,0:T(8,128)S(1)}, u32[]{:S(2)}, u32[]{:S(2)}) collective-permute-start(f32[7,70,128]{2,1,0:T(8,128)S(1)} %get-tuple-element.30), channel_id=1, source_target_pairs={{0,4},{1,5},{2,6},{3,7},{4,0},{5,1},{6,2},{7,3},{8,12},{9,13},{10,... | collective-permute-start | bytes 752648 | tf_op jit(solution)/shard_map/ppermute | solution.py:400
  8.7 3.6 %collective-permute-start.1 = (f32[7,70,128]{2,1,0:T(8,128)S(1)}, f32[7,70,128]{2,1,0:T(8,128)S(1)}, u32[]{:S(2)}, u32[]{:S(2)}) collective-permute-start(f32[7,70,128]{2,1,0:T(8,128)S(1)} %get-tuple-element.31), channel_id=1, source_target_pairs={{0,28},{1,29},{2,30},{3,31},{4,8},{5,9},{6,10},{7,11},{8,4},{9,5},... | collective-permute-start | bytes 752648 | tf_op jit(solution)/shard_map/ppermute | solution.py:400
  12.2 0.0 collective-permute-start.2
  12.2 0.0 collective-permute-start.3
  12.2 1.2 %collective-permute-done.2.lat_a = f32[70,128]{1,0:T(8,128)S(1)} collective-permute-done((f32[70,128]{1,0:T(8,128)S(1)}, f32[70,128]{1,0:T(8,128)S(1)}, u32[]{:S(2)}, u32[]{:S(2)}) %collective-permute-start.2) | collective-permute-done | bytes 35872 | tf_op jit(solution)/shard_map/ppermute | solution.py:400
  13.4 4.5 %collective-permute-done.3.lat_b = f32[70,128]{1,0:T(8,128)S(1)} collective-permute-done((f32[70,128]{1,0:T(8,128)S(1)}, f32[70,128]{1,0:T(8,128)S(1)}, u32[]{:S(2)}, u32[]{:S(2)}) %collective-permute-start.3) | collective-permute-done | bytes 35872 | tf_op jit(solution)/shard_map/ppermute | solution.py:400
  18.0 4.4 %collective-permute-start.5 = (f32[2,70,128]{2,1,0:T(8,128)S(1)}, f32[2,70,128]{2,1,0:T(8,128)S(1)}, u32[]{:S(2)}, u32[]{:S(2)}) collective-permute-start(f32[2,70,128]{2,1,0:T(8,128)S(1)} %pad_maximum_fusion), channel_id=1, source_target_pairs={{0,28},{1,29},{2,30},{3,31},{4,8},{5,9},{6,10},{7,11},{8,4},{9,5},... | collective-permute-start | bytes 215048 | tf_op jit(solution)/shard_map/ppermute | solution.py:400
  22.4 0.0 collective-permute-start.4
  22.4 0.3 shard_map.69
  22.7 10.3 %all_to_all.10.sums = f32[32,1,128]{2,1,0:T(1,128)S(1)} all-to-all(f32[32,1,128]{2,1,0:T(1,128)S(1)} %shard_map.69), channel_id=1, replica_groups=mesh['lon'=8,'lat'=4] {'lon','lat'}, dimensions={0} | all-to-all | bytes 32768 | tf_op jit(solution)/shard_map/all_to_all | solution.py:403
  33.0 0.0 collective-permute-done.5.strips_b
  33.0 0.0 collective-permute-done.4.strips_a
  33.0 0.0 collective-permute-done.from_a
  33.1 0.0 collective-permute-done.1.from_b
  33.1 2.2 %shard_map.70 = (f32[280,128]{1,0:T(8,128)S(1)}, f32[280,128]{1,0:T(8,128)S(1)}, f32[280,128]{1,0:T(8,128)S(1)}, f32[4,70,128]{2,1,0:T(8,128)S(1)}, f32[4,70,128...) custom-call(s32[3]{0:T(128)S(1)} %pad_add_fusion.flags, ...), custom_call_target="tpu_custom_call" | custom-call | tf_op jit(solution)/shard_map/pallas_call | solution.py:390
  35.3 0.6 %collective-permute-start.6 = (f32[4,70,128]{2,1,0:T(8,128)S(1)}, f32[4,70,128]{2,1,0:T(8,128)S(1)}, u32[]{:S(2)}, u32[]{:S(2)}) collective-permute-start(f32[4,70,128]{2,1,0:T(8,128)S(1)} %get-tuple-element.37), channel_id=1, source_target_pairs={{0,4},{1,5},{2,6},{3,7},{4,0},{5,1},{6,2},{7,3},{8,12},{9,13},{10,... | collective-permute-start | bytes 430088 | tf_op jit(solution)/shard_map/ppermute | solution.py:400
  35.9 1.5 %collective-permute-start.7 = (f32[4,70,128]{2,1,0:T(8,128)S(1)}, f32[4,70,128]{2,1,0:T(8,128)S(1)}, u32[]{:S(2)}, u32[]{:S(2)}) collective-permute-start(f32[4,70,128]{2,1,0:T(8,128)S(1)} %get-tuple-element.38), channel_id=1, source_target_pairs={{0,28},{1,29},{2,30},{3,31},{4,8},{5,9},{6,10},{7,11},{8,4},{9,5},... | collective-permute-start | bytes 430088 | tf_op jit(solution)/shard_map/ppermute | solution.py:400
  37.4 6.8 %collective-permute-done.6.from_a = f32[4,70,128]{2,1,0:T(8,128)S(1)} collective-permute-done((f32[4,70,128]{2,1,0:T(8,128)S(1)}, f32[4,70,128]{2,1,0:T(8,128)S(1)}, u32[]{:S(2)}, u32[]{:S(2)}) %collective-permute-start.6) | collective-permute-done | bytes 143392 | tf_op jit(solution)/shard_map/ppermute | solution.py:400
  44.1 0.0 collective-permute-done.7.from_b
  44.1 2.0 %shard_map.71 = (f32[280,128]{1,0:T(8,128)S(1)}, f32[280,128]{1,0:T(8,128)S(1)}, f32[280,128]{1,0:T(8,128)S(1)}, f32[32,1,128]{2,1,0:T(1,128)S(1)}) custom-call(s32[3]{0:T(128)S(1)} %pad_add_fusion.flags, f32[280,128]{1,0:T(8,128)S(1)} %get-tuple-element.34.k0, f32[280,128]{1,0:T(8,128)S(1)} %get-tuple-element.35.k1, ...), custom_call_target="tpu_custom_call" | custom-call | tf_op jit(solution)/shard_map/pallas_call | solution.py:390
  46.1 8.9 %all_to_all.11.sums = f32[32,1,128]{2,1,0:T(1,128)S(1)} all-to-all(f32[32,1,128]{2,1,0:T(1,128)S(1)} %get-tuple-element.44), channel_id=1, replica_groups=mesh['lon'=8,'lat'=4] {'lon','lat'}, dimensions={0} | all-to-all | bytes 32768 | tf_op jit(solution)/shard_map/all_to_all | solution.py:403
  55.0 1.0 %shard_map.72 = (f32[280,128]{1,0:T(8,128)}, f32[280,128]{1,0:T(8,128)}) custom-call(f32[32,1,128]{2,1,0:T(1,128)S(1)} %all_to_all.11.sums, f32[1,128]{1,0:T(1,128)S(1)} %get-tuple-element.43.shift_row, f32[280,128]{1,0:T(8,128)S(1)} %bitcast.13, f32[280,128]{1,0:T(8,128)S(1)} %bitcast.16, f32[280,128]{1,0:T(8,128)S(1)} %get-tuple-element.34.k0, ...), custom_call_target="tpu_custom_call" | custom-call | tf_op jit(solution)/shard_map/pallas_call | solution.py:390
  (6 shorter events, 0.0 us)
Async XLA Ops:
  0.6 1.1 %copy-start = (f32[70,4,128]{2,1,0:T(4,128)S(1)}, f32[70,4,128]{2,1,0:T(4,128)}, u32[]{:S(2)}) copy-start(f32[70,4,128]{2,1,0:T(4,128)} %param.6) | copy-start | bytes 430084
  1.7 0.9 %copy-start.1 = (f32[70,4,128]{2,1,0:T(4,128)S(1)}, f32[70,4,128]{2,1,0:T(4,128)}, u32[]{:S(2)}) copy-start(f32[70,4,128]{2,1,0:T(4,128)} %param.7) | copy-start | bytes 430084
  2.6 0.9 %copy-start.3 = (f32[70,4,128]{2,1,0:T(4,128)S(1)}, f32[70,4,128]{2,1,0:T(4,128)}, u32[]{:S(2)}) copy-start(f32[70,4,128]{2,1,0:T(4,128)} %param.5) | copy-start | bytes 430084
  3.5 0.9 %copy-start.4 = (f32[70,4,128]{2,1,0:T(4,128)S(1)}, f32[70,4,128]{2,1,0:T(4,128)}, u32[]{:S(2)}) copy-start(f32[70,4,128]{2,1,0:T(4,128)} %param.8) | copy-start | bytes 430084
  5.6 16.8 %copy-start.2 = (f32[70,4,128]{2,1,0:T(4,128)S(1)}, f32[70,4,128]{2,1,0:T(4,128)}, u32[]{:S(2)}) copy-start(f32[70,4,128]{2,1,0:T(4,128)} %param.7) | copy-start | bytes 430084
  5.6 27.4 %collective-permute-start = (f32[7,70,128]{2,1,0:T(8,128)S(1)}, f32[7,70,128]{2,1,0:T(8,128)S(1)}, u32[]{:S(2)}, u32[]{:S(2)}) collective-permute-start(f32[7,70,128]{2,1,0:T(8,128)S(1)} %get-tuple-element.30), channel_id=1, source_target_pairs={{0,4},{1,5},{2,6},{3,7},{4,0},{5,1},{6,2},{7,3},{8,12},{9,13},{10,... | collective-permute-start | bytes 752648 | tf_op jit(solution)/shard_map/ppermute | solution.py:400
  8.7 24.4 %collective-permute-start.1 = (f32[7,70,128]{2,1,0:T(8,128)S(1)}, f32[7,70,128]{2,1,0:T(8,128)S(1)}, u32[]{:S(2)}, u32[]{:S(2)}) collective-permute-start(f32[7,70,128]{2,1,0:T(8,128)S(1)} %get-tuple-element.31), channel_id=1, source_target_pairs={{0,28},{1,29},{2,30},{3,31},{4,8},{5,9},{6,10},{7,11},{8,4},{9,5},... | collective-permute-start | bytes 752648 | tf_op jit(solution)/shard_map/ppermute | solution.py:400
  12.2 1.2 %collective-permute-start.2 = (f32[70,128]{1,0:T(8,128)S(1)}, f32[70,128]{1,0:T(8,128)S(1)}, u32[]{:S(2)}, u32[]{:S(2)}) collective-permute-start(f32[70,128]{1,0:T(8,128)S(1)} %get-tuple-element.32), channel_id=1, source_target_pairs={{0,1},{1,0},{2,3},{3,2},{4,5},{5,4},{6,7},{7,6},{8,9},{9,8},{10,11... | collective-permute-start | bytes 107528 | tf_op jit(solution)/shard_map/ppermute | solution.py:400
  12.2 5.7 %collective-permute-start.3 = (f32[70,128]{1,0:T(8,128)S(1)}, f32[70,128]{1,0:T(8,128)S(1)}, u32[]{:S(2)}, u32[]{:S(2)}) collective-permute-start(f32[70,128]{1,0:T(8,128)S(1)} %get-tuple-element.33), channel_id=1, source_target_pairs={{0,16},{1,2},{2,1},{3,19},{4,20},{5,6},{6,5},{7,23},{8,24},{9,10},... | collective-permute-start | bytes 107528 | tf_op jit(solution)/shard_map/ppermute | solution.py:400
  18.0 15.1 %collective-permute-start.5 = (f32[2,70,128]{2,1,0:T(8,128)S(1)}, f32[2,70,128]{2,1,0:T(8,128)S(1)}, u32[]{:S(2)}, u32[]{:S(2)}) collective-permute-start(f32[2,70,128]{2,1,0:T(8,128)S(1)} %pad_maximum_fusion), channel_id=1, source_target_pairs={{0,28},{1,29},{2,30},{3,31},{4,8},{5,9},{6,10},{7,11},{8,4},{9,5},... | collective-permute-start | bytes 215048 | tf_op jit(solution)/shard_map/ppermute | solution.py:400
  22.4 10.6 %collective-permute-start.4 = (f32[2,70,128]{2,1,0:T(8,128)S(1)}, f32[2,70,128]{2,1,0:T(8,128)S(1)}, u32[]{:S(2)}, u32[]{:S(2)}) collective-permute-start(f32[2,70,128]{2,1,0:T(8,128)S(1)} %pad_maximum_fusion), channel_id=1, source_target_pairs={{0,4},{1,5},{2,6},{3,7},{4,0},{5,1},{6,2},{7,3},{8,12},{9,13},{10,... | collective-permute-start | bytes 215048 | tf_op jit(solution)/shard_map/ppermute | solution.py:400
  35.3 8.8 %collective-permute-start.6 = (f32[4,70,128]{2,1,0:T(8,128)S(1)}, f32[4,70,128]{2,1,0:T(8,128)S(1)}, u32[]{:S(2)}, u32[]{:S(2)}) collective-permute-start(f32[4,70,128]{2,1,0:T(8,128)S(1)} %get-tuple-element.37), channel_id=1, source_target_pairs={{0,4},{1,5},{2,6},{3,7},{4,0},{5,1},{6,2},{7,3},{8,12},{9,13},{10,... | collective-permute-start | bytes 430088 | tf_op jit(solution)/shard_map/ppermute | solution.py:400
  35.9 8.2 %collective-permute-start.7 = (f32[4,70,128]{2,1,0:T(8,128)S(1)}, f32[4,70,128]{2,1,0:T(8,128)S(1)}, u32[]{:S(2)}, u32[]{:S(2)}) collective-permute-start(f32[4,70,128]{2,1,0:T(8,128)S(1)} %get-tuple-element.38), channel_id=1, source_target_pairs={{0,28},{1,29},{2,30},{3,31},{4,8},{5,9},{6,10},{7,11},{8,4},{9,5},... | collective-permute-start | bytes 430088 | tf_op jit(solution)/shard_map/ppermute | solution.py:400

commit v3 on v2

--- a/solution.py
+++ b/solution.py
@@ -7,13 +7,13 @@
 from jax.experimental.pallas import tpu as pltpu
 from jax.sharding import PartitionSpec as P
 
+
 AXES = ("lon", "lat")
 ITERS = 2
 LANES = 128
 NEAR, FAR = 2, 3
 GROUP = 8
 VMEM = pl.BlockSpec(memory_space=pltpu.VMEM)
-SMEM = pl.BlockSpec(memory_space=pltpu.SMEM)
 FIRST = (("q", 1), ("q", 2), ("g", 1), ("g", 2), ("d", 1), ("d", 2), ("s", 1))
 FIELDS = ("q", "g", "d", "s")
 
@@ -132,14 +132,65 @@
     return {"q": c * x, "g": c * c, "d": (4.0 + h) + (above + below), "s": c * b}
 
 
-def pack_kernel(own, levels, flags, x, b, c, h, above, below, to_a, to_b, lat_a, lat_b, *fields):
+def parity(size):
+    i, j = lax.axis_index("lon"), lax.axis_index("lat")
+    pole = (j == 0) | (j == size - 1)
+    return 1 - lax.rem(i, 2), 1 - lax.rem(j, 2), pole
+
+
+def shift_sums(own, levels, fq, fg, fd, fs, above, below, out, q_ref):
+    lane = lanes_of(levels)
+    clear_ends(q_ref, own, levels)
+    q_ref[own : own * (levels + 1), :] = fq[...]
+    weighted = jnp.zeros((levels, LANES), jnp.float32)
+    total = weighted
+    for i in range(own):
+        q = plane(q_ref, i, own, levels)[...]
+        scale = column(fg, i, own, levels)
+        diagonal = column(fd, i, own, levels)
+        near = jnp.where(lane == LANES - 1, 0.0, turn(q, -1)) + jnp.where(lane == 0, 0.0, turn(q, 1))
+        if i > 0:
+            near = near + plane(q_ref, i - 1, own, levels)[...]
+        if i < own - 1:
+            near = near + plane(q_ref, i + 1, own, levels)[...]
+        near = near + below[...] * plane(q_ref, i, own, levels, 1)[...]
+        near = near + above[...] * plane(q_ref, i, own, levels, -1)[...]
+        rough = column(fs, i, own, levels) - scale * (diagonal * q - near)
+        square = rough * rough
+        total = total + square / scale
+        weighted = weighted + square * diagonal
+    row_lane = lax.broadcasted_iota(jnp.int32, (1, LANES), 1)
+    row = jnp.where(
+        row_lane == 0,
+        jnp.sum(weighted, keepdims=True),
+        jnp.where(row_lane == 1, jnp.sum(total, keepdims=True), 0.0),
+    )
+    out[...] = jnp.broadcast_to(row[None], out.shape)
+
+
+def pack_kernel(own, levels, n_lat, x_hbm, b_hbm, c_hbm, h_hbm, coupling_hbm, to_a, to_b, lat_a, lat_b, above,
+                below, fq, fg, fd, fs, weights, x, b, c, h, coupling, q_ref, sem):
+    copies = []
+    moves = ((coupling_hbm, coupling), (x_hbm, x), (c_hbm, c), (h_hbm, h), (b_hbm, b))
+    for k, (source, target) in enumerate(moves):
+        copies.append(pltpu.make_async_copy(source, target, sem.at[k]))
+        copies[-1].start()
     lane = lanes_of(levels)
     group = lane // GROUP
     groups = LANES // GROUP
-    lon_even, lat_even, pole = flags[0], flags[1], flags[2]
-    store = dict(zip(FIELDS, fields))
+    lon_even, lat_even, pole = parity(n_lat)
+    store = dict(zip(FIELDS, (fq, fg, fd, fs)))
+    copies[0].wait()
+    wide = (levels, levels - 1)
+    row, interface = (lax.broadcasted_iota(jnp.int32, wide, k) for k in (0, 1))
+    strength = jnp.broadcast_to(coupling[...], wide)
+    for out, k in ((below, row), (above, row - 1)):
+        value = jnp.sum(jnp.where(interface == k, strength, 0.0), axis=1, keepdims=True)
+        out[...] = jnp.broadcast_to(value, (levels, LANES))
     north = jnp.zeros((levels, LANES), jnp.float32)
     south = north
+    for copy in copies[1:]:
+        copy.wait()
     for i in range(own):
         values = transformed(
             column(x, i, own, levels),
@@ -155,13 +206,8 @@
             rolled = turn(values[name], GROUP * slot)
             north = jnp.where(group == slot, rolled, north)
             south = jnp.where(group == (slot - 1) % groups, rolled, south)
-    for k, (name, distance) in enumerate(FIRST):
-        east, west = own - distance, distance - 1
-        a = jnp.where(lon_even == 1, east, west)
-        to_a[k] = store[name][pl.ds(a, levels, stride=own), :]
-        to_b[k] = store[name][pl.ds(east + west - a, levels, stride=own), :]
     even = jnp.full((levels, LANES), lat_even, jnp.int32) == 1
-    over = jnp.full((levels, LANES), pole, jnp.int32) == 1
+    over = jnp.full((levels, LANES), pole.astype(jnp.int32), jnp.int32) == 1
     lat_a[...] = jnp.where(even, south, north)
     other = jnp.where(even, north, south)
     mirror = other
@@ -169,37 +215,26 @@
         mirror = jnp.where((lane & bit) != 0, turn(mirror, bit), turn(mirror, -bit))
     mirror = jnp.where(even, turn(mirror, -GROUP), turn(mirror, GROUP))
     lat_b[...] = jnp.where(over, mirror, other)
-
-
-def shift_kernel(own, levels, x, b, c, h, above, below, out, q_ref):
+    for k, (name, distance) in enumerate(FIRST):
+        east, west = own - distance, distance - 1
+        a = jnp.where(lon_even == 1, east, west)
+        to_a[k] = store[name][pl.ds(a, levels, stride=own), :]
+        to_b[k] = store[name][pl.ds(east + west - a, levels, stride=own), :]
+    shift_sums(own, levels, fq, fg, fd, fs, above, below, weights, q_ref)
+
+
+def corner_kernel(own, levels, n_lat, lat_a, lat_b, to_a, to_b):
     lane = lanes_of(levels)
-    clear_ends(q_ref, own, levels)
-    for i in range(own):
-        plane(q_ref, i, own, levels)[...] = column(c, i, own, levels) * column(x, i, own, levels)
-    weighted = jnp.zeros((levels, LANES), jnp.float32)
-    total = weighted
-    for i in range(own):
-        q = plane(q_ref, i, own, levels)[...]
-        scale = column(c, i, own, levels)
-        diagonal = (4.0 + column(h, i, own, levels)) + (above[...] + below[...])
-        near = jnp.where(lane == LANES - 1, 0.0, turn(q, -1)) + jnp.where(lane == 0, 0.0, turn(q, 1))
-        if i > 0:
-            near = near + plane(q_ref, i - 1, own, levels)[...]
-        if i < own - 1:
-            near = near + plane(q_ref, i + 1, own, levels)[...]
-        near = near + below[...] * plane(q_ref, i, own, levels, 1)[...]
-        near = near + above[...] * plane(q_ref, i, own, levels, -1)[...]
-        rough = column(b, i, own, levels) - scale * (diagonal * q - near)
-        weight = rough * rough
-        total = total + weight
-        weighted = weighted + weight * (scale * scale * diagonal)
-    row_lane = lax.broadcasted_iota(jnp.int32, (1, LANES), 1)
-    row = jnp.where(
-        row_lane == 0,
-        jnp.sum(weighted, keepdims=True),
-        jnp.where(row_lane == 1, jnp.sum(total, keepdims=True), 0.0),
-    )
-    out[...] = jnp.broadcast_to(row[None], out.shape)
+    quarter = (lane // GROUP) % own
+    lon_even, lat_even, _ = parity(n_lat)
+    even = jnp.full((levels, LANES), lat_even, jnp.int32) == 1
+    lon = jnp.full((levels, LANES), lon_even, jnp.int32) == 1
+    a, b = lat_a[...], lat_b[...]
+    north, south = jnp.where(even, b, a), jnp.where(even, a, b)
+    east = jnp.where(quarter >= own - NEAR, south, turn(north, GROUP * (1 - NEAR)))
+    west = jnp.where(quarter < NEAR, south, turn(north, GROUP * (1 + NEAR)))
+    to_a[...] = jnp.where(lon, east, west)
+    to_b[...] = jnp.where(lon, west, east)
 
 
 def lane_value(row, k):
@@ -234,12 +269,12 @@
         return out
 
 
-def first_kernel(own, levels, columns, flags, fq, fg, fd, fs, above, below, from_a, from_b, lat_a, lat_b,
-                 strips_a, strips_b, sums, k0, k1, k1_strip, to_a, to_b, g_main, g_strip, d_main, d_strip,
+def first_kernel(own, levels, columns, n_lat, fq, fg, fd, fs, above, below, from_a, from_b, lat_a, lat_b,
+                 corners_a, corners_b, sums, k0, k1, k1_strip, to_a, to_b, g_main, g_strip, d_main, d_strip,
                  shift_out, qa_main, qa_strip, qb_main, qb_strip, s_main, s_strip):
     lane = lanes_of(levels)
     low = lane < LANES // 2
-    lon_even, lat_even = flags[0], flags[1]
+    lon_even, lat_even, _ = parity(n_lat)
     even = jnp.full((levels, LANES), lat_even, jnp.int32) == 1
     qa, qb = (qa_main, qa_strip), (qb_main, qb_strip)
     where_to = {"q": qa, "g": (g_main, g_strip), "d": (d_main, d_strip), "s": (s_main, s_strip)}
@@ -254,30 +289,25 @@
     shift = jnp.broadcast_to(shift, (levels, LANES))
 
     def unpack(north, south, name, i):
-        slot = FIELDS.index(name) * own + i
-        back = -GROUP * slot
+        back = -GROUP * (FIELDS.index(name) * own + i)
         return jnp.where(low, turn(south, back), turn(north, back))
 
-    def halves(a, b):
-        return jnp.where(even, b, a), jnp.where(even, a, b)
-
     fields = dict(zip(FIELDS, (fq, fg, fd, fs)))
-    north, south = halves(lat_a[...], lat_b[...])
+    a, b = lat_a[...], lat_b[...]
+    north, south = jnp.where(even, b, a), jnp.where(even, a, b)
     for name in FIELDS:
         for i in range(own):
             ext.put(where_to[name], 0, FAR + i, column(fields[name], i, own, levels))
             ext.put(where_to[name], 1, FAR + i, unpack(north, south, name, i))
-    for block, tiles, east in ((from_a, strips_a, lon_even), (from_b, strips_b, 1 - lon_even)):
-        north, south = halves(tiles[0], tiles[1])
+    for block, corner, east in ((from_a, corners_a, lon_even), (from_b, corners_b, 1 - lon_even)):
         is_east = jnp.full((levels, LANES), east, jnp.int32) == 1
+        tile = corner[...]
+        north = jnp.where(is_east, turn(tile, -GROUP * (1 + NEAR)), turn(tile, -GROUP * (1 - NEAR)))
         for k, (name, distance) in enumerate(FIRST):
-            e_east, e_west = FAR + own - 1 + distance, FAR - distance
-            e = jnp.where(east == 1, e_east, e_west)
+            e = jnp.where(east == 1, FAR + own - 1 + distance, FAR - distance)
             ext.put(where_to[name], 0, e, block[k])
             strip = jnp.where(
-                is_east,
-                unpack(north, south, name, distance - 1),
-                unpack(north, south, name, own - distance),
+                is_east, unpack(north, tile, name, distance - 1), unpack(north, tile, name, own - distance)
             )
             ext.put(where_to[name], 1, e, strip)
     for e in range(FAR - 1, FAR + own + 1):
@@ -302,10 +332,10 @@
         out[FAR] = packed
 
 
-def second_kernel(own, levels, columns, flags, k0, k1, k1_strip, from_a, from_b, g_main, g_strip, d_main, d_strip,
+def second_kernel(own, levels, columns, n_lat, k0, k1, k1_strip, from_a, from_b, g_main, g_strip, d_main, d_strip,
                   above, below, shift_row, k2, k3, k4, out, qa_main, qa_strip, qb_main, qb_strip):
     lane = lanes_of(levels)
-    lon_even = flags[0]
+    lon_even, _, _ = parity(n_lat)
     qa, qb = (qa_main, qa_strip), (qb_main, qb_strip)
     g = (g_main, g_strip)
     ext = Extended(columns, levels, (d_main, d_strip), g, above, below, lane)
@@ -369,31 +399,27 @@
     rest[...] = combined(residual)
 
 
-def body(right_side, first_guess, cell_scale, helmholtz_term, vertical_coupling):
+def program(right_side, first_guess, cell_scale, helmholtz_term, vertical_coupling):
     n_lon, n_lat = lax.axis_size("lon"), lax.axis_size("lat")
     levels, own, width = right_side.shape
-    assert width == LANES and own >= FAR and len(FIELDS) * own * GROUP <= LANES
+    assert width == LANES and own == 2 * NEAR >= FAR and len(FIELDS) * own * GROUP == LANES
     assert n_lon % 4 == 0 and n_lat % 2 == 0
     columns = own + 2 * FAR
     pairs = swap_pairs(n_lon, n_lat)
-    i, j = lax.axis_index("lon"), lax.axis_index("lat")
-    flags = jnp.stack([1 - i % 2, 1 - j % 2, ((j == 0) | (j == n_lat - 1)).astype(jnp.int32)]).astype(jnp.int32)
-    zero = jnp.zeros((1,), jnp.float32)
-    below = jnp.broadcast_to(jnp.concatenate([vertical_coupling, zero])[:, None], (levels, LANES))
-    above = jnp.broadcast_to(jnp.concatenate([zero, vertical_coupling])[:, None], (levels, LANES))
+    coupling = vertical_coupling.reshape(1, levels - 1)
     b, x, c, h = (v.reshape(levels * own, LANES) for v in (right_side, first_guess, cell_scale, helmholtz_term))
 
     def real(*shape):
         return jax.ShapeDtypeStruct(shape, jnp.float32)
 
-    def call(kernel, ins, outs, scratch=(), flagged=True):
+    def call(kernel, ins, outs, scratch=(), specs=None, grant=32 * 1024 * 1024):
         return pl.pallas_call(
             kernel,
             out_shape=tuple(outs) if len(outs) > 1 else outs[0],
-            in_specs=[SMEM] * flagged + [VMEM] * (len(ins) - flagged),
+            in_specs=specs or [VMEM] * len(ins),
             out_specs=tuple([VMEM] * len(outs)) if len(outs) > 1 else VMEM,
-            scratch_shapes=[pltpu.VMEM(s, jnp.float32) for s in scratch],
-            compiler_params=pltpu.CompilerParams(vmem_limit_bytes=32 * 1024 * 1024),
+            scratch_shapes=[pltpu.VMEM(s, jnp.float32) if isinstance(s, tuple) else s for s in scratch],
+            compiler_params=pltpu.CompilerParams(vmem_limit_bytes=grant),
         )(*ins)
 
     def swap(value, name):
@@ -408,39 +434,40 @@
     padded = ((levels + 2) * own, LANES)
     extended = ((levels + 2) * columns, LANES)
 
-    to_a, to_b, lat_a, lat_b, *fields = call(
-        functools.partial(pack_kernel, own, levels),
-        (flags, x, b, c, h, above, below),
-        [real(len(FIRST), levels, LANES)] * 2 + [tile] * 2 + [whole] * len(FIELDS),
-    )
+    to_a, to_b, lat_a, lat_b, above, below, *fields, weights = call(
+        functools.partial(pack_kernel, own, levels, n_lat),
+        tuple(pltpu.with_memory_space_constraint(v, pltpu.HBM) for v in (x, b, c, h, coupling)),
+        [real(len(FIRST), levels, LANES)] * 2 + [tile] * 4 + [whole] * len(FIELDS) + [rows],
+        [(levels * own, LANES)] * 4 + [(1, levels - 1), padded, pltpu.SemaphoreType.DMA((5,))],
+        [pl.BlockSpec(memory_space=pltpu.HBM)] * 5,
+    )
+    lat_a, lat_b = swap(lat_a, "lat_even"), swap(lat_b, "lat_odd")
     from_a, from_b = swap(to_a, "lon_even"), swap(to_b, "lon_odd")
-    lat_a, lat_b = swap(lat_a, "lat_even"), swap(lat_b, "lat_odd")
-    strips = jnp.stack([lat_a, lat_b])
-    strips_a, strips_b = swap(strips, "lon_even"), swap(strips, "lon_odd")
-    weights = call(
-        functools.partial(shift_kernel, own, levels), (x, b, c, h, above, below), [rows], [padded], flagged=False
-    )
+    corners_a, corners_b = call(
+        functools.partial(corner_kernel, own, levels, n_lat), (lat_a, lat_b), [tile] * 2
+    )
+    corners_a, corners_b = swap(corners_a, "lon_even"), swap(corners_b, "lon_odd")
     weights = everywhere(weights)
     k0, k1, k1_strip, to_a, to_b, *coefficients, shift = call(
-        functools.partial(first_kernel, own, levels, columns),
-        (flags, *fields, above, below, from_a, from_b, lat_a, lat_b, strips_a, strips_b, weights),
+        functools.partial(first_kernel, own, levels, columns, n_lat),
+        (*fields, above, below, from_a, from_b, lat_a, lat_b, corners_a, corners_b, weights),
         [whole] * 3 + [real(FAR + 1, levels, LANES)] * 2 + [real(*extended)] * 4 + [real(1, LANES)],
         [extended] * 6,
     )
     from_a, from_b = swap(to_a, "lon_even"), swap(to_b, "lon_odd")
     k2, k3, k4, sums = call(
-        functools.partial(second_kernel, own, levels, columns),
-        (flags, k0, k1, k1_strip, from_a, from_b, *coefficients, above, below, shift),
+        functools.partial(second_kernel, own, levels, columns, n_lat),
+        (k0, k1, k1_strip, from_a, from_b, *coefficients, above, below, shift),
         [whole] * 3 + [rows],
         [extended] * 4,
     )
     sums = everywhere(sums)
-    out, rest = call(final_kernel, (sums, shift, x, c, k0, k1, k2, k3, k4), [whole] * 2, flagged=False)
+    out, rest = call(final_kernel, (sums, shift, x, c, k0, k1, k2, k3, k4), [whole] * 2)
     return out.reshape(right_side.shape), rest.reshape(right_side.shape)
 
 
 def solution(mesh):
     spec = P(None, "lon", "lat")
     return jax.shard_map(
-        body, mesh=mesh, in_specs=(spec, spec, spec, spec, P()), out_specs=(spec, spec), check_vma=False
-    )
+        program, mesh=mesh, in_specs=(spec, spec, spec, spec, P()), out_specs=(spec, spec), check_vma=False
+    )

time: 56.2 us -> 52.1 us (0.927)
  local copies, waits for them, and re-layouts: 2.89 us -> 0.01 us
  starting transfers between devices: 13.1 us -> 14.9 us
  blocking collectives: 19.2 us -> 17.7 us
  other arithmetic: 0.89 us -> 0 us
    unnamed x10 -> x4, local copies, waits for them, and re-layouts: 2.74 us -> 0.01 us
    ppermute x8, starting transfers between devices: 13.1 us -> 14.9 us  [swap(): return lax.ppermute(value, AXES, pairs[name])]
    all_to_all x2, blocking collectives: 19.2 us -> 17.7 us  [everywhere(): return lax.all_to_all(rows, AXES, 0, 0, tiled=True)]
    concatenate x1 -> x0, other arithmetic: 0.81 us -> none  [body(): jnp.concatenate([vertical_coupling, zero])[:, None]]
  transfers between devices with their start and end apart: 8 -> 8, of which waited for: 3 -> 3; matrix products, arithmetic and copies ran while one was open for 0% -> 0% of each run, Pallas kernels for 1% -> 0%
where the time goes in v3:
time: 52.1 us; the launch traced here: 51.9 us
  blocking collectives  17.7 us (34%)
  starting transfers between devices  14.9 us (29%)
  waiting for transfers between devices  12.4 us (24%)
  Pallas kernels  6.24 us (12%)
  between operations  0.68 us (1%)
    all_to_all x2, blocking collectives, everywhere(): return lax.all_to_all(rows, AXES, 0, 0, tiled=True)  17.7 us
    ppermute x8, starting transfers between devices, swap(): return lax.ppermute(value, AXES, pairs[name])  14.9 us
    ppermute x8, waiting for transfers between devices, swap(): return lax.ppermute(value, AXES, pairs[name])  12.4 us
    pallas_call x5, Pallas kernels, call(): pl.pallas_call(kernel, out_shape=tuple(outs) if len(outs) > 1 else outs[0...  6.24 us
  transfers between devices with their start and end apart: 8, of which 3 were waited for; matrix products, arithmetic and copies ran while one was open for 0% of the time, Pallas kernels for 0%

profile of v3, /device:TPU:0, one launch (start us, length us, event | category | flops | bytes accessed | tf_op | source)
XLA Modules:
  0.0 51.9 jit_solution(8337796548948070552)
XLA Ops:
  0.6 1.9 %shard_map.68 = (f32[7,70,128]{2,1,0:T(8,128)S(1)}, f32[7,70,128]{2,1,0:T(8,128)S(1)}, f32[70,128]{1,0:T(8,128)S(1)}, f32[70,128]{1,0:T(8,128)S(1)}, f32[70,128]...) custom-call(f32[280,128]{1,0:T(8,128)} %bitcast.7, ...), custom_call_target="tpu_custom_call" | custom-call | tf_op jit(solution)/shard_map/pallas_call | solution.py:416
  2.6 3.0 %collective-permute-start = (f32[7,70,128]{2,1,0:T(8,128)S(1)}, f32[7,70,128]{2,1,0:T(8,128)S(1)}, u32[]{:S(2)}, u32[]{:S(2)}) collective-permute-start(f32[7,70,128]{2,1,0:T(8,128)S(1)} %get-tuple-element.37), channel_id=1, source_target_pairs={{0,4},{1,5},{2,6},{3,7},{4,0},{5,1},{6,2},{7,3},{8,12},{9,13},{10,... | collective-permute-start | bytes 752648 | tf_op jit(solution)/shard_map/ppermute | solution.py:426
  5.6 3.6 %collective-permute-start.1 = (f32[7,70,128]{2,1,0:T(8,128)S(1)}, f32[7,70,128]{2,1,0:T(8,128)S(1)}, u32[]{:S(2)}, u32[]{:S(2)}) collective-permute-start(f32[7,70,128]{2,1,0:T(8,128)S(1)} %get-tuple-element.38), channel_id=1, source_target_pairs={{0,28},{1,29},{2,30},{3,31},{4,8},{5,9},{6,10},{7,11},{8,4},{9,5},... | collective-permute-start | bytes 752648 | tf_op jit(solution)/shard_map/ppermute | solution.py:426
  9.2 0.0 collective-permute-start.2
  9.2 0.0 collective-permute-start.3
  9.2 1.2 %collective-permute-done.2.lat_a = f32[70,128]{1,0:T(8,128)S(1)} collective-permute-done((f32[70,128]{1,0:T(8,128)S(1)}, f32[70,128]{1,0:T(8,128)S(1)}, u32[]{:S(2)}, u32[]{:S(2)}) %collective-permute-start.2) | collective-permute-done | bytes 35872 | tf_op jit(solution)/shard_map/ppermute | solution.py:426
  10.4 4.4 %collective-permute-done.3.lat_b = f32[70,128]{1,0:T(8,128)S(1)} collective-permute-done((f32[70,128]{1,0:T(8,128)S(1)}, f32[70,128]{1,0:T(8,128)S(1)}, u32[]{:S(2)}, u32[]{:S(2)}) %collective-permute-start.3) | collective-permute-done | bytes 35872 | tf_op jit(solution)/shard_map/ppermute | solution.py:426
  14.8 0.1 shard_map.69
  14.9 2.6 %collective-permute-start.4 = (f32[70,128]{1,0:T(8,128)S(1)}, f32[70,128]{1,0:T(8,128)S(1)}, u32[]{:S(2)}, u32[]{:S(2)}) collective-permute-start(f32[70,128]{1,0:T(8,128)S(1)} %get-tuple-element.41), channel_id=1, source_target_pairs={{0,4},{1,5},{2,6},{3,7},{4,0},{5,1},{6,2},{7,3},{8,12},{9,13},{10,... | collective-permute-start | bytes 107528 | tf_op jit(solution)/shard_map/ppermute | solution.py:426
  17.5 3.6 %collective-permute-start.5 = (f32[70,128]{1,0:T(8,128)S(1)}, f32[70,128]{1,0:T(8,128)S(1)}, u32[]{:S(2)}, u32[]{:S(2)}) collective-permute-start(f32[70,128]{1,0:T(8,128)S(1)} %get-tuple-element.42), channel_id=1, source_target_pairs={{0,28},{1,29},{2,30},{3,31},{4,8},{5,9},{6,10},{7,11},{8,4},{9,5},... | collective-permute-start | bytes 107528 | tf_op jit(solution)/shard_map/ppermute | solution.py:426
  21.1 8.9 %all_to_all.10.sums = f32[32,1,128]{2,1,0:T(1,128)S(1)} all-to-all(f32[32,1,128]{2,1,0:T(1,128)S(1)} %get-tuple-element.43), channel_id=1, replica_groups=mesh['lon'=8,'lat'=4] {'lon','lat'}, dimensions={0} | all-to-all | bytes 32768 | tf_op jit(solution)/shard_map/all_to_all | solution.py:429
  29.9 0.0 collective-permute-done.4.corners_a
  29.9 0.0 collective-permute-done.5.corners_b
  29.9 0.0 collective-permute-done.from_a
  29.9 0.0 collective-permute-done.1.from_b
  29.9 1.8 %shard_map.70 = (f32[280,128]{1,0:T(8,128)S(1)}, f32[280,128]{1,0:T(8,128)S(1)}, f32[280,128]{1,0:T(8,128)S(1)}, f32[4,70,128]{2,1,0:T(8,128)S(1)}, f32[4,70,128...) custom-call(f32[280,128]{1,0:T(8,128)S(1)} %get-tuple-element.31.fq,, ...), custom_call_target="tpu_custom_call" | custom-call | tf_op jit(solution)/shard_map/pallas_call | solution.py:416
  31.7 0.6 %collective-permute-start.6 = (f32[4,70,128]{2,1,0:T(8,128)S(1)}, f32[4,70,128]{2,1,0:T(8,128)S(1)}, u32[]{:S(2)}, u32[]{:S(2)}) collective-permute-start(f32[4,70,128]{2,1,0:T(8,128)S(1)} %get-tuple-element.47), channel_id=1, source_target_pairs={{0,4},{1,5},{2,6},{3,7},{4,0},{5,1},{6,2},{7,3},{8,12},{9,13},{10,... | collective-permute-start | bytes 430088 | tf_op jit(solution)/shard_map/ppermute | solution.py:426
  32.4 1.5 %collective-permute-start.7 = (f32[4,70,128]{2,1,0:T(8,128)S(1)}, f32[4,70,128]{2,1,0:T(8,128)S(1)}, u32[]{:S(2)}, u32[]{:S(2)}) collective-permute-start(f32[4,70,128]{2,1,0:T(8,128)S(1)} %get-tuple-element.48), channel_id=1, source_target_pairs={{0,28},{1,29},{2,30},{3,31},{4,8},{5,9},{6,10},{7,11},{8,4},{9,5},... | collective-permute-start | bytes 430088 | tf_op jit(solution)/shard_map/ppermute | solution.py:426
  33.8 6.8 %collective-permute-done.6.from_a = f32[4,70,128]{2,1,0:T(8,128)S(1)} collective-permute-done((f32[4,70,128]{2,1,0:T(8,128)S(1)}, f32[4,70,128]{2,1,0:T(8,128)S(1)}, u32[]{:S(2)}, u32[]{:S(2)}) %collective-permute-start.6) | collective-permute-done | bytes 143392 | tf_op jit(solution)/shard_map/ppermute | solution.py:426
  40.6 0.0 collective-permute-done.7.from_b
  40.6 0.0 copy-start
  40.6 0.0 copy-start.1
  40.6 1.5 %shard_map.71 = (f32[280,128]{1,0:T(8,128)S(1)}, f32[280,128]{1,0:T(8,128)S(1)}, f32[280,128]{1,0:T(8,128)S(1)}, f32[32,1,128]{2,1,0:T(1,128)S(1)}) custom-call(f32[280,128]{1,0:T(8,128)S(1)} %get-tuple-element.44.k0, f32[280,128]{1,0:T(8,128)S(1)} %get-tuple-element.45.k1, f32[280,128]{1,0:T(8,128)S(1)} %get-tuple-element.46.k1_strip, ...), custom_call_target="tpu_custom_call" | custom-call | tf_op jit(solution)/shard_map/pallas_call | solution.py:416
  42.0 8.9 %all_to_all.11.sums = f32[32,1,128]{2,1,0:T(1,128)S(1)} all-to-all(f32[32,1,128]{2,1,0:T(1,128)S(1)} %get-tuple-element.54), channel_id=1, replica_groups=mesh['lon'=8,'lat'=4] {'lon','lat'}, dimensions={0} | all-to-all | bytes 32768 | tf_op jit(solution)/shard_map/all_to_all | solution.py:429
  50.9 0.0 copy-done
  50.9 0.0 copy-done.1
  50.9 1.0 %shard_map.72 = (f32[280,128]{1,0:T(8,128)}, f32[280,128]{1,0:T(8,128)}) custom-call(f32[32,1,128]{2,1,0:T(1,128)S(1)} %all_to_all.11.sums, f32[1,128]{1,0:T(1,128)S(1)} %get-tuple-element.53.shift_row, f32[280,128]{1,0:T(8,128)S(1)} %bitcast.8, f32[280,128]{1,0:T(8,128)S(1)} %bitcast.10, f32[280,128]{1,0:T(8,128)S(1)} %get-tuple-element.44.k0, ...), custom_call_target="tpu_custom_call" | custom-call | tf_op jit(solution)/shard_map/pallas_call | solution.py:416
Async XLA Ops:
  2.6 27.4 %collective-permute-start = (f32[7,70,128]{2,1,0:T(8,128)S(1)}, f32[7,70,128]{2,1,0:T(8,128)S(1)}, u32[]{:S(2)}, u32[]{:S(2)}) collective-permute-start(f32[7,70,128]{2,1,0:T(8,128)S(1)} %get-tuple-element.37), channel_id=1, source_target_pairs={{0,4},{1,5},{2,6},{3,7},{4,0},{5,1},{6,2},{7,3},{8,12},{9,13},{10,... | collective-permute-start | bytes 752648 | tf_op jit(solution)/shard_map/ppermute | solution.py:426
  5.6 24.3 %collective-permute-start.1 = (f32[7,70,128]{2,1,0:T(8,128)S(1)}, f32[7,70,128]{2,1,0:T(8,128)S(1)}, u32[]{:S(2)}, u32[]{:S(2)}) collective-permute-start(f32[7,70,128]{2,1,0:T(8,128)S(1)} %get-tuple-element.38), channel_id=1, source_target_pairs={{0,28},{1,29},{2,30},{3,31},{4,8},{5,9},{6,10},{7,11},{8,4},{9,5},... | collective-permute-start | bytes 752648 | tf_op jit(solution)/shard_map/ppermute | solution.py:426
  9.2 1.2 %collective-permute-start.2 = (f32[70,128]{1,0:T(8,128)S(1)}, f32[70,128]{1,0:T(8,128)S(1)}, u32[]{:S(2)}, u32[]{:S(2)}) collective-permute-start(f32[70,128]{1,0:T(8,128)S(1)} %get-tuple-element.39), channel_id=1, source_target_pairs={{0,1},{1,0},{2,3},{3,2},{4,5},{5,4},{6,7},{7,6},{8,9},{9,8},{10,11... | collective-permute-start | bytes 107528 | tf_op jit(solution)/shard_map/ppermute | solution.py:426
  9.2 5.6 %collective-permute-start.3 = (f32[70,128]{1,0:T(8,128)S(1)}, f32[70,128]{1,0:T(8,128)S(1)}, u32[]{:S(2)}, u32[]{:S(2)}) collective-permute-start(f32[70,128]{1,0:T(8,128)S(1)} %get-tuple-element.40), channel_id=1, source_target_pairs={{0,16},{1,2},{2,1},{3,19},{4,20},{5,6},{6,5},{7,23},{8,24},{9,10},... | collective-permute-start | bytes 107528 | tf_op jit(solution)/shard_map/ppermute | solution.py:426
  14.9 15.0 %collective-permute-start.4 = (f32[70,128]{1,0:T(8,128)S(1)}, f32[70,128]{1,0:T(8,128)S(1)}, u32[]{:S(2)}, u32[]{:S(2)}) collective-permute-start(f32[70,128]{1,0:T(8,128)S(1)} %get-tuple-element.41), channel_id=1, source_target_pairs={{0,4},{1,5},{2,6},{3,7},{4,0},{5,1},{6,2},{7,3},{8,12},{9,13},{10,... | collective-permute-start | bytes 107528 | tf_op jit(solution)/shard_map/ppermute | solution.py:426
  17.5 12.4 %collective-permute-start.5 = (f32[70,128]{1,0:T(8,128)S(1)}, f32[70,128]{1,0:T(8,128)S(1)}, u32[]{:S(2)}, u32[]{:S(2)}) collective-permute-start(f32[70,128]{1,0:T(8,128)S(1)} %get-tuple-element.42), channel_id=1, source_target_pairs={{0,28},{1,29},{2,30},{3,31},{4,8},{5,9},{6,10},{7,11},{8,4},{9,5},... | collective-permute-start | bytes 107528 | tf_op jit(solution)/shard_map/ppermute | solution.py:426
  31.7 8.8 %collective-permute-start.6 = (f32[4,70,128]{2,1,0:T(8,128)S(1)}, f32[4,70,128]{2,1,0:T(8,128)S(1)}, u32[]{:S(2)}, u32[]{:S(2)}) collective-permute-start(f32[4,70,128]{2,1,0:T(8,128)S(1)} %get-tuple-element.47), channel_id=1, source_target_pairs={{0,4},{1,5},{2,6},{3,7},{4,0},{5,1},{6,2},{7,3},{8,12},{9,13},{10,... | collective-permute-start | bytes 430088 | tf_op jit(solution)/shard_map/ppermute | solution.py:426
  32.4 8.2 %collective-permute-start.7 = (f32[4,70,128]{2,1,0:T(8,128)S(1)}, f32[4,70,128]{2,1,0:T(8,128)S(1)}, u32[]{:S(2)}, u32[]{:S(2)}) collective-permute-start(f32[4,70,128]{2,1,0:T(8,128)S(1)} %get-tuple-element.48), channel_id=1, source_target_pairs={{0,28},{1,29},{2,30},{3,31},{4,8},{5,9},{6,10},{7,11},{8,4},{9,5},... | collective-permute-start | bytes 430088 | tf_op jit(solution)/shard_map/ppermute | solution.py:426
  40.6 10.3 %copy-start = (f32[70,4,128]{2,1,0:T(4,128)S(1)}, f32[70,4,128]{2,1,0:T(4,128)}, u32[]{:S(2)}) copy-start(f32[70,4,128]{2,1,0:T(4,128)} %param.6) | copy-start | bytes 430084
  40.6 10.3 %copy-start.1 = (f32[70,4,128]{2,1,0:T(4,128)S(1)}, f32[70,4,128]{2,1,0:T(4,128)}, u32[]{:S(2)}) copy-start(f32[70,4,128]{2,1,0:T(4,128)} %param.7) | copy-start | bytes 430084

commit v4 on v3

--- a/solution.py
+++ b/solution.py
@@ -14,7 +14,8 @@
 NEAR, FAR = 2, 3
 GROUP = 8
 VMEM = pl.BlockSpec(memory_space=pltpu.VMEM)
-FIRST = (("q", 1), ("q", 2), ("g", 1), ("g", 2), ("d", 1), ("d", 2), ("s", 1))
+FIRST = (("q", 1), ("q", 2), ("g", 1), ("d", 1), ("s", 1))
+LATER = ("g", "d")
 FIELDS = ("q", "g", "d", "s")
 
 
@@ -42,58 +43,65 @@
     }
 
 
-def convolve(a, b):
-    out = [None] * (len(a) + len(b) - 1)
-    for i, x in enumerate(a):
-        for j, y in enumerate(b):
-            out[i + j] = x * y if out[i + j] is None else out[i + j] + x * y
-    return out
-
-
-def inner(a, b, moments):
-    total = None
-    for k, c in enumerate(convolve(a, b)):
-        term = c * moments[k]
-        total = term if total is None else total + term
-    return total
+def plus(a, b):
+    if a is None or b is None:
+        return b if a is None else a
+    return a + b
+
+
+def times(a, b):
+    return None if a is None or b is None else a * b
 
 
 def add_scaled(a, scale, b):
-    out = []
-    for k in range(max(len(a), len(b))):
-        if k >= len(b):
-            out.append(a[k])
-        elif k >= len(a):
-            out.append(scale * b[k])
-        else:
-            out.append(a[k] + scale * b[k])
-    return out
-
-
-def krylov_coefficients(moments, shift, one):
-    def times_a(a):
-        return add_scaled([0.0 * one] + list(a), shift, a)
+    size = max(len(a), len(b))
+    a, b = (list(v) + [None] * (size - len(v)) for v in (a, b))
+    return [plus(x, times(scale, y)) for x, y in zip(a, b)]
+
+
+def krylov_coefficients(first, mixed, rest, shift, one):
+    def inner(a, b):
+        total = times(times(a[0], b[0]), first)
+        for x, others in ((a[0], b), (b[0], a)):
+            for j in range(1, len(others)):
+                total = plus(total, times(times(x, others[j]), mixed[j - 1]))
+        for k in range(len(a) + len(b) - 3):
+            part = None
+            for i in range(1, len(a)):
+                if 1 <= k + 2 - i < len(b):
+                    part = plus(part, times(a[i], b[k + 2 - i]))
+            total = plus(total, times(part, rest[k]))
+        return total
+
+    def image_of(a):
+        return [None] + [plus(v, times(shift, a[k + 1]) if k + 1 < len(a) else None) for k, v in enumerate(a)]
 
     shadow = [one]
     residual = [one]
     direction = [one]
     solution = []
-    rho = moments[0]
+    rho = first
     for iteration in range(ITERS):
-        image = times_a(direction)
-        alpha = rho / inner(shadow, image, moments)
+        image = image_of(direction)
+        alpha = rho / inner(shadow, image)
         half = add_scaled(residual, -alpha, image)
-        second = times_a(half)
-        omega = inner(second, half, moments) / inner(second, second, moments)
+        second = image_of(half)
+        omega = inner(second, half) / inner(second, second)
         solution = add_scaled(solution, alpha, direction)
         solution = add_scaled(solution, omega, half)
         residual = add_scaled(half, -omega, second)
         if iteration + 1 < ITERS:
-            rho_next = inner(shadow, half, moments) - omega * inner(shadow, second, moments)
+            rho_next = inner(shadow, half) - omega * inner(shadow, second)
             beta = rho_next / rho * (alpha / omega)
             direction = add_scaled(residual, beta, add_scaled(direction, -omega, image))
             rho = rho_next
     return solution, residual
+
+
+PAIRS = (
+    [(0, j) for j in range(2 * ITERS + 1)]
+    + [(1 + k // 2, 1 + k - k // 2) for k in range(4 * ITERS - 1)]
+)
 
 
 def lanes_of(levels):
@@ -138,38 +146,8 @@
     return 1 - lax.rem(i, 2), 1 - lax.rem(j, 2), pole
 
 
-def shift_sums(own, levels, fq, fg, fd, fs, above, below, out, q_ref):
-    lane = lanes_of(levels)
-    clear_ends(q_ref, own, levels)
-    q_ref[own : own * (levels + 1), :] = fq[...]
-    weighted = jnp.zeros((levels, LANES), jnp.float32)
-    total = weighted
-    for i in range(own):
-        q = plane(q_ref, i, own, levels)[...]
-        scale = column(fg, i, own, levels)
-        diagonal = column(fd, i, own, levels)
-        near = jnp.where(lane == LANES - 1, 0.0, turn(q, -1)) + jnp.where(lane == 0, 0.0, turn(q, 1))
-        if i > 0:
-            near = near + plane(q_ref, i - 1, own, levels)[...]
-        if i < own - 1:
-            near = near + plane(q_ref, i + 1, own, levels)[...]
-        near = near + below[...] * plane(q_ref, i, own, levels, 1)[...]
-        near = near + above[...] * plane(q_ref, i, own, levels, -1)[...]
-        rough = column(fs, i, own, levels) - scale * (diagonal * q - near)
-        square = rough * rough
-        total = total + square / scale
-        weighted = weighted + square * diagonal
-    row_lane = lax.broadcasted_iota(jnp.int32, (1, LANES), 1)
-    row = jnp.where(
-        row_lane == 0,
-        jnp.sum(weighted, keepdims=True),
-        jnp.where(row_lane == 1, jnp.sum(total, keepdims=True), 0.0),
-    )
-    out[...] = jnp.broadcast_to(row[None], out.shape)
-
-
 def pack_kernel(own, levels, n_lat, x_hbm, b_hbm, c_hbm, h_hbm, coupling_hbm, to_a, to_b, lat_a, lat_b, above,
-                below, fq, fg, fd, fs, weights, x, b, c, h, coupling, q_ref, sem):
+                below, fq, fg, fd, fs, x, b, c, h, coupling, sem):
     copies = []
     moves = ((coupling_hbm, coupling), (x_hbm, x), (c_hbm, c), (h_hbm, h), (b_hbm, b))
     for k, (source, target) in enumerate(moves):
@@ -220,7 +198,6 @@
         a = jnp.where(lon_even == 1, east, west)
         to_a[k] = store[name][pl.ds(a, levels, stride=own), :]
         to_b[k] = store[name][pl.ds(east + west - a, levels, stride=own), :]
-    shift_sums(own, levels, fq, fg, fd, fs, above, below, weights, q_ref)
 
 
 def corner_kernel(own, levels, n_lat, lat_a, lat_b, to_a, to_b):
@@ -242,18 +219,33 @@
     return jnp.sum(jnp.where(lane == k, row, 0.0), axis=1, keepdims=True)
 
 
+def put_row(out, arrays):
+    lane = lax.broadcasted_iota(jnp.int32, (1, LANES), 1)
+    row = jnp.zeros((1, LANES), jnp.float32)
+    for k, value in enumerate(arrays):
+        row = jnp.where(lane == k, jnp.sum(value, keepdims=True), row)
+    out[...] = jnp.broadcast_to(row[None], out.shape)
+
+
 def total_row(gathered):
     return jnp.sum(gathered[...], axis=0)
 
 
 class Extended:
-    def __init__(self, columns, levels, d, g, above, below, lane):
+    def __init__(self, columns, levels, d, g, above, below, lane, far=None):
         self.columns, self.levels = columns, levels
+        self.far = far
         self.d, self.g = d, g
         self.above, self.below, self.lane = above, below, lane
 
     def at(self, pair, k, e, shift=0):
         return plane(pair[k], e, self.columns, self.levels, shift)[...]
+
+    def coefficient(self, name, k, e):
+        edges = (FAR - NEAR, self.columns - 1 - FAR + NEAR)
+        if self.far is not None and k == 0 and e in edges:
+            return self.far[LATER.index(name), edges.index(e)]
+        return self.at(self.g if name == "g" else self.d, k, e)
 
     def put(self, pair, k, e, value):
         plane(pair[k], e, self.columns, self.levels)[...] = value
@@ -265,13 +257,13 @@
         for k, q in enumerate((main, strip) if strips else (main,)):
             side = self.at(pair, k, e - 1) + self.at(pair, k, e + 1)
             levels = self.below[...] * self.at(pair, k, e, 1) + self.above[...] * self.at(pair, k, e, -1)
-            out.append((q, self.at(self.d, k, e) * q - (side + near[k]) - levels))
+            out.append((q, self.coefficient("d", k, e) * q - (side + near[k]) - levels))
         return out
 
 
 def first_kernel(own, levels, columns, n_lat, fq, fg, fd, fs, above, below, from_a, from_b, lat_a, lat_b,
-                 corners_a, corners_b, sums, k0, k1, k1_strip, to_a, to_b, g_main, g_strip, d_main, d_strip,
-                 shift_out, qa_main, qa_strip, qb_main, qb_strip, s_main, s_strip):
+                 corners_a, corners_b, k0, k1, k1_strip, to_a, to_b, g_main, g_strip, d_main, d_strip,
+                 out, qa_main, qa_strip, qb_main, qb_strip, s_main, s_strip):
     lane = lanes_of(levels)
     low = lane < LANES // 2
     lon_even, lat_even, _ = parity(n_lat)
@@ -281,12 +273,6 @@
     ext = Extended(columns, levels, where_to["d"], where_to["g"], above, below, lane)
     for ref in (*qa, *qb):
         clear_ends(ref, columns, levels)
-
-    row = total_row(sums)
-    weighted, total = lane_value(row, 0), lane_value(row, 1)
-    shift = jnp.where(total > 0.0, weighted / jnp.where(total > 0.0, total, 1.0), 1.0)
-    shift_out[...] = jnp.broadcast_to(shift, shift_out.shape)
-    shift = jnp.broadcast_to(shift, (levels, LANES))
 
     def unpack(north, south, name, i):
         back = -GROUP * (FIELDS.index(name) * own + i)
@@ -303,9 +289,10 @@
         is_east = jnp.full((levels, LANES), east, jnp.int32) == 1
         tile = corner[...]
         north = jnp.where(is_east, turn(tile, -GROUP * (1 + NEAR)), turn(tile, -GROUP * (1 - NEAR)))
-        for k, (name, distance) in enumerate(FIRST):
+        for k, (name, distance) in enumerate(FIRST + tuple((name, NEAR) for name in LATER)):
             e = jnp.where(east == 1, FAR + own - 1 + distance, FAR - distance)
-            ext.put(where_to[name], 0, e, block[k])
+            if k < len(FIRST):
+                ext.put(where_to[name], 0, e, block[k])
             strip = jnp.where(
                 is_east, unpack(north, tile, name, distance - 1), unpack(north, tile, name, own - distance)
             )
@@ -316,32 +303,46 @@
             ext.put(qb, k, e, value)
             if k == 0 and FAR <= e < FAR + own:
                 k0[pl.ds(e - FAR, levels, stride=own), :] = value
+    mixed = jnp.zeros((levels, LANES), jnp.float32)
+    square = mixed
     for e in range(FAR, FAR + own):
         for k, (q, image) in enumerate(ext.stencil(qb, e)):
-            value = ext.at(where_to["g"], k, e) * image - shift * q
-            out = k1 if k == 0 else k1_strip
-            out[pl.ds(e - FAR, levels, stride=own), :] = value
-    for out, side in ((to_a, lon_even), (to_b, 1 - lon_even)):
+            scale = ext.at(where_to["g"], k, e)
+            value = scale * image
+            target = k1 if k == 0 else k1_strip
+            target[pl.ds(e - FAR, levels, stride=own), :] = value
+            if k == 0:
+                mixed = mixed + q * image
+                square = square + value * image
+    put_row(out, (mixed, square))
+    for message, side in ((to_a, lon_even), (to_b, 1 - lon_even)):
         packed = jnp.zeros((levels, LANES), jnp.float32)
         for distance in range(1, FAR + 1):
             i = jnp.where(side == 1, own - distance, distance - 1)
-            out[distance - 1] = k1[pl.ds(i, levels, stride=own), :]
+            message[distance - 1] = k1[pl.ds(i, levels, stride=own), :]
             offset = 2 * GROUP * (distance - 1) + GROUP
             rolled = turn(k1_strip[pl.ds(i, levels, stride=own), :], offset)
             packed = jnp.where(lane // (2 * GROUP) == distance - 1, rolled, packed)
-        out[FAR] = packed
+        message[FAR] = packed
+        i = jnp.where(side == 1, own - NEAR, NEAR - 1)
+        for k, name in enumerate(LATER):
+            message[FAR + 1 + k] = column(fields[name], i, own, levels)
 
 
 def second_kernel(own, levels, columns, n_lat, k0, k1, k1_strip, from_a, from_b, g_main, g_strip, d_main, d_strip,
-                  above, below, shift_row, k2, k3, k4, out, qa_main, qa_strip, qb_main, qb_strip):
+                  above, below, shift_sums, k2, k3, k4, out, shift_row, qa_main, qa_strip, qb_main, qb_strip, far):
     lane = lanes_of(levels)
     lon_even, _, _ = parity(n_lat)
     qa, qb = (qa_main, qa_strip), (qb_main, qb_strip)
     g = (g_main, g_strip)
-    ext = Extended(columns, levels, (d_main, d_strip), g, above, below, lane)
+    ext = Extended(columns, levels, (d_main, d_strip), g, above, below, lane, far)
     for ref in (*qa, *qb):
         clear_ends(ref, columns, levels)
-    shift = jnp.broadcast_to(shift_row[...], (levels, LANES))
+    row = total_row(shift_sums)
+    mixed, square = lane_value(row, 0), lane_value(row, 1)
+    shift = jnp.where(mixed > 0.0, square / jnp.where(mixed > 0.0, mixed, 1.0), 1.0)
+    shift_row[...] = jnp.broadcast_to(shift, shift_row.shape)
+    shift = jnp.broadcast_to(shift, (levels, LANES))
     for i in range(own):
         ext.put(qa, 0, FAR + i, column(k1, i, own, levels))
         ext.put(qa, 1, FAR + i, column(k1_strip, i, own, levels))
@@ -350,17 +351,18 @@
             e = jnp.where(east == 1, FAR + own - 1 + distance, FAR - distance)
             ext.put(qa, 0, e, block[distance - 1])
             ext.put(qa, 1, e, turn(block[FAR], -(2 * GROUP * (distance - 1) + GROUP)))
+        for k in range(len(LATER)):
+            far[k, east] = block[FAR + 1 + k]
     source, target = qa, qb
     for step, reach in ((0, FAR - 1), (1, FAR - 2)):
         for e in range(FAR - reach, FAR + own + reach):
             for k, (q, image) in enumerate(ext.stencil(source, e)):
-                value = ext.at(g, k, e) * image - shift * q
+                value = ext.coefficient("g", k, e) * image - shift * q
                 ext.put(target, k, e, value)
                 if k == 0 and FAR <= e < FAR + own:
                     (k2, k3)[step][pl.ds(e - FAR, levels, stride=own), :] = value
         source, target = target, source
-    count = 4 * ITERS + 1
-    sums = [jnp.zeros((levels, LANES), jnp.float32) for _ in range(count)]
+    sums = [jnp.zeros((levels, LANES), jnp.float32) for _ in PAIRS]
     for i in range(own):
         e = FAR + i
         ((q, image),) = ext.stencil(source, e, strips=False)
@@ -369,22 +371,18 @@
         k4[pl.ds(i, levels, stride=own), :] = last
         v = [column(k0, i, own, levels), column(k1, i, own, levels), column(k2, i, own, levels), q, last]
         w = 1.0 / scale
-        for k in range(count):
-            if k % 2 == 0:
-                lead = v[k // 2] * w
-            sums[k] = sums[k] + lead * v[k - k // 2]
-    row_lane = lax.broadcasted_iota(jnp.int32, (1, LANES), 1)
-    row = jnp.zeros((1, LANES), jnp.float32)
-    for k in range(count):
-        row = jnp.where(row_lane == k, jnp.sum(sums[k], keepdims=True), row)
-    out[...] = jnp.broadcast_to(row[None], out.shape)
+        lead = [a * w for a in v]
+        for k, (a, b) in enumerate(PAIRS):
+            sums[k] = sums[k] + lead[a] * v[b]
+    put_row(out, sums)
 
 
 def final_kernel(sums, shift_row, x, c, k0, k1, k2, k3, k4, out, rest):
     row = total_row(sums)
-    moments = [lane_value(row, k) for k in range(4 * ITERS + 1)]
+    first, *others = [lane_value(row, k) for k in range(len(PAIRS))]
     shift = lane_value(shift_row[...], 0)
-    solution, residual = krylov_coefficients(moments, shift, jnp.ones((1, 1), jnp.float32))
+    one = jnp.ones((1, 1), jnp.float32)
+    solution, residual = krylov_coefficients(first, others[: 2 * ITERS], others[2 * ITERS :], shift, one)
     vectors = (k0, k1, k2, k3, k4)
     inverse = 1.0 / c[...]
 
@@ -431,35 +429,36 @@
     whole = real(levels * own, LANES)
     tile = real(levels, LANES)
     rows = real(n_lon * n_lat, 1, LANES)
-    padded = ((levels + 2) * own, LANES)
     extended = ((levels + 2) * columns, LANES)
 
-    to_a, to_b, lat_a, lat_b, above, below, *fields, weights = call(
+    to_a, to_b, lat_a, lat_b, above, below, *fields = call(
         functools.partial(pack_kernel, own, levels, n_lat),
         tuple(pltpu.with_memory_space_constraint(v, pltpu.HBM) for v in (x, b, c, h, coupling)),
-        [real(len(FIRST), levels, LANES)] * 2 + [tile] * 4 + [whole] * len(FIELDS) + [rows],
-        [(levels * own, LANES)] * 4 + [(1, levels - 1), padded, pltpu.SemaphoreType.DMA((5,))],
+        [real(len(FIRST), levels, LANES)] * 2 + [tile] * 4 + [whole] * len(FIELDS),
+        [(levels * own, LANES)] * 4 + [(1, levels - 1), pltpu.SemaphoreType.DMA((5,))],
         [pl.BlockSpec(memory_space=pltpu.HBM)] * 5,
     )
     lat_a, lat_b = swap(lat_a, "lat_even"), swap(lat_b, "lat_odd")
-    from_a, from_b = swap(to_a, "lon_even"), swap(to_b, "lon_odd")
+    from_a = swap(to_a, "lon_even")
+    from_b = swap(to_b, "lon_odd")
     corners_a, corners_b = call(
         functools.partial(corner_kernel, own, levels, n_lat), (lat_a, lat_b), [tile] * 2
     )
     corners_a, corners_b = swap(corners_a, "lon_even"), swap(corners_b, "lon_odd")
-    weights = everywhere(weights)
-    k0, k1, k1_strip, to_a, to_b, *coefficients, shift = call(
+    k0, k1, k1_strip, to_a, to_b, *coefficients, shift_sums = call(
         functools.partial(first_kernel, own, levels, columns, n_lat),
-        (*fields, above, below, from_a, from_b, lat_a, lat_b, corners_a, corners_b, weights),
-        [whole] * 3 + [real(FAR + 1, levels, LANES)] * 2 + [real(*extended)] * 4 + [real(1, LANES)],
+        (*fields, above, below, from_a, from_b, lat_a, lat_b, corners_a, corners_b),
+        [whole] * 3 + [real(FAR + 1 + len(LATER), levels, LANES)] * 2 + [real(*extended)] * 4 + [rows],
         [extended] * 6,
     )
-    from_a, from_b = swap(to_a, "lon_even"), swap(to_b, "lon_odd")
-    k2, k3, k4, sums = call(
+    from_a = swap(to_a, "lon_even")
+    from_b = swap(to_b, "lon_odd")
+    shift_sums = everywhere(shift_sums)
+    k2, k3, k4, sums, shift = call(
         functools.partial(second_kernel, own, levels, columns, n_lat),
-        (k0, k1, k1_strip, from_a, from_b, *coefficients, above, below, shift),
-        [whole] * 3 + [rows],
-        [extended] * 4,
+        (k0, k1, k1_strip, from_a, from_b, *coefficients, above, below, shift_sums),
+        [whole] * 3 + [rows, real(1, LANES)],
+        [extended] * 4 + [(len(LATER), 2, levels, LANES)],
     )
     sums = everywhere(sums)
     out, rest = call(final_kernel, (sums, shift, x, c, k0, k1, k2, k3, k4), [whole] * 2)

time: 52.1 us -> 48.9 us (0.939)
  waiting for transfers between devices: 12.4 us -> 8.34 us
    ppermute x8, waiting for transfers between devices: 12.4 us -> 8.34 us  [swap(): return lax.ppermute(value, AXES, pairs[name])]
where the time goes in v4:
time: 48.9 us; the launch traced here: 48.8 us
  blocking collectives  18.2 us (37%)
  starting transfers between devices  15.4 us (31%)
  waiting for transfers between devices  8.34 us (17%)
  Pallas kernels  6.18 us (13%)
  between operations  0.69 us (1%)
    all_to_all x2, blocking collectives, everywhere(): return lax.all_to_all(rows, AXES, 0, 0, tiled=True)  18.2 us
    ppermute x8, starting transfers between devices, swap(): return lax.ppermute(value, AXES, pairs[name])  15.4 us
    ppermute x8, waiting for transfers between devices, swap(): return lax.ppermute(value, AXES, pairs[name])  8.34 us
    pallas_call x5, Pallas kernels, call(): pl.pallas_call(kernel, out_shape=tuple(outs) if len(outs) > 1 else outs[0...  6.18 us
  transfers between devices with their start and end apart: 8, of which 3 were waited for; matrix products, arithmetic and copies ran while one was open for 0% of the time, Pallas kernels for 0%

profile of v4, /device:TPU:0, one launch (start us, length us, event | category | flops | bytes accessed | tf_op | source)
XLA Modules:
  0.0 48.8 jit_solution(7185591959950651922)
XLA Ops:
  0.6 1.8 %shard_map.68 = (f32[5,70,128]{2,1,0:T(8,128)S(1)}, f32[5,70,128]{2,1,0:T(8,128)S(1)}, f32[70,128]{1,0:T(8,128)S(1)}, f32[70,128]{1,0:T(8,128)S(1)}, f32[70,128]...) custom-call(f32[280,128]{1,0:T(8,128)} %bitcast.7, ...), custom_call_target="tpu_custom_call" | custom-call | tf_op jit(solution)/shard_map/pallas_call | solution.py:414
  2.4 3.0 %collective-permute-start = (f32[5,70,128]{2,1,0:T(8,128)S(1)}, f32[5,70,128]{2,1,0:T(8,128)S(1)}, u32[]{:S(2)}, u32[]{:S(2)}) collective-permute-start(f32[5,70,128]{2,1,0:T(8,128)S(1)} %get-tuple-element.37), channel_id=1, source_target_pairs={{0,4},{1,5},{2,6},{3,7},{4,0},{5,1},{6,2},{7,3},{8,12},{9,13},{10,... | collective-permute-start | bytes 537608 | tf_op jit(solution)/shard_map/ppermute | solution.py:424
  5.5 3.6 %collective-permute-start.1 = (f32[5,70,128]{2,1,0:T(8,128)S(1)}, f32[5,70,128]{2,1,0:T(8,128)S(1)}, u32[]{:S(2)}, u32[]{:S(2)}) collective-permute-start(f32[5,70,128]{2,1,0:T(8,128)S(1)} %get-tuple-element.38), channel_id=1, source_target_pairs={{0,28},{1,29},{2,30},{3,31},{4,8},{5,9},{6,10},{7,11},{8,4},{9,5},... | collective-permute-start | bytes 537608 | tf_op jit(solution)/shard_map/ppermute | solution.py:424
  9.0 0.0 collective-permute-start.2
  9.0 0.0 collective-permute-start.3
  9.0 1.2 %collective-permute-done.2.lat_a = f32[70,128]{1,0:T(8,128)S(1)} collective-permute-done((f32[70,128]{1,0:T(8,128)S(1)}, f32[70,128]{1,0:T(8,128)S(1)}, u32[]{:S(2)}, u32[]{:S(2)}) %collective-permute-start.2) | collective-permute-done | bytes 35872 | tf_op jit(solution)/shard_map/ppermute | solution.py:424
  10.3 4.0 %collective-permute-done.3.lat_b = f32[70,128]{1,0:T(8,128)S(1)} collective-permute-done((f32[70,128]{1,0:T(8,128)S(1)}, f32[70,128]{1,0:T(8,128)S(1)}, u32[]{:S(2)}, u32[]{:S(2)}) %collective-permute-start.3) | collective-permute-done | bytes 35872 | tf_op jit(solution)/shard_map/ppermute | solution.py:424
  14.3 0.1 shard_map.69
  14.4 1.4 %collective-permute-start.4 = (f32[70,128]{1,0:T(8,128)S(1)}, f32[70,128]{1,0:T(8,128)S(1)}, u32[]{:S(2)}, u32[]{:S(2)}) collective-permute-start(f32[70,128]{1,0:T(8,128)S(1)} %get-tuple-element.41), channel_id=1, source_target_pairs={{0,4},{1,5},{2,6},{3,7},{4,0},{5,1},{6,2},{7,3},{8,12},{9,13},{10,... | collective-permute-start | bytes 107528 | tf_op jit(solution)/shard_map/ppermute | solution.py:424
  15.8 3.6 %collective-permute-start.5 = (f32[70,128]{1,0:T(8,128)S(1)}, f32[70,128]{1,0:T(8,128)S(1)}, u32[]{:S(2)}, u32[]{:S(2)}) collective-permute-start(f32[70,128]{1,0:T(8,128)S(1)} %get-tuple-element.42), channel_id=1, source_target_pairs={{0,28},{1,29},{2,30},{3,31},{4,8},{5,9},{6,10},{7,11},{8,4},{9,5},... | collective-permute-start | bytes 107528 | tf_op jit(solution)/shard_map/ppermute | solution.py:424
  19.4 0.0 collective-permute-done.4.corners_a
  19.4 3.1 %collective-permute-done.5.corners_b = f32[70,128]{1,0:T(8,128)S(1)} collective-permute-done((f32[70,128]{1,0:T(8,128)S(1)}, f32[70,128]{1,0:T(8,128)S(1)}, u32[]{:S(2)}, u32[]{:S(2)}) %collective-permute-start.5) | collective-permute-done | bytes 35872 | tf_op jit(solution)/shard_map/ppermute | solution.py:424
  22.4 0.0 collective-permute-done.from_a
  22.4 0.0 collective-permute-done.1.from_b
  22.4 1.8 %shard_map.70 = (f32[280,128]{1,0:T(8,128)S(1)}, f32[280,128]{1,0:T(8,128)S(1)}, f32[280,128]{1,0:T(8,128)S(1)}, f32[6,70,128]{2,1,0:T(8,128)S(1)}, f32[6,70,128...) custom-call(f32[280,128]{1,0:T(8,128)S(1)} %get-tuple-element.31.fq,, ...), custom_call_target="tpu_custom_call" | custom-call | tf_op jit(solution)/shard_map/pallas_call | solution.py:414
  24.2 0.1 collective-permute-start.6
  24.3 3.7 %collective-permute-start.7 = (f32[6,70,128]{2,1,0:T(8,128)S(1)}, f32[6,70,128]{2,1,0:T(8,128)S(1)}, u32[]{:S(2)}, u32[]{:S(2)}) collective-permute-start(f32[6,70,128]{2,1,0:T(8,128)S(1)} %get-tuple-element.47), channel_id=1, source_target_pairs={{0,28},{1,29},{2,30},{3,31},{4,8},{5,9},{6,10},{7,11},{8,4},{9,5},... | collective-permute-start | bytes 645128 | tf_op jit(solution)/shard_map/ppermute | solution.py:424
  28.1 9.3 %all_to_all.10.shift_sums = f32[32,1,128]{2,1,0:T(1,128)S(1)} all-to-all(f32[32,1,128]{2,1,0:T(1,128)S(1)} %get-tuple-element.52), channel_id=1, replica_groups=mesh['lon'=8,'lat'=4] {'lon','lat'}, dimensions={0} | all-to-all | bytes 32768 | tf_op jit(solution)/shard_map/all_to_all | solution.py:427
  37.3 0.0 collective-permute-done.6.from_a
  37.4 0.0 collective-permute-done.7.from_b
  37.4 0.0 copy-start
  37.4 0.0 copy-start.1
  37.4 1.5 %shard_map.71 = (f32[280,128]{1,0:T(8,128)S(1)}, f32[280,128]{1,0:T(8,128)S(1)}, f32[280,128]{1,0:T(8,128)S(1)}, f32[32,1,128]{2,1,0:T(1,128)S(1)}, f32[1,128]{1,0:T(1,128)S(1)}) custom-call(f32[280,128]{1,0:T(8,128)S(1)} %get-tuple-element.43.k0, f32[280,128]{1,0:T(8,128)S(1)} %get-tuple-element.44.k1, f32[280,128]{1,0:T(8,128)S(1)} %get-tuple-element.45.k1_strip, ...), custom_call_target="tpu_custom_call" | custom-call | tf_op jit(solution)/shard_map/pallas_call | solution.py:414
  38.9 8.9 %all_to_all.11.sums = f32[32,1,128]{2,1,0:T(1,128)S(1)} all-to-all(f32[32,1,128]{2,1,0:T(1,128)S(1)} %get-tuple-element.53), channel_id=1, replica_groups=mesh['lon'=8,'lat'=4] {'lon','lat'}, dimensions={0} | all-to-all | bytes 32768 | tf_op jit(solution)/shard_map/all_to_all | solution.py:427
  47.8 0.0 copy-done
  47.8 0.0 copy-done.1
  47.8 1.0 %shard_map.72 = (f32[280,128]{1,0:T(8,128)}, f32[280,128]{1,0:T(8,128)}) custom-call(f32[32,1,128]{2,1,0:T(1,128)S(1)} %all_to_all.11.sums, f32[1,128]{1,0:T(1,128)S(1)} %get-tuple-element.54.shift_row, f32[280,128]{1,0:T(8,128)S(1)} %bitcast.8, f32[280,128]{1,0:T(8,128)S(1)} %bitcast.10, f32[280,128]{1,0:T(8,128)S(1)} %get-tuple-element.43.k0, ...), custom_call_target="tpu_custom_call" | custom-call | tf_op jit(solution)/shard_map/pallas_call | solution.py:414
Async XLA Ops:
  2.4 20.0 %collective-permute-start = (f32[5,70,128]{2,1,0:T(8,128)S(1)}, f32[5,70,128]{2,1,0:T(8,128)S(1)}, u32[]{:S(2)}, u32[]{:S(2)}) collective-permute-start(f32[5,70,128]{2,1,0:T(8,128)S(1)} %get-tuple-element.37), channel_id=1, source_target_pairs={{0,4},{1,5},{2,6},{3,7},{4,0},{5,1},{6,2},{7,3},{8,12},{9,13},{10,... | collective-permute-start | bytes 537608 | tf_op jit(solution)/shard_map/ppermute | solution.py:424
  5.5 17.0 %collective-permute-start.1 = (f32[5,70,128]{2,1,0:T(8,128)S(1)}, f32[5,70,128]{2,1,0:T(8,128)S(1)}, u32[]{:S(2)}, u32[]{:S(2)}) collective-permute-start(f32[5,70,128]{2,1,0:T(8,128)S(1)} %get-tuple-element.38), channel_id=1, source_target_pairs={{0,28},{1,29},{2,30},{3,31},{4,8},{5,9},{6,10},{7,11},{8,4},{9,5},... | collective-permute-start | bytes 537608 | tf_op jit(solution)/shard_map/ppermute | solution.py:424
  9.0 1.2 %collective-permute-start.2 = (f32[70,128]{1,0:T(8,128)S(1)}, f32[70,128]{1,0:T(8,128)S(1)}, u32[]{:S(2)}, u32[]{:S(2)}) collective-permute-start(f32[70,128]{1,0:T(8,128)S(1)} %get-tuple-element.39), channel_id=1, source_target_pairs={{0,1},{1,0},{2,3},{3,2},{4,5},{5,4},{6,7},{7,6},{8,9},{9,8},{10,11... | collective-permute-start | bytes 107528 | tf_op jit(solution)/shard_map/ppermute | solution.py:424
  9.0 5.3 %collective-permute-start.3 = (f32[70,128]{1,0:T(8,128)S(1)}, f32[70,128]{1,0:T(8,128)S(1)}, u32[]{:S(2)}, u32[]{:S(2)}) collective-permute-start(f32[70,128]{1,0:T(8,128)S(1)} %get-tuple-element.40), channel_id=1, source_target_pairs={{0,16},{1,2},{2,1},{3,19},{4,20},{5,6},{6,5},{7,23},{8,24},{9,10},... | collective-permute-start | bytes 107528 | tf_op jit(solution)/shard_map/ppermute | solution.py:424
  14.4 5.0 %collective-permute-start.4 = (f32[70,128]{1,0:T(8,128)S(1)}, f32[70,128]{1,0:T(8,128)S(1)}, u32[]{:S(2)}, u32[]{:S(2)}) collective-permute-start(f32[70,128]{1,0:T(8,128)S(1)} %get-tuple-element.41), channel_id=1, source_target_pairs={{0,4},{1,5},{2,6},{3,7},{4,0},{5,1},{6,2},{7,3},{8,12},{9,13},{10,... | collective-permute-start | bytes 107528 | tf_op jit(solution)/shard_map/ppermute | solution.py:424
  15.8 6.7 %collective-permute-start.5 = (f32[70,128]{1,0:T(8,128)S(1)}, f32[70,128]{1,0:T(8,128)S(1)}, u32[]{:S(2)}, u32[]{:S(2)}) collective-permute-start(f32[70,128]{1,0:T(8,128)S(1)} %get-tuple-element.42), channel_id=1, source_target_pairs={{0,28},{1,29},{2,30},{3,31},{4,8},{5,9},{6,10},{7,11},{8,4},{9,5},... | collective-permute-start | bytes 107528 | tf_op jit(solution)/shard_map/ppermute | solution.py:424
  24.2 13.1 %collective-permute-start.6 = (f32[6,70,128]{2,1,0:T(8,128)S(1)}, f32[6,70,128]{2,1,0:T(8,128)S(1)}, u32[]{:S(2)}, u32[]{:S(2)}) collective-permute-start(f32[6,70,128]{2,1,0:T(8,128)S(1)} %get-tuple-element.46), channel_id=1, source_target_pairs={{0,4},{1,5},{2,6},{3,7},{4,0},{5,1},{6,2},{7,3},{8,12},{9,13},{10,... | collective-permute-start | bytes 645128 | tf_op jit(solution)/shard_map/ppermute | solution.py:424
  24.3 13.0 %collective-permute-start.7 = (f32[6,70,128]{2,1,0:T(8,128)S(1)}, f32[6,70,128]{2,1,0:T(8,128)S(1)}, u32[]{:S(2)}, u32[]{:S(2)}) collective-permute-start(f32[6,70,128]{2,1,0:T(8,128)S(1)} %get-tuple-element.47), channel_id=1, source_target_pairs={{0,28},{1,29},{2,30},{3,31},{4,8},{5,9},{6,10},{7,11},{8,4},{9,5},... | collective-permute-start | bytes 645128 | tf_op jit(solution)/shard_map/ppermute | solution.py:424
  37.4 10.4 %copy-start = (f32[70,4,128]{2,1,0:T(4,128)S(1)}, f32[70,4,128]{2,1,0:T(4,128)}, u32[]{:S(2)}) copy-start(f32[70,4,128]{2,1,0:T(4,128)} %param.6) | copy-start | bytes 430084
  37.4 10.4 %copy-start.1 = (f32[70,4,128]{2,1,0:T(4,128)S(1)}, f32[70,4,128]{2,1,0:T(4,128)}, u32[]{:S(2)}) copy-start(f32[70,4,128]{2,1,0:T(4,128)} %param.7) | copy-start | bytes 430084

commit v5 on v4

--- a/solution.py
+++ b/solution.py
@@ -11,6 +11,7 @@
 AXES = ("lon", "lat")
 ITERS = 2
 LANES = 128
+SUBLANES = 8
 NEAR, FAR = 2, 3
 GROUP = 8
 VMEM = pl.BlockSpec(memory_space=pltpu.VMEM)
@@ -126,14 +127,14 @@
     return ref[pl.ds(i, levels, stride=own), :]
 
 
-def shifted_rows(main, strip, lane):
+def shifted_rows(main, strip, lane, strips=True):
     main_s, main_n = turn(main, -1), turn(main, 1)
     strip_s, strip_n = turn(strip, -1), turn(strip, 1)
     first, last = lane == 0, lane == LANES - 1
-    return (
-        jnp.where(last, strip_s, main_s) + jnp.where(first, strip_n, main_n),
-        jnp.where(last, main_s, strip_s) + jnp.where(first, main_n, strip_n),
-    )
+    out = [jnp.where(last, strip_s, main_s) + jnp.where(first, strip_n, main_n)]
+    if strips:
+        out.append(jnp.where(last, main_s, strip_s) + jnp.where(first, main_n, strip_n))
+    return out
 
 
 def transformed(x, b, c, h, above, below):
@@ -223,7 +224,7 @@
     lane = lax.broadcasted_iota(jnp.int32, (1, LANES), 1)
     row = jnp.zeros((1, LANES), jnp.float32)
     for k, value in enumerate(arrays):
-        row = jnp.where(lane == k, jnp.sum(value, keepdims=True), row)
+        row = jnp.where(lane == k, value.total(), row)
     out[...] = jnp.broadcast_to(row[None], out.shape)
 
 
@@ -232,117 +233,151 @@
 
 
 class Extended:
-    def __init__(self, columns, levels, d, g, above, below, lane, far=None):
+    def __init__(self, columns, levels, d, g, above, below, far=None):
         self.columns, self.levels = columns, levels
+        self.d, self.g = d, g
+        self.above, self.below = above, below
         self.far = far
-        self.d, self.g = d, g
-        self.above, self.below, self.lane = above, below, lane
-
-    def at(self, pair, k, e, shift=0):
-        return plane(pair[k], e, self.columns, self.levels, shift)[...]
-
-    def coefficient(self, name, k, e):
+
+    def at(self, pair, k, e, rows, shift=0):
+        start, count = rows
+        return pair[k][pl.ds((1 + start + shift) * self.columns + e, count, stride=self.columns), :]
+
+    def set(self, pair, k, e, rows, value):
+        start, count = rows
+        pair[k][pl.ds((1 + start) * self.columns + e, count, stride=self.columns), :] = value
+
+    def put(self, pair, k, e, value):
+        self.set(pair, k, e, (0, self.levels), value)
+
+    def coefficient(self, name, k, e, rows):
         edges = (FAR - NEAR, self.columns - 1 - FAR + NEAR)
         if self.far is not None and k == 0 and e in edges:
-            return self.far[LATER.index(name), edges.index(e)]
-        return self.at(self.g if name == "g" else self.d, k, e)
-
-    def put(self, pair, k, e, value):
-        plane(pair[k], e, self.columns, self.levels)[...] = value
-
-    def stencil(self, pair, e, strips=True):
-        main, strip = self.at(pair, 0, e), self.at(pair, 1, e)
-        near = shifted_rows(main, strip, self.lane)
-        out = []
-        for k, q in enumerate((main, strip) if strips else (main,)):
-            side = self.at(pair, k, e - 1) + self.at(pair, k, e + 1)
-            levels = self.below[...] * self.at(pair, k, e, 1) + self.above[...] * self.at(pair, k, e, -1)
-            out.append((q, self.coefficient("d", k, e) * q - (side + near[k]) - levels))
-        return out
-
-
-def first_kernel(own, levels, columns, n_lat, fq, fg, fd, fs, above, below, from_a, from_b, lat_a, lat_b,
-                 corners_a, corners_b, k0, k1, k1_strip, to_a, to_b, g_main, g_strip, d_main, d_strip,
-                 out, qa_main, qa_strip, qb_main, qb_strip, s_main, s_strip):
+            start, count = rows
+            return self.far[LATER.index(name), edges.index(e), start : start + count, :]
+        return self.at(self.g if name == "g" else self.d, k, e, rows)
+
+    def sweep(self, pair, first, last, strips=True):
+        for start in range(0, self.levels, SUBLANES):
+            rows = start, min(SUBLANES, self.levels - start)
+            lane = lanes_of(rows[1])
+            above, below = (ref[start : start + rows[1], :] for ref in (self.above, self.below))
+            center = {}
+
+            def middle(k, e):
+                if (k, e) not in center:
+                    center[k, e] = self.at(pair, k, e, rows)
+                return center[k, e]
+
+            for e in range(first, last + 1):
+                near = shifted_rows(middle(0, e), middle(1, e), lane, strips)
+                out = []
+                for k in range(1 + strips):
+                    q = middle(k, e)
+                    side = middle(k, e - 1) + middle(k, e + 1)
+                    levels = below * self.at(pair, k, e, rows, 1) + above * self.at(pair, k, e, rows, -1)
+                    out.append((q, self.coefficient("d", k, e, rows) * q - (side + near[k]) - levels))
+                yield rows, e, out
+
+
+class Sums:
+    def __init__(self):
+        self.parts = {}
+
+    def add(self, value):
+        count = value.shape[0]
+        self.parts[count] = self.parts[count] + value if count in self.parts else value
+
+    def total(self):
+        return sum(jnp.sum(v, keepdims=True) for v in self.parts.values())
+
+
+def own_rows(i, own, rows):
+    start, count = rows
+    return pl.ds(start * own + i, count, stride=own), slice(None)
+
+
+def own_kernel(own, levels, columns, n_lat, fq, fg, fd, fs, lat_a, lat_b, *outs):
+    group = lanes_of(levels) // GROUP
+    _, lat_even, _ = parity(n_lat)
+    even = jnp.full((levels, LANES), lat_even, jnp.int32) == 1
+    a, b = lat_a[...], lat_b[...]
+    north, south = jnp.where(even, b, a), jnp.where(even, a, b)
+    for f, field in enumerate((fq, fg, fd, fs)):
+        main, strip = outs[2 * f : 2 * f + 2]
+        if f == 0:
+            clear_ends(main, columns, levels)
+            clear_ends(strip, columns, levels)
+        for i in range(own):
+            slot = f * own + i
+            plane(main, FAR + i, columns, levels)[...] = column(field, i, own, levels)
+            edges = turn(jnp.where(group == slot, south, north), -GROUP * slot)
+            plane(strip, FAR + i, columns, levels)[...] = edges
+
+
+def first_kernel(own, levels, columns, n_lat, fg, fd, above, below, from_a, from_b, corners_a, corners_b, *refs):
+    extended = refs[8:16]
+    k0, k1, k1_strip, to_a, to_b, out, qb_main, qb_strip = refs[16:]
     lane = lanes_of(levels)
     low = lane < LANES // 2
-    lon_even, lat_even, _ = parity(n_lat)
-    even = jnp.full((levels, LANES), lat_even, jnp.int32) == 1
-    qa, qb = (qa_main, qa_strip), (qb_main, qb_strip)
-    where_to = {"q": qa, "g": (g_main, g_strip), "d": (d_main, d_strip), "s": (s_main, s_strip)}
-    ext = Extended(columns, levels, where_to["d"], where_to["g"], above, below, lane)
-    for ref in (*qa, *qb):
+    lon_even, _, _ = parity(n_lat)
+    pairs = {name: extended[2 * f : 2 * f + 2] for f, name in enumerate(FIELDS)}
+    qa, qb = pairs["q"], (qb_main, qb_strip)
+    ext = Extended(columns, levels, pairs["d"], pairs["g"], above, below)
+    for ref in qb:
         clear_ends(ref, columns, levels)
-
-    def unpack(north, south, name, i):
-        back = -GROUP * (FIELDS.index(name) * own + i)
-        return jnp.where(low, turn(south, back), turn(north, back))
-
-    fields = dict(zip(FIELDS, (fq, fg, fd, fs)))
-    a, b = lat_a[...], lat_b[...]
-    north, south = jnp.where(even, b, a), jnp.where(even, a, b)
-    for name in FIELDS:
-        for i in range(own):
-            ext.put(where_to[name], 0, FAR + i, column(fields[name], i, own, levels))
-            ext.put(where_to[name], 1, FAR + i, unpack(north, south, name, i))
     for block, corner, east in ((from_a, corners_a, lon_even), (from_b, corners_b, 1 - lon_even)):
-        is_east = jnp.full((levels, LANES), east, jnp.int32) == 1
         tile = corner[...]
-        north = jnp.where(is_east, turn(tile, -GROUP * (1 + NEAR)), turn(tile, -GROUP * (1 - NEAR)))
         for k, (name, distance) in enumerate(FIRST + tuple((name, NEAR) for name in LATER)):
             e = jnp.where(east == 1, FAR + own - 1 + distance, FAR - distance)
             if k < len(FIRST):
-                ext.put(where_to[name], 0, e, block[k])
-            strip = jnp.where(
-                is_east, unpack(north, tile, name, distance - 1), unpack(north, tile, name, own - distance)
-            )
-            ext.put(where_to[name], 1, e, strip)
-    for e in range(FAR - 1, FAR + own + 1):
-        for k, (_, image) in enumerate(ext.stencil(qa, e)):
-            value = ext.at(where_to["s"], k, e) - ext.at(where_to["g"], k, e) * image
-            ext.put(qb, k, e, value)
+                ext.put(pairs[name], 0, e, block[k])
+            slot = FIELDS.index(name) * own + jnp.where(east == 1, distance - 1, own - distance)
+            south = lax.rem(2 * LANES - GROUP * slot, LANES)
+            north = lax.rem(south + LANES - GROUP * jnp.where(east == 1, 1 + NEAR, 1 - NEAR), LANES)
+            ext.put(pairs[name], 1, e, jnp.where(low, pltpu.roll(tile, south, 1), pltpu.roll(tile, north, 1)))
+    for rows, e, tiles in ext.sweep(qa, FAR - 1, FAR + own):
+        for k, (_, image) in enumerate(tiles):
+            value = ext.at(pairs["s"], k, e, rows) - ext.at(pairs["g"], k, e, rows) * image
+            ext.set(qb, k, e, rows, value)
             if k == 0 and FAR <= e < FAR + own:
-                k0[pl.ds(e - FAR, levels, stride=own), :] = value
-    mixed = jnp.zeros((levels, LANES), jnp.float32)
-    square = mixed
-    for e in range(FAR, FAR + own):
-        for k, (q, image) in enumerate(ext.stencil(qb, e)):
-            scale = ext.at(where_to["g"], k, e)
-            value = scale * image
-            target = k1 if k == 0 else k1_strip
-            target[pl.ds(e - FAR, levels, stride=own), :] = value
+                k0[own_rows(e - FAR, own, rows)] = value
+    mixed, square = Sums(), Sums()
+    for rows, e, tiles in ext.sweep(qb, FAR, FAR + own - 1):
+        for k, (q, image) in enumerate(tiles):
+            value = ext.at(pairs["g"], k, e, rows) * image
+            (k1, k1_strip)[k][own_rows(e - FAR, own, rows)] = value
             if k == 0:
-                mixed = mixed + q * image
-                square = square + value * image
+                mixed.add(q * image)
+                square.add(value * image)
     put_row(out, (mixed, square))
     for message, side in ((to_a, lon_even), (to_b, 1 - lon_even)):
         packed = jnp.zeros((levels, LANES), jnp.float32)
         for distance in range(1, FAR + 1):
             i = jnp.where(side == 1, own - distance, distance - 1)
-            message[distance - 1] = k1[pl.ds(i, levels, stride=own), :]
+            message[distance - 1] = column(k1, i, own, levels)
             offset = 2 * GROUP * (distance - 1) + GROUP
-            rolled = turn(k1_strip[pl.ds(i, levels, stride=own), :], offset)
+            rolled = turn(column(k1_strip, i, own, levels), offset)
             packed = jnp.where(lane // (2 * GROUP) == distance - 1, rolled, packed)
         message[FAR] = packed
         i = jnp.where(side == 1, own - NEAR, NEAR - 1)
-        for k, name in enumerate(LATER):
-            message[FAR + 1 + k] = column(fields[name], i, own, levels)
+        for k, field in enumerate((fg, fd)):
+            message[FAR + 1 + k] = column(field, i, own, levels)
 
 
 def second_kernel(own, levels, columns, n_lat, k0, k1, k1_strip, from_a, from_b, g_main, g_strip, d_main, d_strip,
                   above, below, shift_sums, k2, k3, k4, out, shift_row, qa_main, qa_strip, qb_main, qb_strip, far):
-    lane = lanes_of(levels)
     lon_even, _, _ = parity(n_lat)
     qa, qb = (qa_main, qa_strip), (qb_main, qb_strip)
     g = (g_main, g_strip)
-    ext = Extended(columns, levels, (d_main, d_strip), g, above, below, lane, far)
+    ext = Extended(columns, levels, (d_main, d_strip), g, above, below, far)
     for ref in (*qa, *qb):
         clear_ends(ref, columns, levels)
     row = total_row(shift_sums)
     mixed, square = lane_value(row, 0), lane_value(row, 1)
     shift = jnp.where(mixed > 0.0, square / jnp.where(mixed > 0.0, mixed, 1.0), 1.0)
     shift_row[...] = jnp.broadcast_to(shift, shift_row.shape)
-    shift = jnp.broadcast_to(shift, (levels, LANES))
+    shift = jnp.broadcast_to(shift, (SUBLANES, LANES))
     for i in range(own):
         ext.put(qa, 0, FAR + i, column(k1, i, own, levels))
         ext.put(qa, 1, FAR + i, column(k1_strip, i, own, levels))
@@ -353,27 +388,29 @@
             ext.put(qa, 1, e, turn(block[FAR], -(2 * GROUP * (distance - 1) + GROUP)))
         for k in range(len(LATER)):
             far[k, east] = block[FAR + 1 + k]
-    source, target = qa, qb
-    for step, reach in ((0, FAR - 1), (1, FAR - 2)):
-        for e in range(FAR - reach, FAR + own + reach):
-            for k, (q, image) in enumerate(ext.stencil(source, e)):
-                value = ext.coefficient("g", k, e) * image - shift * q
-                ext.put(target, k, e, value)
-                if k == 0 and FAR <= e < FAR + own:
-                    (k2, k3)[step][pl.ds(e - FAR, levels, stride=own), :] = value
-        source, target = target, source
-    sums = [jnp.zeros((levels, LANES), jnp.float32) for _ in PAIRS]
-    for i in range(own):
-        e = FAR + i
-        ((q, image),) = ext.stencil(source, e, strips=False)
-        scale = ext.at(g, 0, e)
-        last = scale * image - shift * q
-        k4[pl.ds(i, levels, stride=own), :] = last
-        v = [column(k0, i, own, levels), column(k1, i, own, levels), column(k2, i, own, levels), q, last]
+    for rows, e, tiles in ext.sweep(qa, FAR - NEAR, FAR + own - 1 + NEAR):
+        for k, (q, image) in enumerate(tiles):
+            value = ext.coefficient("g", k, e, rows) * image - shift[: rows[1]] * q
+            ext.set(qb, k, e, rows, value)
+            if k == 0 and FAR <= e < FAR + own:
+                k2[own_rows(e - FAR, own, rows)] = value
+    for rows, e, tiles in ext.sweep(qb, FAR - 1, FAR + own):
+        for k, (q, image) in enumerate(tiles):
+            value = ext.at(g, k, e, rows) * image - shift[: rows[1]] * q
+            ext.set(qa, k, e, rows, value)
+            if k == 0 and FAR <= e < FAR + own:
+                k3[own_rows(e - FAR, own, rows)] = value
+    sums = [Sums() for _ in PAIRS]
+    for rows, e, ((q, image),) in ext.sweep(qa, FAR, FAR + own - 1, strips=False):
+        place = own_rows(e - FAR, own, rows)
+        scale = ext.at(g, 0, e, rows)
+        last = scale * image - shift[: rows[1]] * q
+        k4[place] = last
+        v = [k0[place], k1[place], k2[place], q, last]
         w = 1.0 / scale
         lead = [a * w for a in v]
-        for k, (a, b) in enumerate(PAIRS):
-            sums[k] = sums[k] + lead[a] * v[b]
+        for total, (a, b) in zip(sums, PAIRS):
+            total.add(lead[a] * v[b])
     put_row(out, sums)
 
 
@@ -410,14 +447,15 @@
     def real(*shape):
         return jax.ShapeDtypeStruct(shape, jnp.float32)
 
-    def call(kernel, ins, outs, scratch=(), specs=None, grant=32 * 1024 * 1024):
+    def call(kernel, ins, outs, scratch=(), specs=None, aliases=()):
         return pl.pallas_call(
             kernel,
             out_shape=tuple(outs) if len(outs) > 1 else outs[0],
             in_specs=specs or [VMEM] * len(ins),
             out_specs=tuple([VMEM] * len(outs)) if len(outs) > 1 else VMEM,
             scratch_shapes=[pltpu.VMEM(s, jnp.float32) if isinstance(s, tuple) else s for s in scratch],
-            compiler_params=pltpu.CompilerParams(vmem_limit_bytes=grant),
+            compiler_params=pltpu.CompilerParams(vmem_limit_bytes=32 * 1024 * 1024),
+            input_output_aliases=dict(aliases),
         )(*ins)
 
     def swap(value, name):
@@ -438,19 +476,32 @@
         [(levels * own, LANES)] * 4 + [(1, levels - 1), pltpu.SemaphoreType.DMA((5,))],
         [pl.BlockSpec(memory_space=pltpu.HBM)] * 5,
     )
-    lat_a, lat_b = swap(lat_a, "lat_even"), swap(lat_b, "lat_odd")
+    lat_a = swap(lat_a, "lat_even")
+    lat_b = swap(lat_b, "lat_odd")
     from_a = swap(to_a, "lon_even")
     from_b = swap(to_b, "lon_odd")
     corners_a, corners_b = call(
         functools.partial(corner_kernel, own, levels, n_lat), (lat_a, lat_b), [tile] * 2
     )
-    corners_a, corners_b = swap(corners_a, "lon_even"), swap(corners_b, "lon_odd")
-    k0, k1, k1_strip, to_a, to_b, *coefficients, shift_sums = call(
+    corners_a = swap(corners_a, "lon_even")
+    corners_b = swap(corners_b, "lon_odd")
+    buffers = call(
+        functools.partial(own_kernel, own, levels, columns, n_lat),
+        (*fields, lat_a, lat_b),
+        [real(*extended)] * 2 * len(FIELDS),
+    )
+    ins = (fields[1], fields[2], above, below, from_a, from_b, corners_a, corners_b, *buffers)
+    *buffers, k0, k1, k1_strip, to_a, to_b, shift_sums = call(
         functools.partial(first_kernel, own, levels, columns, n_lat),
-        (*fields, above, below, from_a, from_b, lat_a, lat_b, corners_a, corners_b),
-        [whole] * 3 + [real(FAR + 1 + len(LATER), levels, LANES)] * 2 + [real(*extended)] * 4 + [rows],
-        [extended] * 6,
+        ins,
+        [real(*extended)] * 2 * len(FIELDS)
+        + [whole] * 3
+        + [real(FAR + 1 + len(LATER), levels, LANES)] * 2
+        + [rows],
+        [extended] * 2,
+        aliases=[(len(ins) - 2 * len(FIELDS) + k, k) for k in range(2 * len(FIELDS))],
     )
+    coefficients = buffers[2:6]
     from_a = swap(to_a, "lon_even")
     from_b = swap(to_b, "lon_odd")
     shift_sums = everywhere(shift_sums)

time: 48.9 us -> 47.7 us (0.975)
  Pallas kernels: 6.18 us -> 5.19 us
    pallas_call x5 -> x6, Pallas kernels: 6.18 us -> 5.19 us  [call(): pl.pallas_call(kernel, out_shape=tuple(outs) if len(outs) > 1 else outs[0...]
  transfers between devices with their start and end apart: 8 -> 8, of which waited for: 3 -> 3; matrix products, arithmetic and copies ran while one was open for 0% -> 0% of each run, Pallas kernels for 0% -> 1%
where the time goes in v5:
time: 47.7 us; the launch traced here: 47.6 us
  blocking collectives  18.2 us (38%)
  starting transfers between devices  15.4 us (32%)
  waiting for transfers between devices  8.12 us (17%)
  Pallas kernels  5.19 us (11%)
  between operations  0.7 us (1%)
    all_to_all x2, blocking collectives, everywhere(): return lax.all_to_all(rows, AXES, 0, 0, tiled=True)  18.2 us
    ppermute x8, starting transfers between devices, swap(): return lax.ppermute(value, AXES, pairs[name])  15.4 us
    ppermute x8, waiting for transfers between devices, swap(): return lax.ppermute(value, AXES, pairs[name])  8.12 us
    pallas_call x6, Pallas kernels, call(): pl.pallas_call(kernel, out_shape=tuple(outs) if len(outs) > 1 else outs[0...  5.19 us
  transfers between devices with their start and end apart: 8, of which 3 were waited for; matrix products, arithmetic and copies ran while one was open for 0% of the time, Pallas kernels for 1%

profile of v5, /device:TPU:0, one launch (start us, length us, event | category | flops | bytes accessed | tf_op | source)
XLA Modules:
  0.0 47.6 jit_solution(13701022468511428467)
XLA Ops:
  0.6 1.8 %shard_map.68 = (f32[5,70,128]{2,1,0:T(8,128)S(1)}, f32[5,70,128]{2,1,0:T(8,128)S(1)}, f32[70,128]{1,0:T(8,128)S(1)}, f32[70,128]{1,0:T(8,128)S(1)}, f32[70,128]...) custom-call(f32[280,128]{1,0:T(8,128)} %bitcast.7, ...), custom_call_target="tpu_custom_call" | custom-call | tf_op jit(solution)/shard_map/pallas_call | solution.py:451
  2.4 3.0 %collective-permute-start = (f32[5,70,128]{2,1,0:T(8,128)S(1)}, f32[5,70,128]{2,1,0:T(8,128)S(1)}, u32[]{:S(2)}, u32[]{:S(2)}) collective-permute-start(f32[5,70,128]{2,1,0:T(8,128)S(1)} %get-tuple-element.43), channel_id=1, source_target_pairs={{0,4},{1,5},{2,6},{3,7},{4,0},{5,1},{6,2},{7,3},{8,12},{9,13},{10,... | collective-permute-start | bytes 537608 | tf_op jit(solution)/shard_map/ppermute | solution.py:462
  5.5 3.6 %collective-permute-start.1 = (f32[5,70,128]{2,1,0:T(8,128)S(1)}, f32[5,70,128]{2,1,0:T(8,128)S(1)}, u32[]{:S(2)}, u32[]{:S(2)}) collective-permute-start(f32[5,70,128]{2,1,0:T(8,128)S(1)} %get-tuple-element.44), channel_id=1, source_target_pairs={{0,28},{1,29},{2,30},{3,31},{4,8},{5,9},{6,10},{7,11},{8,4},{9,5},... | collective-permute-start | bytes 537608 | tf_op jit(solution)/shard_map/ppermute | solution.py:462
  9.0 0.0 collective-permute-start.2
  9.0 0.0 collective-permute-start.3
  9.0 1.2 %collective-permute-done.2.lat_a = f32[70,128]{1,0:T(8,128)S(1)} collective-permute-done((f32[70,128]{1,0:T(8,128)S(1)}, f32[70,128]{1,0:T(8,128)S(1)}, u32[]{:S(2)}, u32[]{:S(2)}) %collective-permute-start.2) | collective-permute-done | bytes 35872 | tf_op jit(solution)/shard_map/ppermute | solution.py:462
  10.3 4.0 %collective-permute-done.3.lat_b = f32[70,128]{1,0:T(8,128)S(1)} collective-permute-done((f32[70,128]{1,0:T(8,128)S(1)}, f32[70,128]{1,0:T(8,128)S(1)}, u32[]{:S(2)}, u32[]{:S(2)}) %collective-permute-start.3) | collective-permute-done | bytes 35872 | tf_op jit(solution)/shard_map/ppermute | solution.py:462
  14.3 0.1 shard_map.69
  14.4 1.4 %collective-permute-start.4 = (f32[70,128]{1,0:T(8,128)S(1)}, f32[70,128]{1,0:T(8,128)S(1)}, u32[]{:S(2)}, u32[]{:S(2)}) collective-permute-start(f32[70,128]{1,0:T(8,128)S(1)} %get-tuple-element.47), channel_id=1, source_target_pairs={{0,4},{1,5},{2,6},{3,7},{4,0},{5,1},{6,2},{7,3},{8,12},{9,13},{10,... | collective-permute-start | bytes 107528 | tf_op jit(solution)/shard_map/ppermute | solution.py:462
  15.8 3.6 %collective-permute-start.5 = (f32[70,128]{1,0:T(8,128)S(1)}, f32[70,128]{1,0:T(8,128)S(1)}, u32[]{:S(2)}, u32[]{:S(2)}) collective-permute-start(f32[70,128]{1,0:T(8,128)S(1)} %get-tuple-element.48), channel_id=1, source_target_pairs={{0,28},{1,29},{2,30},{3,31},{4,8},{5,9},{6,10},{7,11},{8,4},{9,5},... | collective-permute-start | bytes 107528 | tf_op jit(solution)/shard_map/ppermute | solution.py:462
  19.4 0.2 shard_map.70
  19.6 0.0 collective-permute-done.4.corners_a
  19.6 2.9 %collective-permute-done.5.corners_b = f32[70,128]{1,0:T(8,128)S(1)} collective-permute-done((f32[70,128]{1,0:T(8,128)S(1)}, f32[70,128]{1,0:T(8,128)S(1)}, u32[]{:S(2)}, u32[]{:S(2)}) %collective-permute-start.5) | collective-permute-done | bytes 35872 | tf_op jit(solution)/shard_map/ppermute | solution.py:462
  22.4 0.0 collective-permute-done.from_a
  22.4 0.0 collective-permute-done.1.from_b
  22.4 0.9 %shard_map.71 = (f32[720,128]{1,0:T(8,128)S(1)}, f32[720,128]{1,0:T(8,128)S(1)}, f32[720,128]{1,0:T(8,128)S(1)}, f32[720,128]{1,0:T(8,128)S(1)}, f32[720,128]{1,...) custom-call(f32[280,128]{1,0:T(8,128)S(1)} %get-tuple-element.39.fg,, ...), custom_call_target="tpu_custom_call", output_to_operand_aliasing={{0}: (8, {}), {1}: (9, {}), {2}: (10, {}), {3}: (11, {}), {... | custom-call | tf_op jit(solution)/shard_map/pallas_call | solution.py:451
  23.4 0.1 collective-permute-start.6
  23.4 3.7 %collective-permute-start.7 = (f32[6,70,128]{2,1,0:T(8,128)S(1)}, f32[6,70,128]{2,1,0:T(8,128)S(1)}, u32[]{:S(2)}, u32[]{:S(2)}) collective-permute-start(f32[6,70,128]{2,1,0:T(8,128)S(1)} %get-tuple-element.63), channel_id=1, source_target_pairs={{0,28},{1,29},{2,30},{3,31},{4,8},{5,9},{6,10},{7,11},{8,4},{9,5},... | collective-permute-start | bytes 645128 | tf_op jit(solution)/shard_map/ppermute | solution.py:462
  27.2 9.3 %all_to_all.10.shift_sums = f32[32,1,128]{2,1,0:T(1,128)S(1)} all-to-all(f32[32,1,128]{2,1,0:T(1,128)S(1)} %get-tuple-element.68), channel_id=1, replica_groups=mesh['lon'=8,'lat'=4] {'lon','lat'}, dimensions={0} | all-to-all | bytes 32768 | tf_op jit(solution)/shard_map/all_to_all | solution.py:465
  36.5 0.0 collective-permute-done.6.from_a
  36.5 0.0 collective-permute-done.7.from_b
  36.5 0.0 copy-start
  36.5 0.0 copy-start.1
  36.5 1.2 %shard_map.72 = (f32[280,128]{1,0:T(8,128)S(1)}, f32[280,128]{1,0:T(8,128)S(1)}, f32[280,128]{1,0:T(8,128)S(1)}, f32[32,1,128]{2,1,0:T(1,128)S(1)}, f32[1,128]{1,0:T(1,128)S(1)}) custom-call(f32[280,128]{1,0:T(8,128)S(1)} %get-tuple-element.59.k0, f32[280,128]{1,0:T(8,128)S(1)} %get-tuple-element.60.k1, f32[280,128]{1,0:T(8,128)S(1)} %get-tuple-element.61.k1_strip, ...), custom_call_target="tpu_custom_call" | custom-call | tf_op jit(solution)/shard_map/pallas_call | solution.py:451
  37.7 8.9 %all_to_all.11.sums = f32[32,1,128]{2,1,0:T(1,128)S(1)} all-to-all(f32[32,1,128]{2,1,0:T(1,128)S(1)} %get-tuple-element.69), channel_id=1, replica_groups=mesh['lon'=8,'lat'=4] {'lon','lat'}, dimensions={0} | all-to-all | bytes 32768 | tf_op jit(solution)/shard_map/all_to_all | solution.py:465
  46.6 0.0 copy-done
  46.6 0.0 copy-done.1
  46.6 1.0 %shard_map.73 = (f32[280,128]{1,0:T(8,128)}, f32[280,128]{1,0:T(8,128)}) custom-call(f32[32,1,128]{2,1,0:T(1,128)S(1)} %all_to_all.11.sums, f32[1,128]{1,0:T(1,128)S(1)} %get-tuple-element.70.shift_row, f32[280,128]{1,0:T(8,128)S(1)} %bitcast.8, f32[280,128]{1,0:T(8,128)S(1)} %bitcast.10, f32[280,128]{1,0:T(8,128)S(1)} %get-tuple-element.59.k0, ...), custom_call_target="tpu_custom_call" | custom-call | tf_op jit(solution)/shard_map/pallas_call | solution.py:451
Async XLA Ops:
  2.4 20.0 %collective-permute-start = (f32[5,70,128]{2,1,0:T(8,128)S(1)}, f32[5,70,128]{2,1,0:T(8,128)S(1)}, u32[]{:S(2)}, u32[]{:S(2)}) collective-permute-start(f32[5,70,128]{2,1,0:T(8,128)S(1)} %get-tuple-element.43), channel_id=1, source_target_pairs={{0,4},{1,5},{2,6},{3,7},{4,0},{5,1},{6,2},{7,3},{8,12},{9,13},{10,... | collective-permute-start | bytes 537608 | tf_op jit(solution)/shard_map/ppermute | solution.py:462
  5.5 17.0 %collective-permute-start.1 = (f32[5,70,128]{2,1,0:T(8,128)S(1)}, f32[5,70,128]{2,1,0:T(8,128)S(1)}, u32[]{:S(2)}, u32[]{:S(2)}) collective-permute-start(f32[5,70,128]{2,1,0:T(8,128)S(1)} %get-tuple-element.44), channel_id=1, source_target_pairs={{0,28},{1,29},{2,30},{3,31},{4,8},{5,9},{6,10},{7,11},{8,4},{9,5},... | collective-permute-start | bytes 537608 | tf_op jit(solution)/shard_map/ppermute | solution.py:462
  9.0 1.2 %collective-permute-start.2 = (f32[70,128]{1,0:T(8,128)S(1)}, f32[70,128]{1,0:T(8,128)S(1)}, u32[]{:S(2)}, u32[]{:S(2)}) collective-permute-start(f32[70,128]{1,0:T(8,128)S(1)} %get-tuple-element.45), channel_id=1, source_target_pairs={{0,1},{1,0},{2,3},{3,2},{4,5},{5,4},{6,7},{7,6},{8,9},{9,8},{10,11... | collective-permute-start | bytes 107528 | tf_op jit(solution)/shard_map/ppermute | solution.py:462
  9.0 5.3 %collective-permute-start.3 = (f32[70,128]{1,0:T(8,128)S(1)}, f32[70,128]{1,0:T(8,128)S(1)}, u32[]{:S(2)}, u32[]{:S(2)}) collective-permute-start(f32[70,128]{1,0:T(8,128)S(1)} %get-tuple-element.46), channel_id=1, source_target_pairs={{0,16},{1,2},{2,1},{3,19},{4,20},{5,6},{6,5},{7,23},{8,24},{9,10},... | collective-permute-start | bytes 107528 | tf_op jit(solution)/shard_map/ppermute | solution.py:462
  14.4 5.2 %collective-permute-start.4 = (f32[70,128]{1,0:T(8,128)S(1)}, f32[70,128]{1,0:T(8,128)S(1)}, u32[]{:S(2)}, u32[]{:S(2)}) collective-permute-start(f32[70,128]{1,0:T(8,128)S(1)} %get-tuple-element.47), channel_id=1, source_target_pairs={{0,4},{1,5},{2,6},{3,7},{4,0},{5,1},{6,2},{7,3},{8,12},{9,13},{10,... | collective-permute-start | bytes 107528 | tf_op jit(solution)/shard_map/ppermute | solution.py:462
  15.8 6.7 %collective-permute-start.5 = (f32[70,128]{1,0:T(8,128)S(1)}, f32[70,128]{1,0:T(8,128)S(1)}, u32[]{:S(2)}, u32[]{:S(2)}) collective-permute-start(f32[70,128]{1,0:T(8,128)S(1)} %get-tuple-element.48), channel_id=1, source_target_pairs={{0,28},{1,29},{2,30},{3,31},{4,8},{5,9},{6,10},{7,11},{8,4},{9,5},... | collective-permute-start | bytes 107528 | tf_op jit(solution)/shard_map/ppermute | solution.py:462
  23.4 13.1 %collective-permute-start.6 = (f32[6,70,128]{2,1,0:T(8,128)S(1)}, f32[6,70,128]{2,1,0:T(8,128)S(1)}, u32[]{:S(2)}, u32[]{:S(2)}) collective-permute-start(f32[6,70,128]{2,1,0:T(8,128)S(1)} %get-tuple-element.62), channel_id=1, source_target_pairs={{0,4},{1,5},{2,6},{3,7},{4,0},{5,1},{6,2},{7,3},{8,12},{9,13},{10,... | collective-permute-start | bytes 645128 | tf_op jit(solution)/shard_map/ppermute | solution.py:462
  23.4 13.0 %collective-permute-start.7 = (f32[6,70,128]{2,1,0:T(8,128)S(1)}, f32[6,70,128]{2,1,0:T(8,128)S(1)}, u32[]{:S(2)}, u32[]{:S(2)}) collective-permute-start(f32[6,70,128]{2,1,0:T(8,128)S(1)} %get-tuple-element.63), channel_id=1, source_target_pairs={{0,28},{1,29},{2,30},{3,31},{4,8},{5,9},{6,10},{7,11},{8,4},{9,5},... | collective-permute-start | bytes 645128 | tf_op jit(solution)/shard_map/ppermute | solution.py:462
  36.5 10.1 %copy-start = (f32[70,4,128]{2,1,0:T(4,128)S(1)}, f32[70,4,128]{2,1,0:T(4,128)}, u32[]{:S(2)}) copy-start(f32[70,4,128]{2,1,0:T(4,128)} %param.6) | copy-start | bytes 430084
  36.5 10.1 %copy-start.1 = (f32[70,4,128]{2,1,0:T(4,128)S(1)}, f32[70,4,128]{2,1,0:T(4,128)}, u32[]{:S(2)}) copy-start(f32[70,4,128]{2,1,0:T(4,128)} %param.7) | copy-start | bytes 430084

commit v6 on v5

--- a/solution.py
+++ b/solution.py
@@ -15,8 +15,9 @@
 NEAR, FAR = 2, 3
 GROUP = 8
 VMEM = pl.BlockSpec(memory_space=pltpu.VMEM)
-FIRST = (("q", 1), ("q", 2), ("g", 1), ("d", 1), ("s", 1))
-LATER = ("g", "d")
+FIRST = ("q", "s", "g")
+STRIPS = (("q", 1), ("q", 2), ("g", 1), ("d", 1), ("s", 1))
+SECOND = 5
 FIELDS = ("q", "g", "d", "s")
 
 
@@ -148,7 +149,7 @@
 
 
 def pack_kernel(own, levels, n_lat, x_hbm, b_hbm, c_hbm, h_hbm, coupling_hbm, to_a, to_b, lat_a, lat_b, above,
-                below, fq, fg, fd, fs, x, b, c, h, coupling, sem):
+                below, fq, fg, fd, fs, x, b, c, h, coupling, q_ref, partial, sem):
     copies = []
     moves = ((coupling_hbm, coupling), (x_hbm, x), (c_hbm, c), (h_hbm, h), (b_hbm, b))
     for k, (source, target) in enumerate(moves):
@@ -181,6 +182,8 @@
         )
         for f, name in enumerate(FIELDS):
             store[name][pl.ds(i, levels, stride=own), :] = values[name]
+            if name == "q":
+                plane(q_ref, i, own, levels)[...] = values[name]
             slot = f * own + i
             rolled = turn(values[name], GROUP * slot)
             north = jnp.where(group == slot, rolled, north)
@@ -194,11 +197,20 @@
         mirror = jnp.where((lane & bit) != 0, turn(mirror, bit), turn(mirror, -bit))
     mirror = jnp.where(even, turn(mirror, -GROUP), turn(mirror, GROUP))
     lat_b[...] = jnp.where(over, mirror, other)
-    for k, (name, distance) in enumerate(FIRST):
-        east, west = own - distance, distance - 1
-        a = jnp.where(lon_even == 1, east, west)
-        to_a[k] = store[name][pl.ds(a, levels, stride=own), :]
-        to_b[k] = store[name][pl.ds(east + west - a, levels, stride=own), :]
+    clear_ends(q_ref, own, levels)
+    for k, (i, inner) in enumerate(((0, 1), (own - 1, own - 2))):
+        q = plane(q_ref, i, own, levels)[...]
+        near = jnp.where(lane == LANES - 1, 0.0, turn(q, -1)) + jnp.where(lane == 0, 0.0, turn(q, 1))
+        near = near + plane(q_ref, inner, own, levels)[...]
+        near = near + below[...] * plane(q_ref, i, own, levels, 1)[...]
+        near = near + above[...] * plane(q_ref, i, own, levels, -1)[...]
+        image = column(fd, i, own, levels) * q - near
+        partial[k] = column(fs, i, own, levels) - column(fg, i, own, levels) * image
+    for message, side in ((to_a, lon_even), (to_b, 1 - lon_even)):
+        i = jnp.where(side == 1, own - 1, 0)
+        message[0] = column(fq, i, own, levels)
+        message[1] = partial[side]
+        message[2] = column(fg, i, own, levels)
 
 
 def corner_kernel(own, levels, n_lat, lat_a, lat_b, to_a, to_b):
@@ -250,12 +262,12 @@
     def put(self, pair, k, e, value):
         self.set(pair, k, e, (0, self.levels), value)
 
-    def coefficient(self, name, k, e, rows):
-        edges = (FAR - NEAR, self.columns - 1 - FAR + NEAR)
+    def diagonal(self, k, e, rows):
+        edges = (FAR - 1, self.columns - FAR)
         if self.far is not None and k == 0 and e in edges:
             start, count = rows
-            return self.far[LATER.index(name), edges.index(e), start : start + count, :]
-        return self.at(self.g if name == "g" else self.d, k, e, rows)
+            return self.far[edges.index(e), start : start + count, :]
+        return self.at(self.d, k, e, rows)
 
     def sweep(self, pair, first, last, strips=True):
         for start in range(0, self.levels, SUBLANES):
@@ -276,7 +288,7 @@
                     q = middle(k, e)
                     side = middle(k, e - 1) + middle(k, e + 1)
                     levels = below * self.at(pair, k, e, rows, 1) + above * self.at(pair, k, e, rows, -1)
-                    out.append((q, self.coefficient("d", k, e, rows) * q - (side + near[k]) - levels))
+                    out.append((q, self.diagonal(k, e, rows) * q - (side + near[k]) - levels))
                 yield rows, e, out
 
 
@@ -315,7 +327,7 @@
             plane(strip, FAR + i, columns, levels)[...] = edges
 
 
-def first_kernel(own, levels, columns, n_lat, fg, fd, above, below, from_a, from_b, corners_a, corners_b, *refs):
+def first_kernel(own, levels, columns, n_lat, fd, above, below, from_a, from_b, corners_a, corners_b, *refs):
     extended = refs[8:16]
     k0, k1, k1_strip, to_a, to_b, out, qb_main, qb_strip = refs[16:]
     lane = lanes_of(levels)
@@ -328,16 +340,24 @@
         clear_ends(ref, columns, levels)
     for block, corner, east in ((from_a, corners_a, lon_even), (from_b, corners_b, 1 - lon_even)):
         tile = corner[...]
-        for k, (name, distance) in enumerate(FIRST + tuple((name, NEAR) for name in LATER)):
+        for k, name in enumerate(FIRST):
+            ext.put(pairs[name], 0, jnp.where(east == 1, FAR + own, FAR - 1), block[k])
+        for name, distance in STRIPS:
             e = jnp.where(east == 1, FAR + own - 1 + distance, FAR - distance)
-            if k < len(FIRST):
-                ext.put(pairs[name], 0, e, block[k])
             slot = FIELDS.index(name) * own + jnp.where(east == 1, distance - 1, own - distance)
             south = lax.rem(2 * LANES - GROUP * slot, LANES)
             north = lax.rem(south + LANES - GROUP * jnp.where(east == 1, 1 + NEAR, 1 - NEAR), LANES)
             ext.put(pairs[name], 1, e, jnp.where(low, pltpu.roll(tile, south, 1), pltpu.roll(tile, north, 1)))
+    edges = {FAR - 1: FAR, FAR + own: FAR + own - 1}
     for rows, e, tiles in ext.sweep(qa, FAR - 1, FAR + own):
         for k, (_, image) in enumerate(tiles):
+            if k == 0 and e in edges:
+                edge, strip = ext.at(qa, 0, edges[e], rows), ext.at(qa, 1, e, rows)
+                place = lanes_of(rows[1])
+                beyond = jnp.where(place == LANES - 1, turn(strip, -1), 0.0) + jnp.where(
+                    place == 0, turn(strip, 1), 0.0
+                )
+                image = -(edge + beyond)
             value = ext.at(pairs["s"], k, e, rows) - ext.at(pairs["g"], k, e, rows) * image
             ext.set(qb, k, e, rows, value)
             if k == 0 and FAR <= e < FAR + own:
@@ -347,22 +367,29 @@
         for k, (q, image) in enumerate(tiles):
             value = ext.at(pairs["g"], k, e, rows) * image
             (k1, k1_strip)[k][own_rows(e - FAR, own, rows)] = value
+            ext.set(qa, k, e, rows, value)
             if k == 0:
                 mixed.add(q * image)
                 square.add(value * image)
     put_row(out, (mixed, square))
+    for rows, e, tiles in ext.sweep(qa, FAR + NEAR - 1, FAR + own - NEAR):
+        for k, (_, image) in enumerate(tiles):
+            ext.set(qb, k, e, rows, ext.at(pairs["g"], k, e, rows) * image)
     for message, side in ((to_a, lon_even), (to_b, 1 - lon_even)):
+        near, next_one = (jnp.where(side == 1, own - d, d - 1) for d in (1, NEAR))
         packed = jnp.zeros((levels, LANES), jnp.float32)
-        for distance in range(1, FAR + 1):
-            i = jnp.where(side == 1, own - distance, distance - 1)
-            message[distance - 1] = column(k1, i, own, levels)
-            offset = 2 * GROUP * (distance - 1) + GROUP
-            rolled = turn(column(k1_strip, i, own, levels), offset)
-            packed = jnp.where(lane // (2 * GROUP) == distance - 1, rolled, packed)
-        message[FAR] = packed
-        i = jnp.where(side == 1, own - NEAR, NEAR - 1)
-        for k, field in enumerate((fg, fd)):
-            message[FAR + 1 + k] = column(field, i, own, levels)
+        for k, (main, strip) in enumerate(
+            (
+                (column(k1, near, own, levels), column(k1_strip, near, own, levels)),
+                (column(k1, next_one, own, levels), column(k1_strip, next_one, own, levels)),
+                [plane(ref, FAR + next_one, columns, levels)[...] for ref in qb],
+            )
+        ):
+            message[k] = main
+            rolled = turn(strip, 2 * GROUP * k + GROUP)
+            packed = jnp.where(lane // (2 * GROUP) == k, rolled, packed)
+        message[SECOND - 2] = packed
+        message[SECOND - 1] = column(fd, near, own, levels)
 
 
 def second_kernel(own, levels, columns, n_lat, k0, k1, k1_strip, from_a, from_b, g_main, g_strip, d_main, d_strip,
@@ -377,20 +404,23 @@
     mixed, square = lane_value(row, 0), lane_value(row, 1)
     shift = jnp.where(mixed > 0.0, square / jnp.where(mixed > 0.0, mixed, 1.0), 1.0)
     shift_row[...] = jnp.broadcast_to(shift, shift_row.shape)
-    shift = jnp.broadcast_to(shift, (SUBLANES, LANES))
+    shift = jnp.broadcast_to(shift, (levels, LANES))
     for i in range(own):
         ext.put(qa, 0, FAR + i, column(k1, i, own, levels))
         ext.put(qa, 1, FAR + i, column(k1_strip, i, own, levels))
     for block, east in ((from_a, lon_even), (from_b, 1 - lon_even)):
-        for distance in range(1, FAR + 1):
-            e = jnp.where(east == 1, FAR + own - 1 + distance, FAR - distance)
-            ext.put(qa, 0, e, block[distance - 1])
-            ext.put(qa, 1, e, turn(block[FAR], -(2 * GROUP * (distance - 1) + GROUP)))
-        for k in range(len(LATER)):
-            far[k, east] = block[FAR + 1 + k]
-    for rows, e, tiles in ext.sweep(qa, FAR - NEAR, FAR + own - 1 + NEAR):
+        strips = [turn(block[SECOND - 2], -(2 * GROUP * k + GROUP)) for k in range(3)]
+        near, next_one = (jnp.where(east == 1, FAR + own - 1 + d, FAR - d) for d in (1, NEAR))
+        for k in range(2):
+            first, other, image = ((block[d], strips[d])[k] for d in range(3))
+            ext.put(qa, k, near, first)
+            ext.put(qa, k, next_one, other)
+            ext.put(qb, k, next_one, image - shift * other)
+        far[east] = block[SECOND - 1]
+    shift = shift[:SUBLANES]
+    for rows, e, tiles in ext.sweep(qa, FAR - 1, FAR + own):
         for k, (q, image) in enumerate(tiles):
-            value = ext.coefficient("g", k, e, rows) * image - shift[: rows[1]] * q
+            value = ext.at(g, k, e, rows) * image - shift[: rows[1]] * q
             ext.set(qb, k, e, rows, value)
             if k == 0 and FAR <= e < FAR + own:
                 k2[own_rows(e - FAR, own, rows)] = value
@@ -473,7 +503,8 @@
         functools.partial(pack_kernel, own, levels, n_lat),
         tuple(pltpu.with_memory_space_constraint(v, pltpu.HBM) for v in (x, b, c, h, coupling)),
         [real(len(FIRST), levels, LANES)] * 2 + [tile] * 4 + [whole] * len(FIELDS),
-        [(levels * own, LANES)] * 4 + [(1, levels - 1), pltpu.SemaphoreType.DMA((5,))],
+        [(levels * own, LANES)] * 4
+        + [(1, levels - 1), ((levels + 2) * own, LANES), (2, levels, LANES), pltpu.SemaphoreType.DMA((5,))],
         [pl.BlockSpec(memory_space=pltpu.HBM)] * 5,
     )
     lat_a = swap(lat_a, "lat_even")
@@ -490,13 +521,13 @@
         (*fields, lat_a, lat_b),
         [real(*extended)] * 2 * len(FIELDS),
     )
-    ins = (fields[1], fields[2], above, below, from_a, from_b, corners_a, corners_b, *buffers)
+    ins = (fields[2], above, below, from_a, from_b, corners_a, corners_b, *buffers)
     *buffers, k0, k1, k1_strip, to_a, to_b, shift_sums = call(
         functools.partial(first_kernel, own, levels, columns, n_lat),
         ins,
         [real(*extended)] * 2 * len(FIELDS)
         + [whole] * 3
-        + [real(FAR + 1 + len(LATER), levels, LANES)] * 2
+        + [real(SECOND, levels, LANES)] * 2
         + [rows],
         [extended] * 2,
         aliases=[(len(ins) - 2 * len(FIELDS) + k, k) for k in range(2 * len(FIELDS))],
@@ -509,7 +540,7 @@
         functools.partial(second_kernel, own, levels, columns, n_lat),
         (k0, k1, k1_strip, from_a, from_b, *coefficients, above, below, shift_sums),
         [whole] * 3 + [rows, real(1, LANES)],
-        [extended] * 4 + [(len(LATER), 2, levels, LANES)],
+        [extended] * 4 + [(2, levels, LANES)],
     )
     sums = everywhere(sums)
     out, rest = call(final_kernel, (sums, shift, x, c, k0, k1, k2, k3, k4), [whole] * 2)

time: 47.7 us -> 45.9 us (0.962)
  starting transfers between devices: 15.4 us -> 14.2 us
    ppermute x8, starting transfers between devices: 15.4 us -> 14.2 us  [swap(): return lax.ppermute(value, AXES, pairs[name])]
where the time goes in v6:
time: 45.9 us; the launch traced here: 45.7 us
  blocking collectives  18.2 us (40%)
  starting transfers between devices  14.2 us (31%)
  waiting for transfers between devices  7.68 us (17%)
  Pallas kernels  5.03 us (11%)
  between operations  0.69 us (2%)
    all_to_all x2, blocking collectives, everywhere(): return lax.all_to_all(rows, AXES, 0, 0, tiled=True)  18.2 us
    ppermute x8, starting transfers between devices, swap(): return lax.ppermute(value, AXES, pairs[name])  14.2 us
    ppermute x8, waiting for transfers between devices, swap(): return lax.ppermute(value, AXES, pairs[name])  7.68 us
    pallas_call x6, Pallas kernels, call(): pl.pallas_call(kernel, out_shape=tuple(outs) if len(outs) > 1 else outs[0...  5.03 us
  transfers between devices with their start and end apart: 8, of which 3 were waited for; matrix products, arithmetic and copies ran while one was open for 0% of the time, Pallas kernels for 1%

profile of v6, /device:TPU:0, one launch (start us, length us, event | category | flops | bytes accessed | tf_op | source)
XLA Modules:
  0.0 45.7 jit_solution(18250030856428163059)
XLA Ops:
  0.6 1.8 %shard_map.68 = (f32[3,70,128]{2,1,0:T(8,128)S(1)}, f32[3,70,128]{2,1,0:T(8,128)S(1)}, f32[70,128]{1,0:T(8,128)S(1)}, f32[70,128]{1,0:T(8,128)S(1)}, f32[70,128]...) custom-call(f32[280,128]{1,0:T(8,128)} %bitcast.7, ...), custom_call_target="tpu_custom_call" | custom-call | tf_op jit(solution)/shard_map/pallas_call | solution.py:481
  2.4 3.0 %collective-permute-start = (f32[3,70,128]{2,1,0:T(8,128)S(1)}, f32[3,70,128]{2,1,0:T(8,128)S(1)}, u32[]{:S(2)}, u32[]{:S(2)}) collective-permute-start(f32[3,70,128]{2,1,0:T(8,128)S(1)} %get-tuple-element.42), channel_id=1, source_target_pairs={{0,4},{1,5},{2,6},{3,7},{4,0},{5,1},{6,2},{7,3},{8,12},{9,13},{10,... | collective-permute-start | bytes 322568 | tf_op jit(solution)/shard_map/ppermute | solution.py:492
  5.4 3.6 %collective-permute-start.1 = (f32[3,70,128]{2,1,0:T(8,128)S(1)}, f32[3,70,128]{2,1,0:T(8,128)S(1)}, u32[]{:S(2)}, u32[]{:S(2)}) collective-permute-start(f32[3,70,128]{2,1,0:T(8,128)S(1)} %get-tuple-element.43), channel_id=1, source_target_pairs={{0,28},{1,29},{2,30},{3,31},{4,8},{5,9},{6,10},{7,11},{8,4},{9,5},... | collective-permute-start | bytes 322568 | tf_op jit(solution)/shard_map/ppermute | solution.py:492
  9.0 0.0 collective-permute-start.2
  9.0 0.0 collective-permute-start.3
  9.0 1.2 %collective-permute-done.2.lat_a = f32[70,128]{1,0:T(8,128)S(1)} collective-permute-done((f32[70,128]{1,0:T(8,128)S(1)}, f32[70,128]{1,0:T(8,128)S(1)}, u32[]{:S(2)}, u32[]{:S(2)}) %collective-permute-start.2) | collective-permute-done | bytes 35872 | tf_op jit(solution)/shard_map/ppermute | solution.py:492
  10.2 3.6 %collective-permute-done.3.lat_b = f32[70,128]{1,0:T(8,128)S(1)} collective-permute-done((f32[70,128]{1,0:T(8,128)S(1)}, f32[70,128]{1,0:T(8,128)S(1)}, u32[]{:S(2)}, u32[]{:S(2)}) %collective-permute-start.3) | collective-permute-done | bytes 35872 | tf_op jit(solution)/shard_map/ppermute | solution.py:492
  13.9 0.1 shard_map.69
  14.0 0.1 collective-permute-start.4
  14.0 3.7 %collective-permute-start.5 = (f32[70,128]{1,0:T(8,128)S(1)}, f32[70,128]{1,0:T(8,128)S(1)}, u32[]{:S(2)}, u32[]{:S(2)}) collective-permute-start(f32[70,128]{1,0:T(8,128)S(1)} %get-tuple-element.47), channel_id=1, source_target_pairs={{0,28},{1,29},{2,30},{3,31},{4,8},{5,9},{6,10},{7,11},{8,4},{9,5},... | collective-permute-start | bytes 107528 | tf_op jit(solution)/shard_map/ppermute | solution.py:492
  17.7 0.2 shard_map.70
  18.0 0.0 collective-permute-done.4.corners_a
  18.0 2.8 %collective-permute-done.5.corners_b = f32[70,128]{1,0:T(8,128)S(1)} collective-permute-done((f32[70,128]{1,0:T(8,128)S(1)}, f32[70,128]{1,0:T(8,128)S(1)}, u32[]{:S(2)}, u32[]{:S(2)}) %collective-permute-start.5) | collective-permute-done | bytes 35872 | tf_op jit(solution)/shard_map/ppermute | solution.py:492
  20.8 0.0 collective-permute-done.from_a
  20.8 0.0 collective-permute-done.1.from_b
  20.8 1.0 %shard_map.71 = (f32[720,128]{1,0:T(8,128)S(1)}, f32[720,128]{1,0:T(8,128)S(1)}, f32[720,128]{1,0:T(8,128)S(1)}, f32[720,128]{1,0:T(8,128)S(1)}, f32[720,128]{1,...) custom-call(f32[280,128]{1,0:T(8,128)S(1)} %get-tuple-element.39.fd,, ...), custom_call_target="tpu_custom_call", output_to_operand_aliasing={{0}: (7, {}), {1}: (8, {}), {2}: (9, {}), {3}: (10, {}), {4... | custom-call | tf_op jit(solution)/shard_map/pallas_call | solution.py:481
  21.8 0.2 collective-permute-start.6
  22.0 3.6 %collective-permute-start.7 = (f32[5,70,128]{2,1,0:T(8,128)S(1)}, f32[5,70,128]{2,1,0:T(8,128)S(1)}, u32[]{:S(2)}, u32[]{:S(2)}) collective-permute-start(f32[5,70,128]{2,1,0:T(8,128)S(1)} %get-tuple-element.63), channel_id=1, source_target_pairs={{0,28},{1,29},{2,30},{3,31},{4,8},{5,9},{6,10},{7,11},{8,4},{9,5},... | collective-permute-start | bytes 537608 | tf_op jit(solution)/shard_map/ppermute | solution.py:492
  25.5 9.3 %all_to_all.10.shift_sums = f32[32,1,128]{2,1,0:T(1,128)S(1)} all-to-all(f32[32,1,128]{2,1,0:T(1,128)S(1)} %get-tuple-element.68), channel_id=1, replica_groups=mesh['lon'=8,'lat'=4] {'lon','lat'}, dimensions={0} | all-to-all | bytes 32768 | tf_op jit(solution)/shard_map/all_to_all | solution.py:495
  34.8 0.0 collective-permute-done.6.from_a
  34.8 0.0 collective-permute-done.7.from_b
  34.8 0.0 copy-start
  34.8 0.0 copy-start.1
  34.9 1.0 %shard_map.72 = (f32[280,128]{1,0:T(8,128)S(1)}, f32[280,128]{1,0:T(8,128)S(1)}, f32[280,128]{1,0:T(8,128)S(1)}, f32[32,1,128]{2,1,0:T(1,128)S(1)}, f32[1,128]{1,0:T(1,128)S(1)}) custom-call(f32[280,128]{1,0:T(8,128)S(1)} %get-tuple-element.59.k0, f32[280,128]{1,0:T(8,128)S(1)} %get-tuple-element.60.k1, f32[280,128]{1,0:T(8,128)S(1)} %get-tuple-element.61.k1_strip, ...), custom_call_target="tpu_custom_call" | custom-call | tf_op jit(solution)/shard_map/pallas_call | solution.py:481
  35.9 8.9 %all_to_all.11.sums = f32[32,1,128]{2,1,0:T(1,128)S(1)} all-to-all(f32[32,1,128]{2,1,0:T(1,128)S(1)} %get-tuple-element.69), channel_id=1, replica_groups=mesh['lon'=8,'lat'=4] {'lon','lat'}, dimensions={0} | all-to-all | bytes 32768 | tf_op jit(solution)/shard_map/all_to_all | solution.py:495
  44.7 0.0 copy-done
  44.7 0.0 copy-done.1
  44.7 1.0 %shard_map.73 = (f32[280,128]{1,0:T(8,128)}, f32[280,128]{1,0:T(8,128)}) custom-call(f32[32,1,128]{2,1,0:T(1,128)S(1)} %all_to_all.11.sums, f32[1,128]{1,0:T(1,128)S(1)} %get-tuple-element.70.shift_row, f32[280,128]{1,0:T(8,128)S(1)} %bitcast.8, f32[280,128]{1,0:T(8,128)S(1)} %bitcast.10, f32[280,128]{1,0:T(8,128)S(1)} %get-tuple-element.59.k0, ...), custom_call_target="tpu_custom_call" | custom-call | tf_op jit(solution)/shard_map/pallas_call | solution.py:481
Async XLA Ops:
  2.4 18.4 %collective-permute-start = (f32[3,70,128]{2,1,0:T(8,128)S(1)}, f32[3,70,128]{2,1,0:T(8,128)S(1)}, u32[]{:S(2)}, u32[]{:S(2)}) collective-permute-start(f32[3,70,128]{2,1,0:T(8,128)S(1)} %get-tuple-element.42), channel_id=1, source_target_pairs={{0,4},{1,5},{2,6},{3,7},{4,0},{5,1},{6,2},{7,3},{8,12},{9,13},{10,... | collective-permute-start | bytes 322568 | tf_op jit(solution)/shard_map/ppermute | solution.py:492
  5.4 15.3 %collective-permute-start.1 = (f32[3,70,128]{2,1,0:T(8,128)S(1)}, f32[3,70,128]{2,1,0:T(8,128)S(1)}, u32[]{:S(2)}, u32[]{:S(2)}) collective-permute-start(f32[3,70,128]{2,1,0:T(8,128)S(1)} %get-tuple-element.43), channel_id=1, source_target_pairs={{0,28},{1,29},{2,30},{3,31},{4,8},{5,9},{6,10},{7,11},{8,4},{9,5},... | collective-permute-start | bytes 322568 | tf_op jit(solution)/shard_map/ppermute | solution.py:492
  9.0 1.2 %collective-permute-start.2 = (f32[70,128]{1,0:T(8,128)S(1)}, f32[70,128]{1,0:T(8,128)S(1)}, u32[]{:S(2)}, u32[]{:S(2)}) collective-permute-start(f32[70,128]{1,0:T(8,128)S(1)} %get-tuple-element.44), channel_id=1, source_target_pairs={{0,1},{1,0},{2,3},{3,2},{4,5},{5,4},{6,7},{7,6},{8,9},{9,8},{10,11... | collective-permute-start | bytes 107528 | tf_op jit(solution)/shard_map/ppermute | solution.py:492
  9.0 4.9 %collective-permute-start.3 = (f32[70,128]{1,0:T(8,128)S(1)}, f32[70,128]{1,0:T(8,128)S(1)}, u32[]{:S(2)}, u32[]{:S(2)}) collective-permute-start(f32[70,128]{1,0:T(8,128)S(1)} %get-tuple-element.45), channel_id=1, source_target_pairs={{0,16},{1,2},{2,1},{3,19},{4,20},{5,6},{6,5},{7,23},{8,24},{9,10},... | collective-permute-start | bytes 107528 | tf_op jit(solution)/shard_map/ppermute | solution.py:492
  14.0 4.0 %collective-permute-start.4 = (f32[70,128]{1,0:T(8,128)S(1)}, f32[70,128]{1,0:T(8,128)S(1)}, u32[]{:S(2)}, u32[]{:S(2)}) collective-permute-start(f32[70,128]{1,0:T(8,128)S(1)} %get-tuple-element.46), channel_id=1, source_target_pairs={{0,4},{1,5},{2,6},{3,7},{4,0},{5,1},{6,2},{7,3},{8,12},{9,13},{10,... | collective-permute-start | bytes 107528 | tf_op jit(solution)/shard_map/ppermute | solution.py:492
  14.0 6.7 %collective-permute-start.5 = (f32[70,128]{1,0:T(8,128)S(1)}, f32[70,128]{1,0:T(8,128)S(1)}, u32[]{:S(2)}, u32[]{:S(2)}) collective-permute-start(f32[70,128]{1,0:T(8,128)S(1)} %get-tuple-element.47), channel_id=1, source_target_pairs={{0,28},{1,29},{2,30},{3,31},{4,8},{5,9},{6,10},{7,11},{8,4},{9,5},... | collective-permute-start | bytes 107528 | tf_op jit(solution)/shard_map/ppermute | solution.py:492
  21.8 13.1 %collective-permute-start.6 = (f32[5,70,128]{2,1,0:T(8,128)S(1)}, f32[5,70,128]{2,1,0:T(8,128)S(1)}, u32[]{:S(2)}, u32[]{:S(2)}) collective-permute-start(f32[5,70,128]{2,1,0:T(8,128)S(1)} %get-tuple-element.62), channel_id=1, source_target_pairs={{0,4},{1,5},{2,6},{3,7},{4,0},{5,1},{6,2},{7,3},{8,12},{9,13},{10,... | collective-permute-start | bytes 537608 | tf_op jit(solution)/shard_map/ppermute | solution.py:492
  22.0 12.9 %collective-permute-start.7 = (f32[5,70,128]{2,1,0:T(8,128)S(1)}, f32[5,70,128]{2,1,0:T(8,128)S(1)}, u32[]{:S(2)}, u32[]{:S(2)}) collective-permute-start(f32[5,70,128]{2,1,0:T(8,128)S(1)} %get-tuple-element.63), channel_id=1, source_target_pairs={{0,28},{1,29},{2,30},{3,31},{4,8},{5,9},{6,10},{7,11},{8,4},{9,5},... | collective-permute-start | bytes 537608 | tf_op jit(solution)/shard_map/ppermute | solution.py:492
  34.8 9.9 %copy-start = (f32[70,4,128]{2,1,0:T(4,128)S(1)}, f32[70,4,128]{2,1,0:T(4,128)}, u32[]{:S(2)}) copy-start(f32[70,4,128]{2,1,0:T(4,128)} %param.6) | copy-start | bytes 430084
  34.8 9.9 %copy-start.1 = (f32[70,4,128]{2,1,0:T(4,128)S(1)}, f32[70,4,128]{2,1,0:T(4,128)}, u32[]{:S(2)}) copy-start(f32[70,4,128]{2,1,0:T(4,128)} %param.7) | copy-start | bytes 430084

commit v7 on v6

--- a/solution.py
+++ b/solution.py
@@ -156,7 +156,6 @@
         copies.append(pltpu.make_async_copy(source, target, sem.at[k]))
         copies[-1].start()
     lane = lanes_of(levels)
-    group = lane // GROUP
     groups = LANES // GROUP
     lon_even, lat_even, pole = parity(n_lat)
     store = dict(zip(FIELDS, (fq, fg, fd, fs)))
@@ -167,36 +166,35 @@
     for out, k in ((below, row), (above, row - 1)):
         value = jnp.sum(jnp.where(interface == k, strength, 0.0), axis=1, keepdims=True)
         out[...] = jnp.broadcast_to(value, (levels, LANES))
-    north = jnp.zeros((levels, LANES), jnp.float32)
-    south = north
     for copy in copies[1:]:
         copy.wait()
-    for i in range(own):
-        values = transformed(
-            column(x, i, own, levels),
-            column(b, i, own, levels),
-            column(c, i, own, levels),
-            column(h, i, own, levels),
-            above[...],
-            below[...],
-        )
-        for f, name in enumerate(FIELDS):
-            store[name][pl.ds(i, levels, stride=own), :] = values[name]
-            if name == "q":
-                plane(q_ref, i, own, levels)[...] = values[name]
-            slot = f * own + i
-            rolled = turn(values[name], GROUP * slot)
-            north = jnp.where(group == slot, rolled, north)
-            south = jnp.where(group == (slot - 1) % groups, rolled, south)
-    even = jnp.full((levels, LANES), lat_even, jnp.int32) == 1
-    over = jnp.full((levels, LANES), pole.astype(jnp.int32), jnp.int32) == 1
-    lat_a[...] = jnp.where(even, south, north)
-    other = jnp.where(even, north, south)
-    mirror = other
-    for bit in (1, 2, 4):
-        mirror = jnp.where((lane & bit) != 0, turn(mirror, bit), turn(mirror, -bit))
-    mirror = jnp.where(even, turn(mirror, -GROUP), turn(mirror, GROUP))
-    lat_b[...] = jnp.where(over, mirror, other)
+    for start in range(0, levels, SUBLANES):
+        rows = start, min(SUBLANES, levels - start)
+        block, shape = slice(start, start + rows[1]), (rows[1], LANES)
+        row_lane = lanes_of(rows[1])
+        group = row_lane // GROUP
+        north = jnp.zeros(shape, jnp.float32)
+        south = north
+        for i in range(own):
+            place = own_rows(i, own, rows)
+            values = transformed(x[place], b[place], c[place], h[place], above[block, :], below[block, :])
+            for f, name in enumerate(FIELDS):
+                store[name][place] = values[name]
+                if name == "q":
+                    q_ref[pl.ds((1 + start) * own + i, rows[1], stride=own), :] = values[name]
+                slot = f * own + i
+                rolled = turn(values[name], GROUP * slot)
+                north = jnp.where(group == slot, rolled, north)
+                south = jnp.where(group == (slot - 1) % groups, rolled, south)
+        even = jnp.full(shape, lat_even, jnp.int32) == 1
+        over = jnp.full(shape, pole.astype(jnp.int32), jnp.int32) == 1
+        lat_a[block, :] = jnp.where(even, south, north)
+        other = jnp.where(even, north, south)
+        mirror = other
+        for bit in (1, 2, 4):
+            mirror = jnp.where((row_lane & bit) != 0, turn(mirror, bit), turn(mirror, -bit))
+        mirror = jnp.where(even, turn(mirror, -GROUP), turn(mirror, GROUP))
+        lat_b[block, :] = jnp.where(over, mirror, other)
     clear_ends(q_ref, own, levels)
     for k, (i, inner) in enumerate(((0, 1), (own - 1, own - 2))):
         q = plane(q_ref, i, own, levels)[...]

time: 45.9 us -> 45.9 us (level)
  no operation moved by 1% of the time
where the time goes in v7:
time: 45.9 us; the launch traced here: 45.7 us
  blocking collectives  18.2 us (40%)
  starting transfers between devices  14.2 us (31%)
  waiting for transfers between devices  7.68 us (17%)
  Pallas kernels  5 us (11%)
  between operations  0.69 us (2%)
    all_to_all x2, blocking collectives, everywhere(): return lax.all_to_all(rows, AXES, 0, 0, tiled=True)  18.2 us
    ppermute x8, starting transfers between devices, swap(): return lax.ppermute(value, AXES, pairs[name])  14.2 us
    ppermute x8, waiting for transfers between devices, swap(): return lax.ppermute(value, AXES, pairs[name])  7.68 us
    pallas_call x6, Pallas kernels, call(): pl.pallas_call(kernel, out_shape=tuple(outs) if len(outs) > 1 else outs[0...  5 us
  transfers between devices with their start and end apart: 8, of which 3 were waited for; matrix products, arithmetic and copies ran while one was open for 0% of the time, Pallas kernels for 1%

profile of v7, /device:TPU:0, one launch (start us, length us, event | category | flops | bytes accessed | tf_op | source)
XLA Modules:
  0.0 45.7 jit_solution(7643593611774662549)
XLA Ops:
  0.6 1.7 %shard_map.68 = (f32[3,70,128]{2,1,0:T(8,128)S(1)}, f32[3,70,128]{2,1,0:T(8,128)S(1)}, f32[70,128]{1,0:T(8,128)S(1)}, f32[70,128]{1,0:T(8,128)S(1)}, f32[70,128]...) custom-call(f32[280,128]{1,0:T(8,128)} %bitcast.7, ...), custom_call_target="tpu_custom_call" | custom-call | tf_op jit(solution)/shard_map/pallas_call | solution.py:479
  2.4 3.0 %collective-permute-start = (f32[3,70,128]{2,1,0:T(8,128)S(1)}, f32[3,70,128]{2,1,0:T(8,128)S(1)}, u32[]{:S(2)}, u32[]{:S(2)}) collective-permute-start(f32[3,70,128]{2,1,0:T(8,128)S(1)} %get-tuple-element.42), channel_id=1, source_target_pairs={{0,4},{1,5},{2,6},{3,7},{4,0},{5,1},{6,2},{7,3},{8,12},{9,13},{10,... | collective-permute-start | bytes 322568 | tf_op jit(solution)/shard_map/ppermute | solution.py:490
  5.4 3.6 %collective-permute-start.1 = (f32[3,70,128]{2,1,0:T(8,128)S(1)}, f32[3,70,128]{2,1,0:T(8,128)S(1)}, u32[]{:S(2)}, u32[]{:S(2)}) collective-permute-start(f32[3,70,128]{2,1,0:T(8,128)S(1)} %get-tuple-element.43), channel_id=1, source_target_pairs={{0,28},{1,29},{2,30},{3,31},{4,8},{5,9},{6,10},{7,11},{8,4},{9,5},... | collective-permute-start | bytes 322568 | tf_op jit(solution)/shard_map/ppermute | solution.py:490
  9.0 0.0 collective-permute-start.2
  9.0 0.0 collective-permute-start.3
  9.0 1.2 %collective-permute-done.2.lat_a = f32[70,128]{1,0:T(8,128)S(1)} collective-permute-done((f32[70,128]{1,0:T(8,128)S(1)}, f32[70,128]{1,0:T(8,128)S(1)}, u32[]{:S(2)}, u32[]{:S(2)}) %collective-permute-start.2) | collective-permute-done | bytes 35872 | tf_op jit(solution)/shard_map/ppermute | solution.py:490
  10.2 3.6 %collective-permute-done.3.lat_b = f32[70,128]{1,0:T(8,128)S(1)} collective-permute-done((f32[70,128]{1,0:T(8,128)S(1)}, f32[70,128]{1,0:T(8,128)S(1)}, u32[]{:S(2)}, u32[]{:S(2)}) %collective-permute-start.3) | collective-permute-done | bytes 35872 | tf_op jit(solution)/shard_map/ppermute | solution.py:490
  13.8 0.1 shard_map.69
  13.9 0.1 collective-permute-start.4
  14.0 3.7 %collective-permute-start.5 = (f32[70,128]{1,0:T(8,128)S(1)}, f32[70,128]{1,0:T(8,128)S(1)}, u32[]{:S(2)}, u32[]{:S(2)}) collective-permute-start(f32[70,128]{1,0:T(8,128)S(1)} %get-tuple-element.47), channel_id=1, source_target_pairs={{0,28},{1,29},{2,30},{3,31},{4,8},{5,9},{6,10},{7,11},{8,4},{9,5},... | collective-permute-start | bytes 107528 | tf_op jit(solution)/shard_map/ppermute | solution.py:490
  17.7 0.2 shard_map.70
  17.9 0.0 collective-permute-done.4.corners_a
  18.0 2.8 %collective-permute-done.5.corners_b = f32[70,128]{1,0:T(8,128)S(1)} collective-permute-done((f32[70,128]{1,0:T(8,128)S(1)}, f32[70,128]{1,0:T(8,128)S(1)}, u32[]{:S(2)}, u32[]{:S(2)}) %collective-permute-start.5) | collective-permute-done | bytes 35872 | tf_op jit(solution)/shard_map/ppermute | solution.py:490
  20.7 0.0 collective-permute-done.from_a
  20.7 0.0 collective-permute-done.1.from_b
  20.7 1.0 %shard_map.71 = (f32[720,128]{1,0:T(8,128)S(1)}, f32[720,128]{1,0:T(8,128)S(1)}, f32[720,128]{1,0:T(8,128)S(1)}, f32[720,128]{1,0:T(8,128)S(1)}, f32[720,128]{1,...) custom-call(f32[280,128]{1,0:T(8,128)S(1)} %get-tuple-element.39.fd,, ...), custom_call_target="tpu_custom_call", output_to_operand_aliasing={{0}: (7, {}), {1}: (8, {}), {2}: (9, {}), {3}: (10, {}), {4... | custom-call | tf_op jit(solution)/shard_map/pallas_call | solution.py:479
  21.7 0.2 collective-permute-start.6
  21.9 3.6 %collective-permute-start.7 = (f32[5,70,128]{2,1,0:T(8,128)S(1)}, f32[5,70,128]{2,1,0:T(8,128)S(1)}, u32[]{:S(2)}, u32[]{:S(2)}) collective-permute-start(f32[5,70,128]{2,1,0:T(8,128)S(1)} %get-tuple-element.63), channel_id=1, source_target_pairs={{0,28},{1,29},{2,30},{3,31},{4,8},{5,9},{6,10},{7,11},{8,4},{9,5},... | collective-permute-start | bytes 537608 | tf_op jit(solution)/shard_map/ppermute | solution.py:490
  25.5 9.3 %all_to_all.10.shift_sums = f32[32,1,128]{2,1,0:T(1,128)S(1)} all-to-all(f32[32,1,128]{2,1,0:T(1,128)S(1)} %get-tuple-element.68), channel_id=1, replica_groups=mesh['lon'=8,'lat'=4] {'lon','lat'}, dimensions={0} | all-to-all | bytes 32768 | tf_op jit(solution)/shard_map/all_to_all | solution.py:493
  34.8 0.0 collective-permute-done.6.from_a
  34.8 0.0 collective-permute-done.7.from_b
  34.8 0.0 copy-start
  34.8 0.0 copy-start.1
  34.8 1.0 %shard_map.72 = (f32[280,128]{1,0:T(8,128)S(1)}, f32[280,128]{1,0:T(8,128)S(1)}, f32[280,128]{1,0:T(8,128)S(1)}, f32[32,1,128]{2,1,0:T(1,128)S(1)}, f32[1,128]{1,0:T(1,128)S(1)}) custom-call(f32[280,128]{1,0:T(8,128)S(1)} %get-tuple-element.59.k0, f32[280,128]{1,0:T(8,128)S(1)} %get-tuple-element.60.k1, f32[280,128]{1,0:T(8,128)S(1)} %get-tuple-element.61.k1_strip, ...), custom_call_target="tpu_custom_call" | custom-call | tf_op jit(solution)/shard_map/pallas_call | solution.py:479
  35.8 8.9 %all_to_all.11.sums = f32[32,1,128]{2,1,0:T(1,128)S(1)} all-to-all(f32[32,1,128]{2,1,0:T(1,128)S(1)} %get-tuple-element.69), channel_id=1, replica_groups=mesh['lon'=8,'lat'=4] {'lon','lat'}, dimensions={0} | all-to-all | bytes 32768 | tf_op jit(solution)/shard_map/all_to_all | solution.py:493
  44.7 0.0 copy-done
  44.7 0.0 copy-done.1
  44.7 1.0 %shard_map.73 = (f32[280,128]{1,0:T(8,128)}, f32[280,128]{1,0:T(8,128)}) custom-call(f32[32,1,128]{2,1,0:T(1,128)S(1)} %all_to_all.11.sums, f32[1,128]{1,0:T(1,128)S(1)} %get-tuple-element.70.shift_row, f32[280,128]{1,0:T(8,128)S(1)} %bitcast.8, f32[280,128]{1,0:T(8,128)S(1)} %bitcast.10, f32[280,128]{1,0:T(8,128)S(1)} %get-tuple-element.59.k0, ...), custom_call_target="tpu_custom_call" | custom-call | tf_op jit(solution)/shard_map/pallas_call | solution.py:479
Async XLA Ops:
  2.4 18.4 %collective-permute-start = (f32[3,70,128]{2,1,0:T(8,128)S(1)}, f32[3,70,128]{2,1,0:T(8,128)S(1)}, u32[]{:S(2)}, u32[]{:S(2)}) collective-permute-start(f32[3,70,128]{2,1,0:T(8,128)S(1)} %get-tuple-element.42), channel_id=1, source_target_pairs={{0,4},{1,5},{2,6},{3,7},{4,0},{5,1},{6,2},{7,3},{8,12},{9,13},{10,... | collective-permute-start | bytes 322568 | tf_op jit(solution)/shard_map/ppermute | solution.py:490
  5.4 15.3 %collective-permute-start.1 = (f32[3,70,128]{2,1,0:T(8,128)S(1)}, f32[3,70,128]{2,1,0:T(8,128)S(1)}, u32[]{:S(2)}, u32[]{:S(2)}) collective-permute-start(f32[3,70,128]{2,1,0:T(8,128)S(1)} %get-tuple-element.43), channel_id=1, source_target_pairs={{0,28},{1,29},{2,30},{3,31},{4,8},{5,9},{6,10},{7,11},{8,4},{9,5},... | collective-permute-start | bytes 322568 | tf_op jit(solution)/shard_map/ppermute | solution.py:490
  9.0 1.2 %collective-permute-start.2 = (f32[70,128]{1,0:T(8,128)S(1)}, f32[70,128]{1,0:T(8,128)S(1)}, u32[]{:S(2)}, u32[]{:S(2)}) collective-permute-start(f32[70,128]{1,0:T(8,128)S(1)} %get-tuple-element.44), channel_id=1, source_target_pairs={{0,1},{1,0},{2,3},{3,2},{4,5},{5,4},{6,7},{7,6},{8,9},{9,8},{10,11... | collective-permute-start | bytes 107528 | tf_op jit(solution)/shard_map/ppermute | solution.py:490
  9.0 4.9 %collective-permute-start.3 = (f32[70,128]{1,0:T(8,128)S(1)}, f32[70,128]{1,0:T(8,128)S(1)}, u32[]{:S(2)}, u32[]{:S(2)}) collective-permute-start(f32[70,128]{1,0:T(8,128)S(1)} %get-tuple-element.45), channel_id=1, source_target_pairs={{0,16},{1,2},{2,1},{3,19},{4,20},{5,6},{6,5},{7,23},{8,24},{9,10},... | collective-permute-start | bytes 107528 | tf_op jit(solution)/shard_map/ppermute | solution.py:490
  13.9 4.0 %collective-permute-start.4 = (f32[70,128]{1,0:T(8,128)S(1)}, f32[70,128]{1,0:T(8,128)S(1)}, u32[]{:S(2)}, u32[]{:S(2)}) collective-permute-start(f32[70,128]{1,0:T(8,128)S(1)} %get-tuple-element.46), channel_id=1, source_target_pairs={{0,4},{1,5},{2,6},{3,7},{4,0},{5,1},{6,2},{7,3},{8,12},{9,13},{10,... | collective-permute-start | bytes 107528 | tf_op jit(solution)/shard_map/ppermute | solution.py:490
  14.0 6.7 %collective-permute-start.5 = (f32[70,128]{1,0:T(8,128)S(1)}, f32[70,128]{1,0:T(8,128)S(1)}, u32[]{:S(2)}, u32[]{:S(2)}) collective-permute-start(f32[70,128]{1,0:T(8,128)S(1)} %get-tuple-element.47), channel_id=1, source_target_pairs={{0,28},{1,29},{2,30},{3,31},{4,8},{5,9},{6,10},{7,11},{8,4},{9,5},... | collective-permute-start | bytes 107528 | tf_op jit(solution)/shard_map/ppermute | solution.py:490
  21.7 13.1 %collective-permute-start.6 = (f32[5,70,128]{2,1,0:T(8,128)S(1)}, f32[5,70,128]{2,1,0:T(8,128)S(1)}, u32[]{:S(2)}, u32[]{:S(2)}) collective-permute-start(f32[5,70,128]{2,1,0:T(8,128)S(1)} %get-tuple-element.62), channel_id=1, source_target_pairs={{0,4},{1,5},{2,6},{3,7},{4,0},{5,1},{6,2},{7,3},{8,12},{9,13},{10,... | collective-permute-start | bytes 537608 | tf_op jit(solution)/shard_map/ppermute | solution.py:490
  21.9 12.9 %collective-permute-start.7 = (f32[5,70,128]{2,1,0:T(8,128)S(1)}, f32[5,70,128]{2,1,0:T(8,128)S(1)}, u32[]{:S(2)}, u32[]{:S(2)}) collective-permute-start(f32[5,70,128]{2,1,0:T(8,128)S(1)} %get-tuple-element.63), channel_id=1, source_target_pairs={{0,28},{1,29},{2,30},{3,31},{4,8},{5,9},{6,10},{7,11},{8,4},{9,5},... | collective-permute-start | bytes 537608 | tf_op jit(solution)/shard_map/ppermute | solution.py:490
  34.8 9.9 %copy-start = (f32[70,4,128]{2,1,0:T(4,128)S(1)}, f32[70,4,128]{2,1,0:T(4,128)}, u32[]{:S(2)}) copy-start(f32[70,4,128]{2,1,0:T(4,128)} %param.6) | copy-start | bytes 430084
  34.8 9.9 %copy-start.1 = (f32[70,4,128]{2,1,0:T(4,128)S(1)}, f32[70,4,128]{2,1,0:T(4,128)}, u32[]{:S(2)}) copy-start(f32[70,4,128]{2,1,0:T(4,128)} %param.7) | copy-start | bytes 430084

commit v8 on v7

--- a/solution.py
+++ b/solution.py
@@ -449,17 +449,23 @@
     one = jnp.ones((1, 1), jnp.float32)
     solution, residual = krylov_coefficients(first, others[: 2 * ITERS], others[2 * ITERS :], shift, one)
     vectors = (k0, k1, k2, k3, k4)
-    inverse = 1.0 / c[...]
-
-    def combined(coefficients):
-        total = None
-        for a, v in zip(coefficients, vectors):
-            term = a * v[...]
-            total = term if total is None else total + term
-        return total * inverse
-
-    out[...] = x[...] + combined(solution)
-    rest[...] = combined(residual)
+    solution, residual = ([jnp.broadcast_to(a, (SUBLANES, LANES)) for a in v] for v in (solution, residual))
+    size = x.shape[0]
+    for start in range(0, size, SUBLANES):
+        count = min(SUBLANES, size - start)
+        block = slice(start, start + count)
+        inverse = 1.0 / c[block, :]
+        values = [v[block, :] for v in vectors]
+
+        def combined(coefficients):
+            total = None
+            for a, v in zip(coefficients, values):
+                term = a[:count] * v
+                total = term if total is None else total + term
+            return total * inverse
+
+        out[block, :] = x[block, :] + combined(solution)
+        rest[block, :] = combined(residual)
 
 
 def program(right_side, first_guess, cell_scale, helmholtz_term, vertical_coupling):

time: 45.9 us -> 45.9 us (level)
  no operation moved by 1% of the time
where the time goes in v8:
time: 45.9 us; the launch traced here: 45.7 us
  blocking collectives  18.2 us (40%)
  starting transfers between devices  14.2 us (31%)
  waiting for transfers between devices  7.68 us (17%)
  Pallas kernels  5.01 us (11%)
  between operations  0.69 us (2%)
    all_to_all x2, blocking collectives, everywhere(): return lax.all_to_all(rows, AXES, 0, 0, tiled=True)  18.2 us
    ppermute x8, starting transfers between devices, swap(): return lax.ppermute(value, AXES, pairs[name])  14.2 us
    ppermute x8, waiting for transfers between devices, swap(): return lax.ppermute(value, AXES, pairs[name])  7.68 us
    pallas_call x6, Pallas kernels, call(): pl.pallas_call(kernel, out_shape=tuple(outs) if len(outs) > 1 else outs[0...  5.01 us
  transfers between devices with their start and end apart: 8, of which 3 were waited for; matrix products, arithmetic and copies ran while one was open for 0% of the time, Pallas kernels for 1%

profile of v8, /device:TPU:0, one launch (start us, length us, event | category | flops | bytes accessed | tf_op | source)
XLA Modules:
  0.0 45.7 jit_solution(290028451246650249)
XLA Ops:
  0.6 1.7 %shard_map.68 = (f32[3,70,128]{2,1,0:T(8,128)S(1)}, f32[3,70,128]{2,1,0:T(8,128)S(1)}, f32[70,128]{1,0:T(8,128)S(1)}, f32[70,128]{1,0:T(8,128)S(1)}, f32[70,128]...) custom-call(f32[280,128]{1,0:T(8,128)} %bitcast.7, ...), custom_call_target="tpu_custom_call" | custom-call | tf_op jit(solution)/shard_map/pallas_call | solution.py:485
  2.4 3.0 %collective-permute-start = (f32[3,70,128]{2,1,0:T(8,128)S(1)}, f32[3,70,128]{2,1,0:T(8,128)S(1)}, u32[]{:S(2)}, u32[]{:S(2)}) collective-permute-start(f32[3,70,128]{2,1,0:T(8,128)S(1)} %get-tuple-element.42), channel_id=1, source_target_pairs={{0,4},{1,5},{2,6},{3,7},{4,0},{5,1},{6,2},{7,3},{8,12},{9,13},{10,... | collective-permute-start | bytes 322568 | tf_op jit(solution)/shard_map/ppermute | solution.py:496
  5.4 3.6 %collective-permute-start.1 = (f32[3,70,128]{2,1,0:T(8,128)S(1)}, f32[3,70,128]{2,1,0:T(8,128)S(1)}, u32[]{:S(2)}, u32[]{:S(2)}) collective-permute-start(f32[3,70,128]{2,1,0:T(8,128)S(1)} %get-tuple-element.43), channel_id=1, source_target_pairs={{0,28},{1,29},{2,30},{3,31},{4,8},{5,9},{6,10},{7,11},{8,4},{9,5},... | collective-permute-start | bytes 322568 | tf_op jit(solution)/shard_map/ppermute | solution.py:496
  9.0 0.0 collective-permute-start.2
  9.0 0.0 collective-permute-start.3
  9.0 1.2 %collective-permute-done.2.lat_a = f32[70,128]{1,0:T(8,128)S(1)} collective-permute-done((f32[70,128]{1,0:T(8,128)S(1)}, f32[70,128]{1,0:T(8,128)S(1)}, u32[]{:S(2)}, u32[]{:S(2)}) %collective-permute-start.2) | collective-permute-done | bytes 35872 | tf_op jit(solution)/shard_map/ppermute | solution.py:496
  10.2 3.6 %collective-permute-done.3.lat_b = f32[70,128]{1,0:T(8,128)S(1)} collective-permute-done((f32[70,128]{1,0:T(8,128)S(1)}, f32[70,128]{1,0:T(8,128)S(1)}, u32[]{:S(2)}, u32[]{:S(2)}) %collective-permute-start.3) | collective-permute-done | bytes 35872 | tf_op jit(solution)/shard_map/ppermute | solution.py:496
  13.8 0.1 shard_map.69
  13.9 0.1 collective-permute-start.4
  14.0 3.7 %collective-permute-start.5 = (f32[70,128]{1,0:T(8,128)S(1)}, f32[70,128]{1,0:T(8,128)S(1)}, u32[]{:S(2)}, u32[]{:S(2)}) collective-permute-start(f32[70,128]{1,0:T(8,128)S(1)} %get-tuple-element.47), channel_id=1, source_target_pairs={{0,28},{1,29},{2,30},{3,31},{4,8},{5,9},{6,10},{7,11},{8,4},{9,5},... | collective-permute-start | bytes 107528 | tf_op jit(solution)/shard_map/ppermute | solution.py:496
  17.7 0.2 shard_map.70
  17.9 0.0 collective-permute-done.4.corners_a
  18.0 2.8 %collective-permute-done.5.corners_b = f32[70,128]{1,0:T(8,128)S(1)} collective-permute-done((f32[70,128]{1,0:T(8,128)S(1)}, f32[70,128]{1,0:T(8,128)S(1)}, u32[]{:S(2)}, u32[]{:S(2)}) %collective-permute-start.5) | collective-permute-done | bytes 35872 | tf_op jit(solution)/shard_map/ppermute | solution.py:496
  20.7 0.0 collective-permute-done.from_a
  20.7 0.0 collective-permute-done.1.from_b
  20.7 1.0 %shard_map.71 = (f32[720,128]{1,0:T(8,128)S(1)}, f32[720,128]{1,0:T(8,128)S(1)}, f32[720,128]{1,0:T(8,128)S(1)}, f32[720,128]{1,0:T(8,128)S(1)}, f32[720,128]{1,...) custom-call(f32[280,128]{1,0:T(8,128)S(1)} %get-tuple-element.39.fd,, ...), custom_call_target="tpu_custom_call", output_to_operand_aliasing={{0}: (7, {}), {1}: (8, {}), {2}: (9, {}), {3}: (10, {}), {4... | custom-call | tf_op jit(solution)/shard_map/pallas_call | solution.py:485
  21.7 0.2 collective-permute-start.6
  21.9 3.6 %collective-permute-start.7 = (f32[5,70,128]{2,1,0:T(8,128)S(1)}, f32[5,70,128]{2,1,0:T(8,128)S(1)}, u32[]{:S(2)}, u32[]{:S(2)}) collective-permute-start(f32[5,70,128]{2,1,0:T(8,128)S(1)} %get-tuple-element.63), channel_id=1, source_target_pairs={{0,28},{1,29},{2,30},{3,31},{4,8},{5,9},{6,10},{7,11},{8,4},{9,5},... | collective-permute-start | bytes 537608 | tf_op jit(solution)/shard_map/ppermute | solution.py:496
  25.5 9.3 %all_to_all.10.shift_sums = f32[32,1,128]{2,1,0:T(1,128)S(1)} all-to-all(f32[32,1,128]{2,1,0:T(1,128)S(1)} %get-tuple-element.68), channel_id=1, replica_groups=mesh['lon'=8,'lat'=4] {'lon','lat'}, dimensions={0} | all-to-all | bytes 32768 | tf_op jit(solution)/shard_map/all_to_all | solution.py:499
  34.8 0.0 collective-permute-done.6.from_a
  34.8 0.0 collective-permute-done.7.from_b
  34.8 0.0 copy-start
  34.8 0.0 copy-start.1
  34.8 1.0 %shard_map.72 = (f32[280,128]{1,0:T(8,128)S(1)}, f32[280,128]{1,0:T(8,128)S(1)}, f32[280,128]{1,0:T(8,128)S(1)}, f32[32,1,128]{2,1,0:T(1,128)S(1)}, f32[1,128]{1,0:T(1,128)S(1)}) custom-call(f32[280,128]{1,0:T(8,128)S(1)} %get-tuple-element.59.k0, f32[280,128]{1,0:T(8,128)S(1)} %get-tuple-element.60.k1, f32[280,128]{1,0:T(8,128)S(1)} %get-tuple-element.61.k1_strip, ...), custom_call_target="tpu_custom_call" | custom-call | tf_op jit(solution)/shard_map/pallas_call | solution.py:485
  35.8 8.9 %all_to_all.11.sums = f32[32,1,128]{2,1,0:T(1,128)S(1)} all-to-all(f32[32,1,128]{2,1,0:T(1,128)S(1)} %get-tuple-element.69), channel_id=1, replica_groups=mesh['lon'=8,'lat'=4] {'lon','lat'}, dimensions={0} | all-to-all | bytes 32768 | tf_op jit(solution)/shard_map/all_to_all | solution.py:499
  44.7 0.0 copy-done
  44.7 0.0 copy-done.1
  44.7 1.0 %shard_map.73 = (f32[280,128]{1,0:T(8,128)}, f32[280,128]{1,0:T(8,128)}) custom-call(f32[32,1,128]{2,1,0:T(1,128)S(1)} %all_to_all.11.sums, f32[1,128]{1,0:T(1,128)S(1)} %get-tuple-element.70.shift_row, f32[280,128]{1,0:T(8,128)S(1)} %bitcast.8, f32[280,128]{1,0:T(8,128)S(1)} %bitcast.10, f32[280,128]{1,0:T(8,128)S(1)} %get-tuple-element.59.k0, ...), custom_call_target="tpu_custom_call" | custom-call | tf_op jit(solution)/shard_map/pallas_call | solution.py:485
Async XLA Ops:
  2.4 18.4 %collective-permute-start = (f32[3,70,128]{2,1,0:T(8,128)S(1)}, f32[3,70,128]{2,1,0:T(8,128)S(1)}, u32[]{:S(2)}, u32[]{:S(2)}) collective-permute-start(f32[3,70,128]{2,1,0:T(8,128)S(1)} %get-tuple-element.42), channel_id=1, source_target_pairs={{0,4},{1,5},{2,6},{3,7},{4,0},{5,1},{6,2},{7,3},{8,12},{9,13},{10,... | collective-permute-start | bytes 322568 | tf_op jit(solution)/shard_map/ppermute | solution.py:496
  5.4 15.3 %collective-permute-start.1 = (f32[3,70,128]{2,1,0:T(8,128)S(1)}, f32[3,70,128]{2,1,0:T(8,128)S(1)}, u32[]{:S(2)}, u32[]{:S(2)}) collective-permute-start(f32[3,70,128]{2,1,0:T(8,128)S(1)} %get-tuple-element.43), channel_id=1, source_target_pairs={{0,28},{1,29},{2,30},{3,31},{4,8},{5,9},{6,10},{7,11},{8,4},{9,5},... | collective-permute-start | bytes 322568 | tf_op jit(solution)/shard_map/ppermute | solution.py:496
  9.0 1.2 %collective-permute-start.2 = (f32[70,128]{1,0:T(8,128)S(1)}, f32[70,128]{1,0:T(8,128)S(1)}, u32[]{:S(2)}, u32[]{:S(2)}) collective-permute-start(f32[70,128]{1,0:T(8,128)S(1)} %get-tuple-element.44), channel_id=1, source_target_pairs={{0,1},{1,0},{2,3},{3,2},{4,5},{5,4},{6,7},{7,6},{8,9},{9,8},{10,11... | collective-permute-start | bytes 107528 | tf_op jit(solution)/shard_map/ppermute | solution.py:496
  9.0 4.9 %collective-permute-start.3 = (f32[70,128]{1,0:T(8,128)S(1)}, f32[70,128]{1,0:T(8,128)S(1)}, u32[]{:S(2)}, u32[]{:S(2)}) collective-permute-start(f32[70,128]{1,0:T(8,128)S(1)} %get-tuple-element.45), channel_id=1, source_target_pairs={{0,16},{1,2},{2,1},{3,19},{4,20},{5,6},{6,5},{7,23},{8,24},{9,10},... | collective-permute-start | bytes 107528 | tf_op jit(solution)/shard_map/ppermute | solution.py:496
  13.9 4.0 %collective-permute-start.4 = (f32[70,128]{1,0:T(8,128)S(1)}, f32[70,128]{1,0:T(8,128)S(1)}, u32[]{:S(2)}, u32[]{:S(2)}) collective-permute-start(f32[70,128]{1,0:T(8,128)S(1)} %get-tuple-element.46), channel_id=1, source_target_pairs={{0,4},{1,5},{2,6},{3,7},{4,0},{5,1},{6,2},{7,3},{8,12},{9,13},{10,... | collective-permute-start | bytes 107528 | tf_op jit(solution)/shard_map/ppermute | solution.py:496
  14.0 6.7 %collective-permute-start.5 = (f32[70,128]{1,0:T(8,128)S(1)}, f32[70,128]{1,0:T(8,128)S(1)}, u32[]{:S(2)}, u32[]{:S(2)}) collective-permute-start(f32[70,128]{1,0:T(8,128)S(1)} %get-tuple-element.47), channel_id=1, source_target_pairs={{0,28},{1,29},{2,30},{3,31},{4,8},{5,9},{6,10},{7,11},{8,4},{9,5},... | collective-permute-start | bytes 107528 | tf_op jit(solution)/shard_map/ppermute | solution.py:496
  21.7 13.1 %collective-permute-start.6 = (f32[5,70,128]{2,1,0:T(8,128)S(1)}, f32[5,70,128]{2,1,0:T(8,128)S(1)}, u32[]{:S(2)}, u32[]{:S(2)}) collective-permute-start(f32[5,70,128]{2,1,0:T(8,128)S(1)} %get-tuple-element.62), channel_id=1, source_target_pairs={{0,4},{1,5},{2,6},{3,7},{4,0},{5,1},{6,2},{7,3},{8,12},{9,13},{10,... | collective-permute-start | bytes 537608 | tf_op jit(solution)/shard_map/ppermute | solution.py:496
  21.9 12.9 %collective-permute-start.7 = (f32[5,70,128]{2,1,0:T(8,128)S(1)}, f32[5,70,128]{2,1,0:T(8,128)S(1)}, u32[]{:S(2)}, u32[]{:S(2)}) collective-permute-start(f32[5,70,128]{2,1,0:T(8,128)S(1)} %get-tuple-element.63), channel_id=1, source_target_pairs={{0,28},{1,29},{2,30},{3,31},{4,8},{5,9},{6,10},{7,11},{8,4},{9,5},... | collective-permute-start | bytes 537608 | tf_op jit(solution)/shard_map/ppermute | solution.py:496
  34.8 9.9 %copy-start = (f32[70,4,128]{2,1,0:T(4,128)S(1)}, f32[70,4,128]{2,1,0:T(4,128)}, u32[]{:S(2)}) copy-start(f32[70,4,128]{2,1,0:T(4,128)} %param.6) | copy-start | bytes 430084
  34.8 9.9 %copy-start.1 = (f32[70,4,128]{2,1,0:T(4,128)S(1)}, f32[70,4,128]{2,1,0:T(4,128)}, u32[]{:S(2)}) copy-start(f32[70,4,128]{2,1,0:T(4,128)} %param.7) | copy-start | bytes 430084
